TPU v7x, 512 devices: a whole 4x8x8 slice. The times are simulated.
512 devices in a mesh: rows: 64 (over z, x, core), cols: 8 (over y).
Axes of the slice: x: 4, y: 8, z: 8, core: 2. Of those that a mesh axis runs over, the one named last changes fastest.
Arguments:
- rhs: float32 [3, 128, 256, 128], P(None, 'rows', 'cols'), may hold values from -6 to 6
- diag_inv: float32 [3, 128, 256, 256], P(None, 'rows', 'cols'), may hold values from -1 to 3.1, as said below
- factor_tiles: float32 [2, 128, 8, 256, 256], P(None, 'rows', None, 'cols'), may hold values from -0.125 to 0.125
- tile_source: int32 [2, 128, 8], P(None, 'rows'), may hold values from 0 to 255, as said below
- tile_count: int32 [2, 128], P(None, 'rows'), may hold values from 1 to 8, as said below
Outputs:
- solution: float32 [3, 128, 256, 128], P(None, 'rows', 'cols')
Inputs may be any that keep to these rules, and one draw needn't show every extreme that they name: `tile_source`: each source lies at a lower level than its target; supernode g mod 128 belongs to rows index (g mod 128) // 2, and that index differs from the target's by at most 7. The 8 sources of one supernode are distinct. `tile_count`: slots at or beyond the count hold no tile of the factor. At every target level some supernode has all 8 slots live. `diag_inv`: each block is lower triangular with a positive diagonal.
All inputs are finite; a program needn't handle non-finite values.
Results may differ from a plain program's by a relative error of at most 0.0003.
Values sent between devices are 32-bit elements; how exact they have to be, the bound alone decides.
A program may use at most 64 MiB of HBM per device.

v0:
```python
import jax
import jax.numpy as jnp
from jax import lax
from jax.sharding import PartitionSpec as P

KDEV = 7


def from_behind(value, axis, steps):
    count = lax.axis_size(axis)
    leading, last = (max(0, -steps), min(count, count - steps))
    return lax.ppermute(value, axis, [(source, source + steps) for source in range(leading, last)])


def local(rhs, diag_inv, factor_tiles, tile_source, tile_count):
    levels = rhs.shape[0]
    owned_count = rhs.shape[1]
    share_rows = rhs.shape[2]
    columns = rhs.shape[3]
    slot_count = tile_source.shape[2]
    reach_dev = KDEV
    window_len = 2 * reach_dev + 1
    total_sup = lax.axis_size("rows") * owned_count
    row_place = lax.axis_index("rows")
    highest = lax.Precision.HIGHEST
    slot_ids = jnp.arange(slot_count, dtype=jnp.int32)

    def window_places(sources):
        src_level = sources // total_sup
        within = sources % total_sup
        return (
            src_level * window_len + within // owned_count - row_place + reach_dev
        ) * owned_count + within % owned_count

    def live_mask(counts):
        return (slot_ids[None, :] < counts[:, None]).astype(jnp.float32)

    def full_rows(piece):
        return lax.all_gather(piece, "cols", axis=1, tiled=True)

    forward_values = []
    windows = []
    for height in range(levels):
        if height == 0:
            whole_block = full_rows(rhs[0])
        else:
            stacked = jnp.stack(windows, 0).reshape(
                height * window_len * owned_count, share_rows, columns
            )
            places = window_places(tile_source[height - 1])
            picked = (
                jnp.take(stacked, places, axis=0)
                * live_mask(tile_count[height - 1])[:, :, None, None]
            )
            partial_value = jnp.einsum(
                "skci,skcr->sir", factor_tiles[height - 1], picked, precision=highest
            )
            whole_block = full_rows(
                rhs[height]
                - lax.psum_scatter(partial_value, "cols", scatter_dimension=1, tiled=True)
            )
        values = jnp.einsum("sci,sir->scr", diag_inv[height], whole_block, precision=highest)
        forward_values.append(values)
        if height + 1 < levels:
            pieces = []
            for pull_offset in range(-reach_dev, reach_dev + 1):
                if pull_offset == 0:
                    pieces.append(values)
                else:
                    pieces.append(from_behind(values, "rows", -pull_offset))
            windows.append(jnp.stack(pieces, 0))
    carried = [jnp.zeros_like(forward_values[0]) for height in range(levels)]
    solution = [None] * levels
    for height in reversed(range(levels)):
        partial_value = jnp.einsum(
            "sci,scr->sir",
            diag_inv[height],
            forward_values[height] - carried[height],
            precision=highest,
        )
        own_share = lax.psum_scatter(partial_value, "cols", scatter_dimension=1, tiled=True)
        if height > 0:
            whole_block = lax.all_gather(own_share, "cols", axis=1, tiled=True)
        solution[height] = own_share
        if height > 0:
            term_set = jnp.einsum(
                "skci,sir->skcr", factor_tiles[height - 1], whole_block, precision=highest
            )
            term_set = term_set * live_mask(tile_count[height - 1])[:, :, None, None]
            places = window_places(tile_source[height - 1]).reshape(-1)
            targets = height * window_len * owned_count
            one_hot = (jnp.arange(targets, dtype=jnp.int32)[:, None] == places[None, :]).astype(
                jnp.float32
            )
            outgoing = jnp.einsum(
                "ms,slg->mlg",
                one_hot,
                term_set.reshape(owned_count * slot_count, share_rows, columns),
                precision=highest,
            )
            push_outgoing = outgoing.reshape(height, window_len, owned_count, share_rows, columns)
            received = push_outgoing[:, reach_dev]
            for offset in range(-reach_dev, reach_dev + 1):
                if offset != 0:
                    received = received + from_behind(
                        push_outgoing[:, reach_dev + offset], "rows", offset
                    )
            for lower_level in range(height):
                carried[lower_level] = carried[lower_level] + received[lower_level]
    return jnp.stack(solution, 0)


def solution(mesh):
    placed = (
        P(None, "rows", "cols", None),
        P(None, "rows", "cols", None),
        P(None, "rows", None, "cols", None),
        P(None, "rows", None),
        P(None, "rows"),
    )
    return jax.shard_map(
        local, mesh=mesh, in_specs=placed, out_specs=P(None, "rows", "cols", None), check_vma=False
    )
```

profile of v0, /device:TPU:1, one launch (start us, length us, event | category | flops | bytes accessed | tf_op | source)
XLA Modules:
  0.0 667.1 jit_solution(4755036083736061673)
XLA Ops:
  7.3 21.0 %all-gather = f32[1,2,256,128]{3,2,1,0:T(8,128)S(1)} all-gather(f32[1,2,32,128]{3,2,1,0:T(8,128)S(1)} %slice-done), channel_id=2, replica_groups=mesh['rows'=64,'cols'=8] {'cols'}, dimensions={2}, use_global_device_ids=true | all-gather | bytes 294912 | tf_op jit(solution)/shard_map/all_gather | solution.py:39
  28.6 10.9 %collective-permute-start = (f32[2,32,128]{2,1,0:T(8,128)S(1)}, f32[2,32,128]{2,1,0:T(8,128)S(1)}, u32[]{:S(2)}, u32[]{:S(2)}) collective-permute-start(f32[2,32,128]{2,1,0:T(8,128)S(1)} %fusion.14), channel_id=1, source_target_pairs={{0,56},{8,64},{16,72},{24,80},{32,88},{40,96},{48,104},{56,112},{6... | collective-permute-start | bytes 98312 | tf_op jit(solution)/shard_map/ppermute | solution.py:12
  39.5 4.4 collective-permute-start.1
  46.3 3.9 collective-permute-start.3
  50.3 7.0 %collective-permute-start.4 = (f32[2,32,128]{2,1,0:T(8,128)S(1)}, f32[2,32,128]{2,1,0:T(8,128)S(1)}, u32[]{:S(2)}, u32[]{:S(2)}) collective-permute-start(f32[2,32,128]{2,1,0:T(8,128)S(1)} %fusion.14), channel_id=1, source_target_pairs={{0,24},{8,32},{16,40},{24,48},{32,56},{40,64},{48,72},{56,80},{64,... | collective-permute-start | bytes 98312 | tf_op jit(solution)/shard_map/ppermute | solution.py:12
  86.8 39.0 %reduce-scatter.3.cloned.1.call-done = f32[2,32,128]{2,1,0:T(8,128)} async-done(((f32[2,256,128]{2,1,0:T(8,128)}), f32[2,32,128]{2,1,0:T(8,128)}) %reduce-scatter.3.cloned.1.call-update) | async-done | bytes 32784 | tf_op jit(solution)/shard_map/reduce_scatter | solution.py:60
  126.5 18.8 %all_gather.16 = f32[2,256,128]{2,1,0:T(8,128)S(1)} all-gather(f32[2,32,128]{2,1,0:T(8,128)S(1)} %bitcast_subtract_fusion), channel_id=1, replica_groups=mesh['rows'=64,'cols'=8] {'cols'}, dimensions={1}, use_global_device_ids=true | all-gather | bytes 294912 | tf_op jit(solution)/shard_map/all_gather | solution.py:39
  145.6 15.0 %collective-permute-start.14 = (f32[2,32,128]{2,1,0:T(8,128)S(1)}, f32[2,32,128]{2,1,0:T(8,128)S(1)}, u32[]{:S(2)}, u32[]{:S(2)}) collective-permute-start(f32[2,32,128]{2,1,0:T(8,128)S(1)} %bitcast.360), channel_id=1, source_target_pairs={{0,56},{8,64},{16,72},{24,80},{32,88},{40,96},{48,104},{56,112},{6... | collective-permute-start | bytes 98312 | tf_op jit(solution)/shard_map/ppermute | solution.py:12
  160.6 4.3 collective-permute-start.15
  170.7 6.3 collective-permute-start.18
  205.4 37.2 %reduce-scatter.5.cloned.1.call-done = f32[2,32,128]{2,1,0:T(8,128)} async-done(((f32[2,256,128]{2,1,0:T(8,128)}), f32[2,32,128]{2,1,0:T(8,128)}) %reduce-scatter.5.cloned.1.call-update) | async-done | bytes 32784 | tf_op jit(solution)/shard_map/reduce_scatter | solution.py:60
  243.4 18.4 %all_gather.17 = f32[2,256,128]{2,1,0:T(8,128)S(1)} all-gather(f32[2,32,128]{2,1,0:T(8,128)S(1)} %bitcast_subtract_fusion.1), channel_id=1, replica_groups=mesh['rows'=64,'cols'=8] {'cols'}, dimensions={1}, use_global_device_ids=true | all-gather | bytes 294912 | tf_op jit(solution)/shard_map/all_gather | solution.py:39
  265.5 81.7 %all-reduce.7.cloned.1.call-done = f32[2,256,128]{2,0,1:T(2,128)} async-done(((f32[2,256,128]{2,0,1:T(2,128)}), f32[2,256,128]{2,0,1:T(2,128)}) %all-reduce.7.cloned.1.call-update) | async-done | bytes 262160
  348.1 18.4 %all_gather.18 = f32[2,256,128]{2,0,1:T(2,128)S(1)} all-gather(f32[2,32,128]{2,0,1:T(2,128)S(1)} %constant_dynamic-slice_fusion.1), channel_id=1, replica_groups=mesh['rows'=64,'cols'=8] {'cols'}, dimensions={1}, use_global_device_ids=true | all-gather | bytes 294912 | tf_op jit(solution)/shard_map/all_gather | solution.py:83
  368.7 15.0 %collective-permute-start.41 = (f32[2,2,32,128]{3,2,1,0:T(8,128)S(1)}, f32[2,2,32,128]{3,2,1,0:T(8,128)S(1)}, u32[]{:S(2)}, u32[]{:S(2)}) collective-permute-start(f32[2,2,32,128]{3,2,1,0:T(8,128)S(1)} %bitcast.388), channel_id=1, source_target_pairs={{0,56},{8,64},{16,72},{24,80},{32,88},{40,96},{48,104},{56,112},{6... | collective-permute-start | bytes 196616 | tf_op jit(solution)/shard_map/ppermute | solution.py:12
  383.7 4.3 collective-permute-start.40
  393.8 6.2 collective-permute-start.37
  427.8 76.2 %all-reduce.9.cloned.1.call-done = f32[2,256,128]{2,0,1:T(2,128)} async-done(((f32[2,256,128]{2,0,1:T(2,128)}), f32[2,256,128]{2,0,1:T(2,128)}) %all-reduce.9.cloned.1.call-update) | async-done | bytes 262160
  504.8 18.4 %all_gather.19 = f32[2,256,128]{2,0,1:T(2,128)S(1)} all-gather(f32[2,32,128]{2,0,1:T(2,128)S(1)} %constant_dynamic-slice_fusion), channel_id=1, replica_groups=mesh['rows'=64,'cols'=8] {'cols'}, dimensions={1}, use_global_device_ids=true | all-gather | bytes 294912 | tf_op jit(solution)/shard_map/all_gather | solution.py:83
  524.5 15.0 %collective-permute-start.55 = (f32[1,2,32,128]{3,2,1,0:T(8,128)S(1)}, f32[1,2,32,128]{3,2,1,0:T(8,128)S(1)}, u32[]{:S(2)}, u32[]{:S(2)}) collective-permute-start(f32[1,2,32,128]{3,2,1,0:T(8,128)S(1)} %get-tuple-element.21), channel_id=1, source_target_pairs={{0,56},{8,64},{16,72},{24,80},{32,88},{40,96},{48,104},{56,112},{6... | collective-permute-start | bytes 98312 | tf_op jit(solution)/shard_map/ppermute | solution.py:12
  539.5 4.3 collective-permute-start.54
  546.3 3.3 collective-permute-start.52
  549.6 6.2 collective-permute-start.51
  584.5 74.6 %all-reduce.11.cloned.1.call-done = f32[2,256,128]{2,0,1:T(2,128)} async-done(((f32[2,256,128]{2,0,1:T(2,128)}), f32[2,256,128]{2,0,1:T(2,128)}) %all-reduce.11.cloned.1.call-update) | async-done | bytes 262160
  (198 shorter events, 142.3 us)
Async XLA Ops:
  6.5 119.2 %reduce-scatter.3.cloned.1.call-start = ((), (), s32[]{:S(2)}) async-start(), calls=%async_computation.2 | async-start | bytes 294912 | tf_op jit(solution)/shard_map/reduce_scatter | solution.py:60
  28.6 28.9 %collective-permute-start = (f32[2,32,128]{2,1,0:T(8,128)S(1)}, f32[2,32,128]{2,1,0:T(8,128)S(1)}, u32[]{:S(2)}, u32[]{:S(2)}) collective-permute-start(f32[2,32,128]{2,1,0:T(8,128)S(1)} %fusion.14), channel_id=1, source_target_pairs={{0,56},{8,64},{16,72},{24,80},{32,88},{40,96},{48,104},{56,112},{6... | collective-permute-start | bytes 98312 | tf_op jit(solution)/shard_map/ppermute | solution.py:12
  39.5 20.6 %collective-permute-start.1 = (f32[2,32,128]{2,1,0:T(8,128)S(1)}, f32[2,32,128]{2,1,0:T(8,128)S(1)}, u32[]{:S(2)}, u32[]{:S(2)}) collective-permute-start(f32[2,32,128]{2,1,0:T(8,128)S(1)} %fusion.14), channel_id=1, source_target_pairs={{0,48},{8,56},{16,64},{24,72},{32,80},{40,88},{48,96},{56,104},{64... | collective-permute-start | bytes 98312 | tf_op jit(solution)/shard_map/ppermute | solution.py:12
  43.8 18.1 %collective-permute-start.2 = (f32[2,32,128]{2,1,0:T(8,128)S(1)}, f32[2,32,128]{2,1,0:T(8,128)S(1)}, u32[]{:S(2)}, u32[]{:S(2)}) collective-permute-start(f32[2,32,128]{2,1,0:T(8,128)S(1)} %fusion.14), channel_id=1, source_target_pairs={{0,40},{8,48},{16,56},{24,64},{32,72},{40,80},{48,88},{56,96},{64,... | collective-permute-start | bytes 98312 | tf_op jit(solution)/shard_map/ppermute | solution.py:12
  46.3 18.1 %collective-permute-start.3 = (f32[2,32,128]{2,1,0:T(8,128)S(1)}, f32[2,32,128]{2,1,0:T(8,128)S(1)}, u32[]{:S(2)}, u32[]{:S(2)}) collective-permute-start(f32[2,32,128]{2,1,0:T(8,128)S(1)} %fusion.14), channel_id=1, source_target_pairs={{0,32},{8,40},{16,48},{24,56},{32,64},{40,72},{48,80},{56,88},{64,... | collective-permute-start | bytes 98312 | tf_op jit(solution)/shard_map/ppermute | solution.py:12
  50.3 15.5 %collective-permute-start.4 = (f32[2,32,128]{2,1,0:T(8,128)S(1)}, f32[2,32,128]{2,1,0:T(8,128)S(1)}, u32[]{:S(2)}, u32[]{:S(2)}) collective-permute-start(f32[2,32,128]{2,1,0:T(8,128)S(1)} %fusion.14), channel_id=1, source_target_pairs={{0,24},{8,32},{16,40},{24,48},{32,56},{40,64},{48,72},{56,80},{64,... | collective-permute-start | bytes 98312 | tf_op jit(solution)/shard_map/ppermute | solution.py:12
  86.6 156.1 %reduce-scatter.5.cloned.1.call-start = ((), (), s32[]{:S(2)}) async-start(), calls=%async_computation.3 | async-start | bytes 294912 | tf_op jit(solution)/shard_map/reduce_scatter | solution.py:60
  145.6 31.3 %collective-permute-start.14 = (f32[2,32,128]{2,1,0:T(8,128)S(1)}, f32[2,32,128]{2,1,0:T(8,128)S(1)}, u32[]{:S(2)}, u32[]{:S(2)}) collective-permute-start(f32[2,32,128]{2,1,0:T(8,128)S(1)} %bitcast.360), channel_id=1, source_target_pairs={{0,56},{8,64},{16,72},{24,80},{32,88},{40,96},{48,104},{56,112},{6... | collective-permute-start | bytes 98312 | tf_op jit(solution)/shard_map/ppermute | solution.py:12
  160.6 18.8 %collective-permute-start.15 = (f32[2,32,128]{2,1,0:T(8,128)S(1)}, f32[2,32,128]{2,1,0:T(8,128)S(1)}, u32[]{:S(2)}, u32[]{:S(2)}) collective-permute-start(f32[2,32,128]{2,1,0:T(8,128)S(1)} %bitcast.361), channel_id=1, source_target_pairs={{0,48},{8,56},{16,64},{24,72},{32,80},{40,88},{48,96},{56,104},{64... | collective-permute-start | bytes 98312 | tf_op jit(solution)/shard_map/ppermute | solution.py:12
  164.9 16.5 %collective-permute-start.16 = (f32[2,32,128]{2,1,0:T(8,128)S(1)}, f32[2,32,128]{2,1,0:T(8,128)S(1)}, u32[]{:S(2)}, u32[]{:S(2)}) collective-permute-start(f32[2,32,128]{2,1,0:T(8,128)S(1)} %bitcast.362), channel_id=1, source_target_pairs={{0,40},{8,48},{16,56},{24,64},{32,72},{40,80},{48,88},{56,96},{64,... | collective-permute-start | bytes 98312 | tf_op jit(solution)/shard_map/ppermute | solution.py:12
  167.5 16.3 %collective-permute-start.17 = (f32[2,32,128]{2,1,0:T(8,128)S(1)}, f32[2,32,128]{2,1,0:T(8,128)S(1)}, u32[]{:S(2)}, u32[]{:S(2)}) collective-permute-start(f32[2,32,128]{2,1,0:T(8,128)S(1)} %bitcast.363), channel_id=1, source_target_pairs={{0,32},{8,40},{16,48},{24,56},{32,64},{40,72},{48,80},{56,88},{64,... | collective-permute-start | bytes 98312 | tf_op jit(solution)/shard_map/ppermute | solution.py:12
  170.7 14.5 %collective-permute-start.18 = (f32[2,32,128]{2,1,0:T(8,128)S(1)}, f32[2,32,128]{2,1,0:T(8,128)S(1)}, u32[]{:S(2)}, u32[]{:S(2)}) collective-permute-start(f32[2,32,128]{2,1,0:T(8,128)S(1)} %bitcast.364), channel_id=1, source_target_pairs={{0,24},{8,32},{16,40},{24,48},{32,56},{40,64},{48,72},{56,80},{64,... | collective-permute-start | bytes 98312 | tf_op jit(solution)/shard_map/ppermute | solution.py:12
  205.4 141.9 %all-reduce.7.cloned.1.call-start = ((), (), s32[]{:S(2)}) async-start(), calls=%async_computation.4 | async-start | bytes 524288
  263.4 240.6 %all-reduce.9.cloned.1.call-start = ((), (), s32[]{:S(2)}) async-start(), calls=%async_computation.5 | async-start | bytes 524288
  368.7 31.3 %collective-permute-start.41 = (f32[2,2,32,128]{3,2,1,0:T(8,128)S(1)}, f32[2,2,32,128]{3,2,1,0:T(8,128)S(1)}, u32[]{:S(2)}, u32[]{:S(2)}) collective-permute-start(f32[2,2,32,128]{3,2,1,0:T(8,128)S(1)} %bitcast.388), channel_id=1, source_target_pairs={{0,56},{8,64},{16,72},{24,80},{32,88},{40,96},{48,104},{56,112},{6... | collective-permute-start | bytes 196616 | tf_op jit(solution)/shard_map/ppermute | solution.py:12
  383.7 18.8 %collective-permute-start.40 = (f32[2,2,32,128]{3,2,1,0:T(8,128)S(1)}, f32[2,2,32,128]{3,2,1,0:T(8,128)S(1)}, u32[]{:S(2)}, u32[]{:S(2)}) collective-permute-start(f32[2,2,32,128]{3,2,1,0:T(8,128)S(1)} %bitcast.387), channel_id=1, source_target_pairs={{0,48},{8,56},{16,64},{24,72},{32,80},{40,88},{48,96},{56,104},{64... | collective-permute-start | bytes 196616 | tf_op jit(solution)/shard_map/ppermute | solution.py:12
  388.0 16.5 %collective-permute-start.39 = (f32[2,2,32,128]{3,2,1,0:T(8,128)S(1)}, f32[2,2,32,128]{3,2,1,0:T(8,128)S(1)}, u32[]{:S(2)}, u32[]{:S(2)}) collective-permute-start(f32[2,2,32,128]{3,2,1,0:T(8,128)S(1)} %bitcast.386), channel_id=1, source_target_pairs={{0,40},{8,48},{16,56},{24,64},{32,72},{40,80},{48,88},{56,96},{64,... | collective-permute-start | bytes 196616 | tf_op jit(solution)/shard_map/ppermute | solution.py:12
  390.5 16.4 %collective-permute-start.38 = (f32[2,2,32,128]{3,2,1,0:T(8,128)S(1)}, f32[2,2,32,128]{3,2,1,0:T(8,128)S(1)}, u32[]{:S(2)}, u32[]{:S(2)}) collective-permute-start(f32[2,2,32,128]{3,2,1,0:T(8,128)S(1)} %bitcast.385), channel_id=1, source_target_pairs={{0,32},{8,40},{16,48},{24,56},{32,64},{40,72},{48,80},{56,88},{64,... | collective-permute-start | bytes 196616 | tf_op jit(solution)/shard_map/ppermute | solution.py:12
  393.8 14.4 %collective-permute-start.37 = (f32[2,2,32,128]{3,2,1,0:T(8,128)S(1)}, f32[2,2,32,128]{3,2,1,0:T(8,128)S(1)}, u32[]{:S(2)}, u32[]{:S(2)}) collective-permute-start(f32[2,2,32,128]{3,2,1,0:T(8,128)S(1)} %bitcast.384), channel_id=1, source_target_pairs={{0,24},{8,32},{16,40},{24,48},{32,56},{40,64},{48,72},{56,80},{64,... | collective-permute-start | bytes 196616 | tf_op jit(solution)/shard_map/ppermute | solution.py:12
  427.8 231.4 %all-reduce.11.cloned.1.call-start = ((), (), s32[]{:S(2)}) async-start(), calls=%async_computation.6 | async-start | bytes 524288
  524.5 31.3 %collective-permute-start.55 = (f32[1,2,32,128]{3,2,1,0:T(8,128)S(1)}, f32[1,2,32,128]{3,2,1,0:T(8,128)S(1)}, u32[]{:S(2)}, u32[]{:S(2)}) collective-permute-start(f32[1,2,32,128]{3,2,1,0:T(8,128)S(1)} %get-tuple-element.21), channel_id=1, source_target_pairs={{0,56},{8,64},{16,72},{24,80},{32,88},{40,96},{48,104},{56,112},{6... | collective-permute-start | bytes 98312 | tf_op jit(solution)/shard_map/ppermute | solution.py:12
  539.5 18.8 %collective-permute-start.54 = (f32[1,2,32,128]{3,2,1,0:T(8,128)S(1)}, f32[1,2,32,128]{3,2,1,0:T(8,128)S(1)}, u32[]{:S(2)}, u32[]{:S(2)}) collective-permute-start(f32[1,2,32,128]{3,2,1,0:T(8,128)S(1)} %get-tuple-element.22), channel_id=1, source_target_pairs={{0,48},{8,56},{16,64},{24,72},{32,80},{40,88},{48,96},{56,104},{64... | collective-permute-start | bytes 98312 | tf_op jit(solution)/shard_map/ppermute | solution.py:12
  543.8 16.5 %collective-permute-start.53 = (f32[1,2,32,128]{3,2,1,0:T(8,128)S(1)}, f32[1,2,32,128]{3,2,1,0:T(8,128)S(1)}, u32[]{:S(2)}, u32[]{:S(2)}) collective-permute-start(f32[1,2,32,128]{3,2,1,0:T(8,128)S(1)} %get-tuple-element.23), channel_id=1, source_target_pairs={{0,40},{8,48},{16,56},{24,64},{32,72},{40,80},{48,88},{56,96},{64,... | collective-permute-start | bytes 98312 | tf_op jit(solution)/shard_map/ppermute | solution.py:12
  546.3 16.4 %collective-permute-start.52 = (f32[1,2,32,128]{3,2,1,0:T(8,128)S(1)}, f32[1,2,32,128]{3,2,1,0:T(8,128)S(1)}, u32[]{:S(2)}, u32[]{:S(2)}) collective-permute-start(f32[1,2,32,128]{3,2,1,0:T(8,128)S(1)} %get-tuple-element.24), channel_id=1, source_target_pairs={{0,32},{8,40},{16,48},{24,56},{32,64},{40,72},{48,80},{56,88},{64,... | collective-permute-start | bytes 98312 | tf_op jit(solution)/shard_map/ppermute | solution.py:12
  (43 other events, 586.3 us)
Sparse Core Ops, SparseCore 0:
  86.7 39.0 reduce-scatter.2
  205.5 37.0 reduce-scatter.4
  263.5 83.7 all-reduce.6
  427.9 76.0 all-reduce.8
  583.1 76.0 all-reduce.10
where the time goes:
time: 673 us; the launch traced here: 667 us
  waiting for transfers between devices  354 us (53%)
  starting transfers between devices  181 us (27%)
  blocking collectives  95.1 us (14%)
  between operations  14.9 us (2%)
  local copies, waits for them, and re-layouts  11.1 us (2%)
  matrix products  8.03 us (1%)
    unnamed x8, waiting for transfers between devices  233 us
    ppermute x56, starting transfers between devices, from_behind(): lax.ppermute(value, axis, [(source, source + steps) for source in range(l...  181 us
    reduce_scatter x2, waiting for transfers between devices, local(): lax.psum_scatter(partial_value, 'cols', scatter_dimension=1, tiled=True)  76.2 us
    all_gather x3, blocking collectives, full_rows(): return lax.all_gather(piece, 'cols', axis=1, tiled=True)  58.3 us
    ppermute x56, waiting for transfers between devices, from_behind(): lax.ppermute(value, axis, [(source, source + steps) for source in range(l...  45.6 us
    all_gather x2, blocking collectives, local(): whole_block = lax.all_gather(own_share, 'cols', axis=1, tiled=True)  36.8 us
  transfers between devices with their start and end apart: 61, of which 25 were waited for; matrix products, arithmetic and copies ran while one was open for 1% of the time, Pallas kernels for 0%

commit v1 on v0

v1 whole, which is shorter than its diff:
```python
import functools

import jax
import jax.numpy as jnp
from jax import lax
from jax.experimental import pallas as pl
from jax.experimental.pallas import tpu as pltpu
from jax.sharding import PartitionSpec as P

KDEV = 7
MESH = pl.DeviceIdType.MESH
OFFSETS = [d for d in range(-KDEV, KDEV + 1) if d != 0]


def _params(cid):
    return pltpu.CompilerParams(collective_id=cid, has_side_effects=True)


def _vmem():
    return pl.BlockSpec(memory_space=pltpu.VMEM)


def _cols_barrier(n, me, row):
    barrier = pltpu.get_barrier_semaphore()
    for k in range(1, n):
        pl.semaphore_signal(
            barrier, 1, device_id=(row, lax.rem(me + k, n)), device_id_type=MESH
        )
    pl.semaphore_wait(barrier, n - 1)


def _cols_copy(src_ref, dst_ref, send, recv, row, peer):
    return pltpu.make_async_remote_copy(
        src_ref=src_ref,
        dst_ref=dst_ref,
        send_sem=send,
        recv_sem=recv,
        device_id=(row, peer),
        device_id_type=MESH,
    )


def _scatter_phase(n, me, row, x_ref, base_ref, got, send, recv):
    sends = []
    for k in range(1, n):
        peer = lax.rem(me + k, n)
        c = _cols_copy(x_ref.at[peer], got.at[me], send.at[peer], recv.at[me], row, peer)
        c.start()
        sends.append(c)
    acc = base_ref[...] + x_ref[me]
    for k in range(1, n):
        src = lax.rem(me + n - k, n)
        c = _cols_copy(x_ref.at[src], got.at[src], send.at[src], recv.at[src], row, src)
        c.wait_recv()
        acc = acc + got[src]
    for c in sends:
        c.wait_send()
    return acc


def _gather_phase(n, me, row, src_ref, got, out_ref, send, recv):
    sends = []
    for k in range(1, n):
        peer = lax.rem(me + k, n)
        c = _cols_copy(src_ref, got.at[me], send.at[peer], recv.at[me], row, peer)
        c.start()
        sends.append(c)
    out_ref[me] = src_ref[...]
    for k in range(1, n):
        src = lax.rem(me + n - k, n)
        c = _cols_copy(src_ref, got.at[src], send.at[src], recv.at[src], row, src)
        c.wait_recv()
        out_ref[src] = got[src]
    for c in sends:
        c.wait_send()


def _allreduce_kernel(x_ref, base_ref, full_ref, own_ref, got1, got2, red, s1, r1, s2, r2):
    n = x_ref.shape[0]
    me = lax.axis_index("cols")
    row = lax.axis_index("rows")
    _cols_barrier(n, me, row)
    acc = _scatter_phase(n, me, row, x_ref, base_ref, got1, s1, r1)
    red[...] = acc
    own_ref[...] = acc
    _gather_phase(n, me, row, red, got2, full_ref, s2, r2)


def _reduce_scatter_kernel(x_ref, base_ref, own_ref, got1, s1, r1):
    n = x_ref.shape[0]
    me = lax.axis_index("cols")
    row = lax.axis_index("rows")
    _cols_barrier(n, me, row)
    own_ref[...] = _scatter_phase(n, me, row, x_ref, base_ref, got1, s1, r1)


def _all_gather_kernel(y_ref, full_ref, got2, s2, r2):
    n = full_ref.shape[0]
    me = lax.axis_index("cols")
    row = lax.axis_index("rows")
    _cols_barrier(n, me, row)
    _gather_phase(n, me, row, y_ref, got2, full_ref, s2, r2)


def cols_allreduce(x, base, cid):
    n = x.shape[0]
    blk = base.shape
    return pl.pallas_call(
        _allreduce_kernel,
        out_shape=(
            jax.ShapeDtypeStruct((n,) + blk, jnp.float32),
            jax.ShapeDtypeStruct(blk, jnp.float32),
        ),
        in_specs=[_vmem(), _vmem()],
        out_specs=(_vmem(), _vmem()),
        scratch_shapes=[
            pltpu.VMEM((n,) + blk, jnp.float32),
            pltpu.VMEM((n,) + blk, jnp.float32),
            pltpu.VMEM(blk, jnp.float32),
            pltpu.SemaphoreType.DMA((n,)),
            pltpu.SemaphoreType.DMA((n,)),
            pltpu.SemaphoreType.DMA((n,)),
            pltpu.SemaphoreType.DMA((n,)),
        ],
        compiler_params=_params(cid),
    )(x, base)


def cols_reduce_scatter(x, base, cid):
    n = x.shape[0]
    blk = base.shape
    return pl.pallas_call(
        _reduce_scatter_kernel,
        out_shape=jax.ShapeDtypeStruct(blk, jnp.float32),
        in_specs=[_vmem(), _vmem()],
        out_specs=_vmem(),
        scratch_shapes=[
            pltpu.VMEM((n,) + blk, jnp.float32),
            pltpu.SemaphoreType.DMA((n,)),
            pltpu.SemaphoreType.DMA((n,)),
        ],
        compiler_params=_params(cid),
    )(x, base)


def cols_all_gather(y, n, cid):
    blk = y.shape
    return pl.pallas_call(
        _all_gather_kernel,
        out_shape=jax.ShapeDtypeStruct((n,) + blk, jnp.float32),
        in_specs=[_vmem()],
        out_specs=_vmem(),
        scratch_shapes=[
            pltpu.VMEM((n,) + blk, jnp.float32),
            pltpu.SemaphoreType.DMA((n,)),
            pltpu.SemaphoreType.DMA((n,)),
        ],
        compiler_params=_params(cid),
    )(y)


def _rows_barrier(count, me, col):
    barrier = pltpu.get_barrier_semaphore()
    for d in OFFSETS:
        pl.semaphore_signal(
            barrier, 1, device_id=(lax.rem(me + d + count, count), col), device_id_type=MESH
        )
    pl.semaphore_wait(barrier, len(OFFSETS))


def _rows_copy(src_ref, dst_ref, send, recv, target, col):
    return pltpu.make_async_remote_copy(
        src_ref=src_ref,
        dst_ref=dst_ref,
        send_sem=send,
        recv_sem=recv,
        device_id=(target, col),
        device_id_type=MESH,
    )


def _rows_bcast_kernel(count, v_ref, win_ref, got, send, recv):
    me = lax.axis_index("rows")
    col = lax.axis_index("cols")
    _rows_barrier(count, me, col)
    sends = []
    for d in OFFSETS:
        target = lax.rem(me + d + count, count)
        c = _rows_copy(v_ref, got.at[KDEV - d], send.at[KDEV + d], recv.at[KDEV - d], target, col)
        c.start()
        sends.append(c)
    win_ref[KDEV] = v_ref[...]
    for o in OFFSETS:
        w = KDEV + o
        source = lax.rem(me + o + count, count)
        c = _rows_copy(v_ref, got.at[w], send.at[w], recv.at[w], source, col)
        c.wait_recv()
        win_ref[w] = got[w]
    for c in sends:
        c.wait_send()


def _rows_reduce_kernel(count, x_ref, sum_ref, got, send, recv):
    me = lax.axis_index("rows")
    col = lax.axis_index("cols")
    _rows_barrier(count, me, col)
    sends = []
    for d in OFFSETS:
        target = lax.rem(me + d + count, count)
        c = _rows_copy(
            x_ref.at[KDEV + d], got.at[KDEV - d], send.at[KDEV + d], recv.at[KDEV - d], target, col
        )
        c.start()
        sends.append(c)
    acc = x_ref[KDEV]
    for o in OFFSETS:
        w = KDEV + o
        source = lax.rem(me + o + count, count)
        c = _rows_copy(x_ref.at[w], got.at[w], send.at[w], recv.at[w], source, col)
        c.wait_recv()
        acc = acc + got[w]
    sum_ref[...] = acc
    for c in sends:
        c.wait_send()


def rows_bcast(v, count, cid):
    slots = 2 * KDEV + 1
    return pl.pallas_call(
        functools.partial(_rows_bcast_kernel, count),
        out_shape=jax.ShapeDtypeStruct((slots,) + v.shape, jnp.float32),
        in_specs=[_vmem()],
        out_specs=_vmem(),
        scratch_shapes=[
            pltpu.VMEM((slots,) + v.shape, jnp.float32),
            pltpu.SemaphoreType.DMA((slots,)),
            pltpu.SemaphoreType.DMA((slots,)),
        ],
        compiler_params=_params(cid),
    )(v)


def rows_reduce(x, count, cid):
    slots = 2 * KDEV + 1
    return pl.pallas_call(
        functools.partial(_rows_reduce_kernel, count),
        out_shape=jax.ShapeDtypeStruct(x.shape[1:], jnp.float32),
        in_specs=[_vmem()],
        out_specs=_vmem(),
        scratch_shapes=[
            pltpu.VMEM(x.shape, jnp.float32),
            pltpu.SemaphoreType.DMA((slots,)),
            pltpu.SemaphoreType.DMA((slots,)),
        ],
        compiler_params=_params(cid),
    )(x)


def to_chunks(block, n):
    s, rows, r = block.shape
    return block.reshape(s, n, rows // n, r).transpose(1, 0, 2, 3)


def from_chunks(chunks):
    n, s, c, r = chunks.shape
    return chunks.transpose(1, 0, 2, 3).reshape(s, n * c, r)


def local(rhs, diag_inv, factor_tiles, tile_source, tile_count):
    levels = rhs.shape[0]
    owned_count = rhs.shape[1]
    share_rows = rhs.shape[2]
    columns = rhs.shape[3]
    slot_count = tile_source.shape[2]
    reach_dev = KDEV
    window_len = 2 * reach_dev + 1
    row_count = lax.axis_size("rows")
    col_count = lax.axis_size("cols")
    total_sup = row_count * owned_count
    row_place = lax.axis_index("rows")
    highest = lax.Precision.HIGHEST
    slot_ids = jnp.arange(slot_count, dtype=jnp.int32)
    ids = iter(range(64))

    def window_places(sources):
        src_level = sources // total_sup
        within = sources % total_sup
        return (
            src_level * window_len + within // owned_count - row_place + reach_dev
        ) * owned_count + within % owned_count

    def live_mask(counts):
        return (slot_ids[None, :] < counts[:, None]).astype(jnp.float32)

    forward_values = []
    windows = []
    for height in range(levels):
        if height == 0:
            whole_block = from_chunks(cols_all_gather(rhs[0], col_count, next(ids)))
        else:
            stacked = jnp.stack(windows, 0).reshape(
                height * window_len * owned_count, share_rows, columns
            )
            places = window_places(tile_source[height - 1])
            picked = (
                jnp.take(stacked, places, axis=0)
                * live_mask(tile_count[height - 1])[:, :, None, None]
            )
            partial_value = jnp.einsum(
                "skci,skcr->sir", factor_tiles[height - 1], picked, precision=highest
            )
            full, unused = cols_allreduce(
                to_chunks(-partial_value, col_count), rhs[height], next(ids)
            )
            whole_block = from_chunks(full)
        values = jnp.einsum("sci,sir->scr", diag_inv[height], whole_block, precision=highest)
        forward_values.append(values)
        if height + 1 < levels:
            windows.append(rows_bcast(values, row_count, next(ids)))
    carried = [jnp.zeros_like(forward_values[0]) for height in range(levels)]
    solution = [None] * levels
    zero_block = jnp.zeros_like(forward_values[0])
    for height in reversed(range(levels)):
        partial_value = jnp.einsum(
            "sci,scr->sir",
            diag_inv[height],
            forward_values[height] - carried[height],
            precision=highest,
        )
        chunks = to_chunks(partial_value, col_count)
        if height > 0:
            full, own_share = cols_allreduce(chunks, zero_block, next(ids))
            whole_block = from_chunks(full)
        else:
            own_share = cols_reduce_scatter(chunks, zero_block, next(ids))
        solution[height] = own_share
        if height > 0:
            term_set = jnp.einsum(
                "skci,sir->skcr", factor_tiles[height - 1], whole_block, precision=highest
            )
            term_set = term_set * live_mask(tile_count[height - 1])[:, :, None, None]
            places = window_places(tile_source[height - 1]).reshape(-1)
            targets = height * window_len * owned_count
            one_hot = (jnp.arange(targets, dtype=jnp.int32)[:, None] == places[None, :]).astype(
                jnp.float32
            )
            outgoing = jnp.einsum(
                "ms,slg->mlg",
                one_hot,
                term_set.reshape(owned_count * slot_count, share_rows, columns),
                precision=highest,
            )
            push_outgoing = outgoing.reshape(height, window_len, owned_count, share_rows, columns)
            received = rows_reduce(
                push_outgoing.transpose(1, 0, 2, 3, 4), row_count, next(ids)
            )
            for lower_level in range(height):
                carried[lower_level] = carried[lower_level] + received[lower_level]
    return jnp.stack(solution, 0)


def solution(mesh):
    placed = (
        P(None, "rows", "cols", None),
        P(None, "rows", "cols", None),
        P(None, "rows", None, "cols", None),
        P(None, "rows", None),
        P(None, "rows"),
    )
    return jax.shard_map(
        local, mesh=mesh, in_specs=placed, out_specs=P(None, "rows", "cols", None), check_vma=False
    )
```

time: 673 us -> 219 us (0.33)
  waiting for transfers between devices: 354 us -> 0 us
  Pallas kernels: 0 us -> 189 us
  starting transfers between devices: 181 us -> 0 us
  blocking collectives: 95.1 us -> 0 us
  between operations: 14.9 us -> 0.37 us
    unnamed x8 -> x0, waiting for transfers between devices: 233 us -> none
    pallas_call x0 -> x10, Pallas kernels: none -> 189 us  [the longest x4 86.8 us: cols_allreduce(): pl.pallas_call(_allreduce_kernel, out_shape=(jax.ShapeDtypeStruct((n,) +...]
    ppermute x56 -> x0, starting transfers between devices: 181 us -> none  [from_behind(): lax.ppermute(value, axis, [(source, source + steps) for source in range(l...]
    all_gather x5 -> x0, blocking collectives: 95.1 us -> none  [the longest x3 58.3 us: full_rows(): return lax.all_gather(piece, 'cols', axis=1, tiled=True)]
    reduce_scatter x2 -> x0, waiting for transfers between devices: 76.2 us -> none  [local(): lax.psum_scatter(partial_value, 'cols', scatter_dimension=1, tiled=True)]
    ppermute x56 -> x0, waiting for transfers between devices: 45.6 us -> none  [from_behind(): lax.ppermute(value, axis, [(source, source + steps) for source in range(l...]
  transfers between devices with their start and end apart: 61 -> 0, of which waited for: 25 -> 0; matrix products, arithmetic and copies ran while one was open for 1% -> 0% of each run, Pallas kernels for 0% -> 0%
where the time goes in v1:
time: 219 us; the launch traced here: 218 us
  Pallas kernels  189 us (86%)
  local copies, waits for them, and re-layouts  17.3 us (8%)
  matrix products  8.55 us (4%)
  other arithmetic  2.7 us (1%)
    pallas_call x4, Pallas kernels, cols_allreduce(): pl.pallas_call(_allreduce_kernel, out_shape=(jax.ShapeDtypeStruct((n,) +...  86.8 us
    pallas_call x2, Pallas kernels, rows_reduce(): pl.pallas_call(functools.partial(_rows_reduce_kernel, count), out_shape=j...  37.8 us
    pallas_call x2, Pallas kernels, rows_bcast(): pl.pallas_call(functools.partial(_rows_bcast_kernel, count), out_shape=ja...  36 us
    pallas_call x1, Pallas kernels, cols_all_gather(): pl.pallas_call(_all_gather_kernel, out_shape=jax.ShapeDtypeStruct((n,) +...  14.4 us
    pallas_call x1, Pallas kernels, cols_reduce_scatter(): pl.pallas_call(_reduce_scatter_kernel, out_shape=jax.ShapeDtypeStruct(blk...  13.7 us
    transpose x5, local copies, waits for them, and re-layouts, from_chunks(): return chunks.transpose(1, 0, 2, 3).reshape(s, n * c, r)  4.93 us

profile of v1, /device:TPU:1, one launch (start us, length us, event | category | flops | bytes accessed | tf_op | source)
XLA Modules:
  0.0 217.5 jit_solution(10713319663809295692)
XLA Ops:
  0.0 1.4 slice_bitcast_fusion
  1.4 14.4 %shard_map.55 = f32[8,2,32,128]{3,2,1,0:T(8,128)} custom-call(f32[2,32,128]{2,1,0:T(8,128)} %get-tuple-element.18.y_ref), custom_call_target="tpu_custom_call" | custom-call | tf_op jit(solution)/shard_map/pallas_call | solution.py:148
  15.8 1.1 copy.10
  17.8 21.8 %shard_map.56 = f32[15,2,32,128]{3,2,1,0:T(8,128)} custom-call(f32[2,32,128]{2,1,0:T(8,128)} %fusion.33.v_ref), custom_call_target="tpu_custom_call" | custom-call | tf_op jit(solution)/shard_map/pallas_call | solution.py:229
  40.4 1.6 gather_fusion
  44.4 21.7 %shard_map.57 = (f32[8,2,32,128]{3,2,1,0:T(8,128)}, f32[2,32,128]{2,1,0:T(8,128)}) custom-call(f32[8,2,32,128]{3,2,1,0:T(8,128)} %bitcast.230, f32[2,32,128]{2,1,0:T(8,128)} %get-tuple-element.19.base_ref), custom_call_target="tpu_custom_call" | custom-call | tf_op jit(solution)/shard_map/pallas_call | solution.py:108
  66.0 1.0 copy.13
  67.0 0.9 convolution_bitcast_fusion.5.v_ref
  67.9 14.2 %shard_map.58 = f32[15,2,32,128]{3,2,1,0:T(8,128)} custom-call(f32[2,32,128]{2,1,0:T(8,128)} %convolution_bitcast_fusion.5.v_ref), custom_call_target="tpu_custom_call" | custom-call | tf_op jit(solution)/shard_map/pallas_call | solution.py:229
  82.1 1.1 pad_maximum_fusion
  85.5 21.4 %shard_map.59 = (f32[8,2,32,128]{3,2,1,0:T(8,128)}, f32[2,32,128]{2,1,0:T(8,128)}) custom-call(f32[8,2,32,128]{3,2,1,0:T(8,128)} %bitcast.228, f32[2,32,128]{2,1,0:T(8,128)} %get-tuple-element.17.base_ref), custom_call_target="tpu_custom_call" | custom-call | tf_op jit(solution)/shard_map/pallas_call | solution.py:108
  106.9 1.0 copy.16
  110.0 22.2 %shard_map.60 = (f32[8,2,32,128]{3,2,1,0:T(8,128)}, f32[2,32,128]{2,1,0:T(8,128)}) custom-call(f32[8,2,32,128]{3,2,1,0:T(8,128)} %bitcast.229, f32[2,32,128]{2,1,0:T(8,128)} %broadcast_in_dim.34.base_ref), custom_call_target="tpu_custom_call" | custom-call | tf_op jit(solution)/shard_map/pallas_call | solution.py:108
  132.2 1.0 copy.19
  134.6 1.3 copy.51
  135.9 20.3 %shard_map.61 = f32[2,2,32,128]{3,2,1,0:T(8,128)} custom-call(f32[15,2,2,32,128]{4,3,2,1,0:T(8,128)} %bitcast.215), custom_call_target="tpu_custom_call" | custom-call | tf_op jit(solution)/shard_map/pallas_call | solution.py:245
  156.1 1.2 convolution_bitcast_fusion.3
  158.2 21.6 %shard_map.62 = (f32[8,2,32,128]{3,2,1,0:T(8,128)}, f32[2,32,128]{2,1,0:T(8,128)}) custom-call(f32[8,2,32,128]{3,2,1,0:T(8,128)} %bitcast.231, f32[2,32,128]{2,1,0:T(8,128)} %broadcast_in_dim.34.base_ref), custom_call_target="tpu_custom_call" | custom-call | tf_op jit(solution)/shard_map/pallas_call | solution.py:108
  179.8 1.0 copy.24
  181.9 0.9 copy.52
  182.8 17.5 %shard_map.63 = f32[1,2,32,128]{3,2,1,0:T(8,128)} custom-call(f32[15,1,2,32,128]{4,3,2,1,0:T(8,128)} %bitcast.218), custom_call_target="tpu_custom_call" | custom-call | tf_op jit(solution)/shard_map/pallas_call | solution.py:245
  200.3 1.2 convolution_bitcast_fusion.2
  202.4 13.7 %shard_map.64 = f32[2,32,128]{2,1,0:T(8,128)} custom-call(f32[8,2,32,128]{3,2,1,0:T(8,128)} %bitcast.227, f32[2,32,128]{2,1,0:T(8,128)} %broadcast_in_dim.34.base_ref), custom_call_target="tpu_custom_call" | custom-call | tf_op jit(solution)/shard_map/pallas_call | solution.py:132
  216.1 1.4 pad_maximum_fusion.1
  (55 shorter events, 12.6 us)
Async XLA Ops:
  1.4 15.5 %copy-start.2 = (f32[3,2,32,256]{3,2,1,0:T(8,128)S(1)}, f32[3,2,32,256]{3,2,1,0:T(8,128)}, u32[]{:S(2)}) copy-start(f32[3,2,32,256]{3,2,1,0:T(8,128)} %param.6) | copy-start | bytes 589828
  15.8 26.9 %copy-start = (f32[2,2,8,32,256]{4,3,2,1,0:T(8,128)S(1)}, f32[2,2,8,32,256]{4,3,2,1,0:T(8,128)}, u32[]{:S(2)}) copy-start(f32[2,2,8,32,256]{4,3,2,1,0:T(8,128)} %param.7) | copy-start | bytes 3145732
  39.6 0.7 copy-start.8
  42.0 0.7 copy-start.9
  67.0 15.1 %copy-start.1 = (f32[15,2,32,128]{3,2,1,0:T(8,128)S(1)}, f32[15,2,32,128]{3,2,1,0:T(8,128)}, u32[]{:S(2)}) copy-start(f32[15,2,32,128]{3,2,1,0:T(8,128)} %shard_map.56) | copy-start | bytes 1474564
  135.9 20.3 %copy-start.3 = (f32[2,32,128]{2,1,0:T(8,128)S(1)}, f32[2,32,128]{2,1,0:T(8,128)}, u32[]{:S(2)}) copy-start(f32[2,32,128]{2,1,0:T(8,128)} %convolution_bitcast_fusion.5.v_ref) | copy-start | bytes 98308
  182.8 17.5 %copy-start.4 = (f32[2,32,128]{2,1,0:T(8,128)S(1)}, f32[2,32,128]{2,1,0:T(8,128)}, u32[]{:S(2)}) copy-start(f32[2,32,128]{2,1,0:T(8,128)} %fusion.33.v_ref) | copy-start | bytes 98308
  182.8 17.5 %copy-start.5 = (f32[2,2,32,128]{3,2,1,0:T(8,128)S(1)}, f32[2,2,32,128]{3,2,1,0:T(8,128)}, u32[]{:S(2)}) copy-start(f32[2,2,32,128]{3,2,1,0:T(8,128)} %shard_map.61) | copy-start | bytes 196612
  202.4 13.8 %copy-start.6 = (f32[2,32,128]{2,1,0:T(8,128)S(1)}, f32[2,32,128]{2,1,0:T(8,128)}, u32[]{:S(2)}) copy-start(f32[2,32,128]{2,1,0:T(8,128)} %get-tuple-element.16) | copy-start | bytes 98308
  202.4 13.8 %copy-start.7 = (f32[2,32,128]{2,1,0:T(8,128)S(1)}, f32[2,32,128]{2,1,0:T(8,128)}, u32[]{:S(2)}) copy-start(f32[2,32,128]{2,1,0:T(8,128)} %get-tuple-element.15) | copy-start | bytes 98308

commit v2 on v1

--- a/solution.py
+++ b/solution.py
@@ -40,99 +40,62 @@
     )
 
 
-def _scatter_phase(n, me, row, x_ref, base_ref, got, send, recv):
-    sends = []
-    for k in range(1, n):
-        peer = lax.rem(me + k, n)
-        c = _cols_copy(x_ref.at[peer], got.at[me], send.at[peer], recv.at[me], row, peer)
-        c.start()
-        sends.append(c)
-    acc = base_ref[...] + x_ref[me]
-    for k in range(1, n):
-        src = lax.rem(me + n - k, n)
-        c = _cols_copy(x_ref.at[src], got.at[src], send.at[src], recv.at[src], row, src)
-        c.wait_recv()
-        acc = acc + got[src]
-    for c in sends:
-        c.wait_send()
-    return acc
-
-
-def _gather_phase(n, me, row, src_ref, got, out_ref, send, recv):
-    sends = []
-    for k in range(1, n):
-        peer = lax.rem(me + k, n)
-        c = _cols_copy(src_ref, got.at[me], send.at[peer], recv.at[me], row, peer)
-        c.start()
-        sends.append(c)
-    out_ref[me] = src_ref[...]
-    for k in range(1, n):
-        src = lax.rem(me + n - k, n)
-        c = _cols_copy(src_ref, got.at[src], send.at[src], recv.at[src], row, src)
-        c.wait_recv()
-        out_ref[src] = got[src]
-    for c in sends:
-        c.wait_send()
-
-
-def _allreduce_kernel(x_ref, base_ref, full_ref, own_ref, got1, got2, red, s1, r1, s2, r2):
-    n = x_ref.shape[0]
+def _rows_of(ref, index, chunk):
+    return ref.at[:, pl.ds(pl.multiple_of(index * chunk, chunk), chunk), :]
+
+
+def _reduce_scatter_kernel(x_ref, own_ref, got, send, recv):
+    n = got.shape[0]
+    chunk = got.shape[2]
     me = lax.axis_index("cols")
     row = lax.axis_index("rows")
     _cols_barrier(n, me, row)
-    acc = _scatter_phase(n, me, row, x_ref, base_ref, got1, s1, r1)
-    red[...] = acc
+    sends = []
+    for k in range(1, n):
+        peer = lax.rem(me + k, n)
+        c = _cols_copy(_rows_of(x_ref, peer, chunk), got.at[me], send.at[peer], recv.at[me], row, peer)
+        c.start()
+        sends.append(c)
+    acc = _rows_of(x_ref, me, chunk)[...]
+    for k in range(1, n):
+        src = lax.rem(me + n - k, n)
+        c = _cols_copy(_rows_of(x_ref, src, chunk), got.at[src], send.at[src], recv.at[src], row, src)
+        c.wait_recv()
+        acc = acc + got[src]
     own_ref[...] = acc
-    _gather_phase(n, me, row, red, got2, full_ref, s2, r2)
-
-
-def _reduce_scatter_kernel(x_ref, base_ref, own_ref, got1, s1, r1):
-    n = x_ref.shape[0]
+    for c in sends:
+        c.wait_send()
+
+
+def _all_gather_kernel(y_ref, full_ref, got, send, recv):
+    n = got.shape[0]
+    chunk = got.shape[2]
     me = lax.axis_index("cols")
     row = lax.axis_index("rows")
     _cols_barrier(n, me, row)
-    own_ref[...] = _scatter_phase(n, me, row, x_ref, base_ref, got1, s1, r1)
-
-
-def _all_gather_kernel(y_ref, full_ref, got2, s2, r2):
-    n = full_ref.shape[0]
-    me = lax.axis_index("cols")
-    row = lax.axis_index("rows")
-    _cols_barrier(n, me, row)
-    _gather_phase(n, me, row, y_ref, got2, full_ref, s2, r2)
-
-
-def cols_allreduce(x, base, cid):
-    n = x.shape[0]
-    blk = base.shape
-    return pl.pallas_call(
-        _allreduce_kernel,
-        out_shape=(
-            jax.ShapeDtypeStruct((n,) + blk, jnp.float32),
-            jax.ShapeDtypeStruct(blk, jnp.float32),
-        ),
-        in_specs=[_vmem(), _vmem()],
-        out_specs=(_vmem(), _vmem()),
-        scratch_shapes=[
-            pltpu.VMEM((n,) + blk, jnp.float32),
-            pltpu.VMEM((n,) + blk, jnp.float32),
-            pltpu.VMEM(blk, jnp.float32),
-            pltpu.SemaphoreType.DMA((n,)),
-            pltpu.SemaphoreType.DMA((n,)),
-            pltpu.SemaphoreType.DMA((n,)),
-            pltpu.SemaphoreType.DMA((n,)),
-        ],
-        compiler_params=_params(cid),
-    )(x, base)
-
-
-def cols_reduce_scatter(x, base, cid):
-    n = x.shape[0]
-    blk = base.shape
+    sends = []
+    for k in range(1, n):
+        peer = lax.rem(me + k, n)
+        c = _cols_copy(y_ref, got.at[me], send.at[peer], recv.at[me], row, peer)
+        c.start()
+        sends.append(c)
+    _rows_of(full_ref, me, chunk)[...] = y_ref[...]
+    for k in range(1, n):
+        src = lax.rem(me + n - k, n)
+        c = _cols_copy(y_ref, got.at[src], send.at[src], recv.at[src], row, src)
+        c.wait_recv()
+        _rows_of(full_ref, src, chunk)[...] = got[src]
+    for c in sends:
+        c.wait_send()
+
+
+def cols_reduce_scatter(x, n, cid):
+    s, rows, r = x.shape
+    blk = (s, rows // n, r)
     return pl.pallas_call(
         _reduce_scatter_kernel,
         out_shape=jax.ShapeDtypeStruct(blk, jnp.float32),
-        in_specs=[_vmem(), _vmem()],
+        in_specs=[_vmem()],
         out_specs=_vmem(),
         scratch_shapes=[
             pltpu.VMEM((n,) + blk, jnp.float32),
@@ -140,18 +103,18 @@
             pltpu.SemaphoreType.DMA((n,)),
         ],
         compiler_params=_params(cid),
-    )(x, base)
+    )(x)
 
 
 def cols_all_gather(y, n, cid):
-    blk = y.shape
+    s, chunk, r = y.shape
     return pl.pallas_call(
         _all_gather_kernel,
-        out_shape=jax.ShapeDtypeStruct((n,) + blk, jnp.float32),
+        out_shape=jax.ShapeDtypeStruct((s, n * chunk, r), jnp.float32),
         in_specs=[_vmem()],
         out_specs=_vmem(),
         scratch_shapes=[
-            pltpu.VMEM((n,) + blk, jnp.float32),
+            pltpu.VMEM((n,) + y.shape, jnp.float32),
             pltpu.SemaphoreType.DMA((n,)),
             pltpu.SemaphoreType.DMA((n,)),
         ],
@@ -256,16 +219,6 @@
     )(x)
 
 
-def to_chunks(block, n):
-    s, rows, r = block.shape
-    return block.reshape(s, n, rows // n, r).transpose(1, 0, 2, 3)
-
-
-def from_chunks(chunks):
-    n, s, c, r = chunks.shape
-    return chunks.transpose(1, 0, 2, 3).reshape(s, n * c, r)
-
-
 def local(rhs, diag_inv, factor_tiles, tile_source, tile_count):
     levels = rhs.shape[0]
     owned_count = rhs.shape[1]
@@ -278,9 +231,11 @@
     col_count = lax.axis_size("cols")
     total_sup = row_count * owned_count
     row_place = lax.axis_index("rows")
+    my_rows = lax.axis_index("cols") * share_rows
     highest = lax.Precision.HIGHEST
     slot_ids = jnp.arange(slot_count, dtype=jnp.int32)
     ids = iter(range(64))
+    diag_whole = lax.all_gather(diag_inv[1:], "cols", axis=2, tiled=True)
 
     def window_places(sources):
         src_level = sources // total_sup
@@ -292,11 +247,15 @@
     def live_mask(counts):
         return (slot_ids[None, :] < counts[:, None]).astype(jnp.float32)
 
+    def own_rows(block):
+        return lax.dynamic_slice_in_dim(block, my_rows, share_rows, axis=1)
+
     forward_values = []
     windows = []
     for height in range(levels):
         if height == 0:
-            whole_block = from_chunks(cols_all_gather(rhs[0], col_count, next(ids)))
+            whole_block = cols_all_gather(rhs[0], col_count, next(ids))
+            values = jnp.einsum("sci,sir->scr", diag_inv[0], whole_block, precision=highest)
         else:
             stacked = jnp.stack(windows, 0).reshape(
                 height * window_len * owned_count, share_rows, columns
@@ -309,31 +268,31 @@
             partial_value = jnp.einsum(
                 "skci,skcr->sir", factor_tiles[height - 1], picked, precision=highest
             )
-            full, unused = cols_allreduce(
-                to_chunks(-partial_value, col_count), rhs[height], next(ids)
-            )
-            whole_block = from_chunks(full)
-        values = jnp.einsum("sci,sir->scr", diag_inv[height], whole_block, precision=highest)
+            share = lax.dynamic_update_slice_in_dim(
+                -partial_value, rhs[height] - own_rows(partial_value), my_rows, axis=1
+            )
+            spread = jnp.einsum(
+                "sij,sjr->sir", diag_whole[height - 1], share, precision=highest
+            )
+            values = cols_reduce_scatter(spread, col_count, next(ids))
         forward_values.append(values)
         if height + 1 < levels:
             windows.append(rows_bcast(values, row_count, next(ids)))
     carried = [jnp.zeros_like(forward_values[0]) for height in range(levels)]
     solution = [None] * levels
-    zero_block = jnp.zeros_like(forward_values[0])
     for height in reversed(range(levels)):
-        partial_value = jnp.einsum(
-            "sci,scr->sir",
-            diag_inv[height],
-            forward_values[height] - carried[height],
-            precision=highest,
-        )
-        chunks = to_chunks(partial_value, col_count)
+        residual = forward_values[height] - carried[height]
         if height > 0:
-            full, own_share = cols_allreduce(chunks, zero_block, next(ids))
-            whole_block = from_chunks(full)
+            whole_residual = cols_all_gather(residual, col_count, next(ids))
+            whole_block = jnp.einsum(
+                "sji,sjr->sir", diag_whole[height - 1], whole_residual, precision=highest
+            )
+            solution[height] = own_rows(whole_block)
         else:
-            own_share = cols_reduce_scatter(chunks, zero_block, next(ids))
-        solution[height] = own_share
+            partial_value = jnp.einsum(
+                "sci,scr->sir", diag_inv[0], residual, precision=highest
+            )
+            solution[height] = cols_reduce_scatter(partial_value, col_count, next(ids))
         if height > 0:
             term_set = jnp.einsum(
                 "skci,sir->skcr", factor_tiles[height - 1], whole_block, precision=highest

time: 219 us -> 204 us (0.932)
  Pallas kernels: 189 us -> 158 us
  between operations: 0.37 us -> 13.7 us
  local copies, waits for them, and re-layouts: 17.3 us -> 11 us
  matrix products: 8.55 us -> 14.6 us
    pallas_call x5 -> x3, Pallas kernels: 101 us -> 41.8 us  [cols_all_gather(): pl.pallas_call(_all_gather_kernel, out_shape=jax.ShapeDtypeStruct((s, n *...]
    pallas_call x1 -> x3, Pallas kernels: 13.7 us -> 39.6 us  [cols_reduce_scatter(): pl.pallas_call(_reduce_scatter_kernel, out_shape=jax.ShapeDtypeStruct(blk...]
    dot_general x6, matrix products: 4.79 us -> 10.9 us  [the longest x2 3.66 us: local(): jnp.einsum('sij,sjr->sir', diag_whole[height - 1], share, precision=highest)]
    transpose x5 -> x0, local copies, waits for them, and re-layouts: 4.93 us -> none  [from_chunks(): return chunks.transpose(1, 0, 2, 3).reshape(s, n * c, r)]
    pallas_call x2, Pallas kernels: 36 us -> 40.8 us  [rows_bcast(): pl.pallas_call(functools.partial(_rows_bcast_kernel, count), out_shape=ja...]
    reshape x5 -> x0, local copies, waits for them, and re-layouts: 3.62 us -> none  [to_chunks(): return block.reshape(s, n, rows // n, r).transpose(1, 0, 2, 3)]
  transfers between devices with their start and end apart: 0 -> 1, of which waited for: 0 -> 0; matrix products, arithmetic and copies ran while one was open for 0% -> 3% of each run, Pallas kernels for 0% -> 18%
where the time goes in v2:
time: 204 us; the launch traced here: 202 us
  Pallas kernels  158 us (77%)
  matrix products  14.6 us (7%)
  between operations  13.7 us (7%)
  local copies, waits for them, and re-layouts  11 us (5%)
  other arithmetic  4.33 us (2%)
    pallas_call x3, Pallas kernels, cols_all_gather(): pl.pallas_call(_all_gather_kernel, out_shape=jax.ShapeDtypeStruct((s, n *...  41.8 us
    pallas_call x2, Pallas kernels, rows_bcast(): pl.pallas_call(functools.partial(_rows_bcast_kernel, count), out_shape=ja...  40.8 us
    pallas_call x3, Pallas kernels, cols_reduce_scatter(): pl.pallas_call(_reduce_scatter_kernel, out_shape=jax.ShapeDtypeStruct(blk...  39.6 us
    pallas_call x2, Pallas kernels, rows_reduce(): pl.pallas_call(functools.partial(_rows_reduce_kernel, count), out_shape=j...  35.9 us
  transfers between devices with their start and end apart: 1, of which 0 were waited for; matrix products, arithmetic and copies ran while one was open for 3% of the time, Pallas kernels for 18%

profile of v2, /device:TPU:1, one launch (start us, length us, event | category | flops | bytes accessed | tf_op | source)
XLA Modules:
  0.0 201.9 jit_solution(10957962840238991812)
XLA Ops:
  6.5 1.6 slice.61
  8.1 0.9 copy-done.6
  9.6 14.4 %shard_map.55 = f32[2,256,128]{2,1,0:T(8,128)} custom-call(f32[2,32,128]{2,1,0:T(8,128)} %get-tuple-element.7.y_ref), custom_call_target="tpu_custom_call" | custom-call | tf_op jit(solution)/shard_map/pallas_call | solution.py:111
  24.0 1.9 fusion.28.v_ref
  25.9 21.8 %shard_map.56 = f32[15,2,32,128]{3,2,1,0:T(8,128)} custom-call(f32[2,32,128]{2,1,0:T(8,128)} %fusion.28.v_ref), custom_call_target="tpu_custom_call" | custom-call | tf_op jit(solution)/shard_map/pallas_call | solution.py:192
  49.0 1.6 gather_fusion
  53.0 2.4 %convolution_bitcast_fusion.2.x_ref = f32[2,256,128]{2,1,0:T(8,128)} fusion(f32[2,256,128]{1,2,0:T(8,128)S(1)} %dynamic_update_slice.6, f32[2,2,256,256]{3,2,1,0:T(8,128)} %all-gather.2.cloned.1.call-done), kind=kOutput, calls=%fused_computation.6 | convolution fusion | flops 201326592 | bytes 1048576 | tf_op jit(solution)/shard_map/sij,sjr->sir/dot_general | solution.py:274
  55.3 11.3 %shard_map.57.v_ref = f32[2,32,128]{2,1,0:T(8,128)} custom-call(f32[2,256,128]{2,1,0:T(8,128)} %convolution_bitcast_fusion.2.x_ref), custom_call_target="tpu_custom_call" | custom-call | tf_op jit(solution)/shard_map/pallas_call | solution.py:95
  66.6 19.0 %shard_map.58 = f32[15,2,32,128]{3,2,1,0:T(8,128)} custom-call(f32[2,32,128]{2,1,0:T(8,128)} %shard_map.57.v_ref), custom_call_target="tpu_custom_call" | custom-call | tf_op jit(solution)/shard_map/pallas_call | solution.py:192
  85.6 1.1 pad_maximum_fusion
  88.9 1.3 convolution_bitcast_fusion.x_ref
  90.2 14.2 %shard_map.59.y_ref = f32[2,32,128]{2,1,0:T(8,128)} custom-call(f32[2,256,128]{2,1,0:T(8,128)} %convolution_bitcast_fusion.x_ref), custom_call_target="tpu_custom_call" | custom-call | tf_op jit(solution)/shard_map/pallas_call | solution.py:95
  104.4 13.7 %shard_map.60 = f32[2,256,128]{2,1,0:T(8,128)} custom-call(f32[2,32,128]{2,1,0:T(8,128)} %shard_map.59.y_ref), custom_call_target="tpu_custom_call" | custom-call | tf_op jit(solution)/shard_map/pallas_call | solution.py:111
  118.1 1.6 fusion.5
  121.0 1.3 copy.43
  122.3 19.6 %shard_map.61 = f32[2,2,32,128]{3,2,1,0:T(8,128)} custom-call(f32[15,2,2,32,128]{4,3,2,1,0:T(8,128)} %bitcast.181), custom_call_target="tpu_custom_call" | custom-call | tf_op jit(solution)/shard_map/pallas_call | solution.py:208
  142.0 1.4 bitcast_subtract_fusion.4.y_ref
  143.3 13.7 %shard_map.62 = f32[2,256,128]{2,1,0:T(8,128)} custom-call(f32[2,32,128]{2,1,0:T(8,128)} %bitcast_subtract_fusion.4.y_ref), custom_call_target="tpu_custom_call" | custom-call | tf_op jit(solution)/shard_map/pallas_call | solution.py:111
  157.1 1.6 fusion.4
  160.0 0.9 copy.44
  161.0 16.3 %shard_map.63 = f32[1,2,32,128]{3,2,1,0:T(8,128)} custom-call(f32[15,1,2,32,128]{4,3,2,1,0:T(8,128)} %bitcast.184), custom_call_target="tpu_custom_call" | custom-call | tf_op jit(solution)/shard_map/pallas_call | solution.py:208
  177.3 2.2 %convolution_bitcast_fusion.4.x_ref = f32[2,256,128]{2,1,0:T(8,128)} fusion(f32[3,2,32,256]{3,2,1,0:T(8,128)} %param.6, f32[2,32,128]{2,1,0:T(8,128)S(1)} %copy-done.4, f32[1,2,32,128]{3,2,1,0:T(8,128)} %shard_map.63, f32[2,2,32,128]{3,2,1,0:T(8,128)S(1)} %copy-done.5), kind=kOutput, calls=%fused_computation.8 | convolution fusion | flops 25182208 | bytes 425984 | tf_op jit(solution)/shard_map/sci,scr->sir/dot_general | solution.py:292
  179.4 14.2 %shard_map.64 = f32[2,32,128]{2,1,0:T(8,128)} custom-call(f32[2,256,128]{2,1,0:T(8,128)} %convolution_bitcast_fusion.4.x_ref), custom_call_target="tpu_custom_call" | custom-call | tf_op jit(solution)/shard_map/pallas_call | solution.py:95
  193.6 1.4 pad_maximum_fusion.1
  (54 shorter events, 9.0 us)
Async XLA Ops:
  6.5 46.4 %all-gather.2.cloned.1.call-start = ((), (), s32[]{:S(2)}) async-start(), calls=%async_computation | async-start | bytes 1179648 | tf_op jit(solution)/shard_map/all_gather | solution.py:238
  8.1 0.9 copy-start.6
  9.6 41.7 %copy-start = (f32[2,2,8,32,256]{4,3,2,1,0:T(8,128)S(1)}, f32[2,2,8,32,256]{4,3,2,1,0:T(8,128)}, u32[]{:S(2)}) copy-start(f32[2,2,8,32,256]{4,3,2,1,0:T(8,128)} %param.7) | copy-start | bytes 3145732
  47.7 0.7 copy-start.7
  50.6 0.7 copy-start.8
  55.3 30.2 %copy-start.2 = (f32[15,2,32,128]{3,2,1,0:T(8,128)S(1)}, f32[15,2,32,128]{3,2,1,0:T(8,128)}, u32[]{:S(2)}) copy-start(f32[15,2,32,128]{3,2,1,0:T(8,128)} %shard_map.56) | copy-start | bytes 1474564
  87.3 1.6 copy-start.1
  122.3 19.6 %copy-start.3 = (f32[2,32,128]{2,1,0:T(8,128)S(1)}, f32[2,32,128]{2,1,0:T(8,128)}, u32[]{:S(2)}) copy-start(f32[2,32,128]{2,1,0:T(8,128)} %shard_map.57.v_ref) | copy-start | bytes 98308
  161.0 16.3 %copy-start.4 = (f32[2,32,128]{2,1,0:T(8,128)S(1)}, f32[2,32,128]{2,1,0:T(8,128)}, u32[]{:S(2)}) copy-start(f32[2,32,128]{2,1,0:T(8,128)} %fusion.28.v_ref) | copy-start | bytes 98308
  161.0 16.3 %copy-start.5 = (f32[2,2,32,128]{3,2,1,0:T(8,128)S(1)}, f32[2,2,32,128]{3,2,1,0:T(8,128)}, u32[]{:S(2)}) copy-start(f32[2,2,32,128]{3,2,1,0:T(8,128)} %shard_map.61) | copy-start | bytes 196612
Sparse Core Ops, SparseCore 0:
  9.4 41.6 all-gather.1

commit v3 on v0

v3 whole, which is shorter than its diff:
```python
import functools

import jax
import jax.numpy as jnp
from jax import lax
from jax.experimental import pallas as pl
from jax.experimental.pallas import tpu as pltpu
from jax.sharding import PartitionSpec as P

KDEV = 7
MESH = pl.DeviceIdType.MESH
OFFSETS = [d for d in range(-KDEV, KDEV + 1) if d != 0]


def _params(cid):
    return pltpu.CompilerParams(collective_id=cid, has_side_effects=True)


def _vmem():
    return pl.BlockSpec(memory_space=pltpu.VMEM)


class Place:
    def __init__(self, n, count):
        self.n = n
        self.count = count
        self.col = lax.axis_index("cols")
        self.row = lax.axis_index("rows")

    def col_peer(self, k):
        return lax.rem(self.col + k, self.n)

    def row_peer(self, d):
        return lax.rem(self.row + d + self.count, self.count)

    def barrier(self, cols, rows):
        targets = []
        if cols:
            targets += [(self.row, self.col_peer(k)) for k in range(1, self.n)]
        if rows:
            targets += [(self.row_peer(d), self.col) for d in OFFSETS]
        barrier = pltpu.get_barrier_semaphore()
        for t in targets:
            pl.semaphore_signal(barrier, 1, device_id=t, device_id_type=MESH)
        pl.semaphore_wait(barrier, len(targets))


def _copy(src_ref, dst_ref, send, recv, device):
    return pltpu.make_async_remote_copy(
        src_ref=src_ref,
        dst_ref=dst_ref,
        send_sem=send,
        recv_sem=recv,
        device_id=device,
        device_id_type=MESH,
    )


def _rows_of(ref, index, chunk):
    return ref.at[:, pl.ds(pl.multiple_of(index * chunk, chunk), chunk), :]


def _start_all(copies):
    for c in copies:
        c.start()
    return copies


def _wait_sends(copies):
    for c in copies:
        c.wait_send()


def scatter_start(p, x_ref, got, send, recv):
    chunk = got.shape[2]
    out = []
    for k in range(1, p.n):
        peer = p.col_peer(k)
        out.append(
            _copy(_rows_of(x_ref, peer, chunk), got.at[p.col], send.at[peer], recv.at[p.col], (p.row, peer))
        )
    return _start_all(out)


def scatter_finish(p, x_ref, got, send, recv):
    chunk = got.shape[2]
    acc = _rows_of(x_ref, p.col, chunk)[...]
    for k in range(1, p.n):
        src = p.col_peer(p.n - k)
        _copy(_rows_of(x_ref, src, chunk), got.at[src], send.at[src], recv.at[src], (p.row, src)).wait_recv()
        acc = acc + got[src]
    return acc


def gather_start(p, y_ref, got, send, recv):
    out = []
    for k in range(1, p.n):
        peer = p.col_peer(k)
        out.append(_copy(y_ref, got.at[p.col], send.at[peer], recv.at[p.col], (p.row, peer)))
    return _start_all(out)


def gather_finish(p, y_ref, got, send, recv, full_ref):
    chunk = got.shape[2]
    _rows_of(full_ref, p.col, chunk)[...] = y_ref[...]
    for k in range(1, p.n):
        src = p.col_peer(p.n - k)
        _copy(y_ref, got.at[src], send.at[src], recv.at[src], (p.row, src)).wait_recv()
        _rows_of(full_ref, src, chunk)[...] = got[src]


def bcast_start(p, v_ref, got, send, recv):
    out = []
    for d in OFFSETS:
        out.append(_copy(v_ref, got.at[KDEV - d], send.at[KDEV + d], recv.at[KDEV - d], (p.row_peer(d), p.col)))
    return _start_all(out)


def bcast_finish(p, v_ref, got, send, recv, win_ref):
    win_ref[KDEV] = v_ref[...]
    for o in OFFSETS:
        w = KDEV + o
        _copy(v_ref, got.at[w], send.at[w], recv.at[w], (p.row_peer(o), p.col)).wait_recv()
        win_ref[w] = got[w]


def spread_start(p, x_ref, got, send, recv):
    out = []
    for d in OFFSETS:
        out.append(
            _copy(x_ref.at[KDEV + d], got.at[KDEV - d], send.at[KDEV + d], recv.at[KDEV - d], (p.row_peer(d), p.col))
        )
    return _start_all(out)


def spread_finish(p, x_ref, got, send, recv):
    acc = x_ref[KDEV]
    for o in OFFSETS:
        w = KDEV + o
        _copy(x_ref.at[w], got.at[w], send.at[w], recv.at[w], (p.row_peer(o), p.col)).wait_recv()
        acc = acc + got[w]
    return acc


def _gather_kernel(n, count, y_ref, full_ref, got, s, r):
    p = Place(n, count)
    p.barrier(True, False)
    sends = gather_start(p, y_ref, got, s, r)
    gather_finish(p, y_ref, got, s, r, full_ref)
    _wait_sends(sends)


def _scatter_kernel(n, count, x_ref, own_ref, got, s, r):
    p = Place(n, count)
    p.barrier(True, False)
    sends = scatter_start(p, x_ref, got, s, r)
    own_ref[...] = scatter_finish(p, x_ref, got, s, r)
    _wait_sends(sends)


def _bcast_gather_kernel(n, count, v_ref, d_ref, win_ref, dfull_ref, got_w, sw, rw, got_d, sd, rd):
    p = Place(n, count)
    p.barrier(True, True)
    sends = bcast_start(p, v_ref, got_w, sw, rw) + gather_start(p, d_ref, got_d, sd, rd)
    bcast_finish(p, v_ref, got_w, sw, rw, win_ref)
    gather_finish(p, d_ref, got_d, sd, rd, dfull_ref)
    _wait_sends(sends)


def _scatter_bcast_gather_kernel(
    n, count, x_ref, d_ref, own_ref, win_ref, dfull_ref, got_x, sx, rx, got_w, sw, rw, got_d, sd, rd
):
    p = Place(n, count)
    p.barrier(True, True)
    sends = scatter_start(p, x_ref, got_x, sx, rx)
    own_ref[...] = scatter_finish(p, x_ref, got_x, sx, rx)
    sends += bcast_start(p, own_ref, got_w, sw, rw) + gather_start(p, d_ref, got_d, sd, rd)
    bcast_finish(p, own_ref, got_w, sw, rw, win_ref)
    gather_finish(p, d_ref, got_d, sd, rd, dfull_ref)
    _wait_sends(sends)


def _scatter_gather_kernel(n, count, x_ref, own_ref, full_ref, got_x, sx, rx, got_y, sy, ry):
    p = Place(n, count)
    p.barrier(True, False)
    sends = scatter_start(p, x_ref, got_x, sx, rx)
    own_ref[...] = scatter_finish(p, x_ref, got_x, sx, rx)
    sends += gather_start(p, own_ref, got_y, sy, ry)
    gather_finish(p, own_ref, got_y, sy, ry, full_ref)
    _wait_sends(sends)


def _spread_gather_kernel(n, count, x_ref, f_ref, sum_ref, full_ref, got_b, sb, rb, res, got_y, sy, ry):
    p = Place(n, count)
    p.barrier(True, True)
    sends = spread_start(p, x_ref, got_b, sb, rb)
    acc = spread_finish(p, x_ref, got_b, sb, rb)
    sum_ref[...] = acc
    res[...] = f_ref[...] - acc[acc.shape[0] - 1]
    sends += gather_start(p, res, got_y, sy, ry)
    gather_finish(p, res, got_y, sy, ry, full_ref)
    _wait_sends(sends)


def _spread_kernel(n, count, x_ref, sum_ref, got_b, sb, rb):
    p = Place(n, count)
    p.barrier(False, True)
    sends = spread_start(p, x_ref, got_b, sb, rb)
    sum_ref[...] = spread_finish(p, x_ref, got_b, sb, rb)
    _wait_sends(sends)


def _f32(shape):
    return jax.ShapeDtypeStruct(shape, jnp.float32)


def _dma(k):
    return [pltpu.SemaphoreType.DMA((k,)), pltpu.SemaphoreType.DMA((k,))]


def _call(body, n, count, cid, args, outs, scratch):
    return pl.pallas_call(
        functools.partial(body, n, count),
        out_shape=tuple(_f32(o) for o in outs),
        in_specs=[_vmem() for a in args],
        out_specs=tuple(_vmem() for o in outs),
        scratch_shapes=scratch,
        compiler_params=_params(cid),
    )(*args)


def local(rhs, diag_inv, factor_tiles, tile_source, tile_count):
    levels = rhs.shape[0]
    owned_count = rhs.shape[1]
    share_rows = rhs.shape[2]
    columns = rhs.shape[3]
    slot_count = tile_source.shape[2]
    reach_dev = KDEV
    window_len = 2 * reach_dev + 1
    n = lax.axis_size("cols")
    count = lax.axis_size("rows")
    total_sup = count * owned_count
    row_place = lax.axis_index("rows")
    my_rows = lax.axis_index("cols") * share_rows
    highest = lax.Precision.HIGHEST
    slot_ids = jnp.arange(slot_count, dtype=jnp.int32)
    assert levels == 3 and count >= window_len
    blk = (owned_count, share_rows, columns)
    whole = (owned_count, n * share_rows, columns)
    dblk = diag_inv.shape[1:]
    dwhole = (owned_count, n * share_rows, diag_inv.shape[3])
    win = (window_len,) + blk
    slots = window_len

    def window_places(sources):
        src_level = sources // total_sup
        within = sources % total_sup
        return (
            src_level * window_len + within // owned_count - row_place + reach_dev
        ) * owned_count + within % owned_count

    def live_mask(counts):
        return (slot_ids[None, :] < counts[:, None]).astype(jnp.float32)

    def own_rows(block):
        return lax.dynamic_slice_in_dim(block, my_rows, share_rows, axis=1)

    def forward_share(height, windows):
        stacked = jnp.stack(windows, 0).reshape(height * window_len * owned_count, share_rows, columns)
        places = window_places(tile_source[height - 1])
        picked = jnp.take(stacked, places, axis=0) * live_mask(tile_count[height - 1])[:, :, None, None]
        partial_value = jnp.einsum(
            "skci,skcr->sir", factor_tiles[height - 1], picked, precision=highest
        )
        return lax.dynamic_update_slice_in_dim(
            -partial_value, rhs[height] - own_rows(partial_value), my_rows, axis=1
        )

    def buckets(height, whole_block):
        term_set = jnp.einsum(
            "skci,sir->skcr", factor_tiles[height - 1], whole_block, precision=highest
        )
        term_set = term_set * live_mask(tile_count[height - 1])[:, :, None, None]
        places = window_places(tile_source[height - 1]).reshape(-1)
        targets = height * window_len * owned_count
        one_hot = (jnp.arange(targets, dtype=jnp.int32)[:, None] == places[None, :]).astype(
            jnp.float32
        )
        outgoing = jnp.einsum(
            "ms,slg->mlg",
            one_hot,
            term_set.reshape(owned_count * slot_count, share_rows, columns),
            precision=highest,
        )
        push_outgoing = outgoing.reshape(height, window_len, owned_count, share_rows, columns)
        return push_outgoing.transpose(1, 0, 2, 3, 4)

    (whole0,) = _call(_gather_kernel, n, count, 0, [rhs[0]], [whole], [pltpu.VMEM((n,) + blk, jnp.float32)] + _dma(n))
    fv0 = jnp.einsum("sci,sir->scr", diag_inv[0], whole0, precision=highest)
    win0, d1 = _call(
        _bcast_gather_kernel, n, count, 1, [fv0, diag_inv[1]], [win, dwhole],
        [pltpu.VMEM(win, jnp.float32)] + _dma(slots) + [pltpu.VMEM((n,) + dblk, jnp.float32)] + _dma(n),
    )
    spread1 = jnp.einsum("sij,sjr->sir", d1, forward_share(1, [win0]), precision=highest)
    fv1, win1, d2 = _call(
        _scatter_bcast_gather_kernel, n, count, 2, [spread1, diag_inv[2]], [blk, win, dwhole],
        [pltpu.VMEM((n,) + blk, jnp.float32)] + _dma(n)
        + [pltpu.VMEM(win, jnp.float32)] + _dma(slots)
        + [pltpu.VMEM((n,) + dblk, jnp.float32)] + _dma(n),
    )
    spread2 = jnp.einsum("sij,sjr->sir", d2, forward_share(2, [win0, win1]), precision=highest)
    fv2, whole_res2 = _call(
        _scatter_gather_kernel, n, count, 3, [spread2], [blk, whole],
        [pltpu.VMEM((n,) + blk, jnp.float32)] + _dma(n) + [pltpu.VMEM((n,) + blk, jnp.float32)] + _dma(n),
    )
    sol2 = jnp.einsum("sji,sjr->sir", d2, whole_res2, precision=highest)
    out2 = buckets(2, sol2)
    got2, whole_res1 = _call(
        _spread_gather_kernel, n, count, 4, [out2, fv1], [out2.shape[1:], whole],
        [pltpu.VMEM(out2.shape, jnp.float32)] + _dma(slots)
        + [pltpu.VMEM(blk, jnp.float32), pltpu.VMEM((n,) + blk, jnp.float32)] + _dma(n),
    )
    sol1 = jnp.einsum("sji,sjr->sir", d1, whole_res1, precision=highest)
    out1 = buckets(1, sol1)
    (got1,) = _call(
        _spread_kernel, n, count, 5, [out1], [out1.shape[1:]],
        [pltpu.VMEM(out1.shape, jnp.float32)] + _dma(slots),
    )
    res0 = fv0 - (got2[0] + got1[0])
    partial0 = jnp.einsum("sci,scr->sir", diag_inv[0], res0, precision=highest)
    (sol0,) = _call(_scatter_kernel, n, count, 6, [partial0], [blk], [pltpu.VMEM((n,) + blk, jnp.float32)] + _dma(n))
    return jnp.stack([sol0, own_rows(sol1), own_rows(sol2)], 0)


def solution(mesh):
    placed = (
        P(None, "rows", "cols", None),
        P(None, "rows", "cols", None),
        P(None, "rows", None, "cols", None),
        P(None, "rows", None),
        P(None, "rows"),
    )
    return jax.shard_map(
        local, mesh=mesh, in_specs=placed, out_specs=P(None, "rows", "cols", None), check_vma=False
    )
```

time: 673 us -> 183 us (0.27)
  waiting for transfers between devices: 354 us -> 0 us
  starting transfers between devices: 181 us -> 0 us
  Pallas kernels: 0 us -> 152 us
  blocking collectives: 95.1 us -> 0 us
  between operations: 14.9 us -> 0.32 us
    unnamed x8 -> x0, waiting for transfers between devices: 233 us -> none
    ppermute x56 -> x0, starting transfers between devices: 181 us -> none  [from_behind(): lax.ppermute(value, axis, [(source, source + steps) for source in range(l...]
    pallas_call x0 -> x7, Pallas kernels: none -> 152 us  [_call(): pl.pallas_call(functools.partial(body, n, count), out_shape=tuple((_f32(o...]
    all_gather x5 -> x0, blocking collectives: 95.1 us -> none  [the longest x3 58.3 us: full_rows(): return lax.all_gather(piece, 'cols', axis=1, tiled=True)]
    reduce_scatter x2 -> x0, waiting for transfers between devices: 76.2 us -> none  [local(): lax.psum_scatter(partial_value, 'cols', scatter_dimension=1, tiled=True)]
    ppermute x56 -> x0, waiting for transfers between devices: 45.6 us -> none  [from_behind(): lax.ppermute(value, axis, [(source, source + steps) for source in range(l...]
  transfers between devices with their start and end apart: 61 -> 0, of which waited for: 25 -> 0; matrix products, arithmetic and copies ran while one was open for 1% -> 0% of each run, Pallas kernels for 0% -> 0%
where the time goes in v3:
time: 183 us; the launch traced here: 181 us
  Pallas kernels  152 us (83%)
  matrix products  14.4 us (8%)
  local copies, waits for them, and re-layouts  11.8 us (6%)
  other arithmetic  2.2 us (1%)
    pallas_call x7, Pallas kernels, _call(): pl.pallas_call(functools.partial(body, n, count), out_shape=tuple((_f32(o...  152 us

profile of v3, /device:TPU:1, one launch (start us, length us, event | category | flops | bytes accessed | tf_op | source)
XLA Modules:
  0.0 181.1 jit_solution(12312159442720028894)
XLA Ops:
  0.0 1.5 fusion.52
  1.5 14.3 %shard_map.55 = f32[2,256,128]{2,1,0:T(8,128)} custom-call(f32[2,32,128]{2,1,0:T(8,128)} %get-tuple-element.25.y_ref), custom_call_target="tpu_custom_call" | custom-call | tf_op jit(solution)/shard_map/pallas_call | solution.py:222
  15.8 1.9 %fusion.26.v_ref = f32[2,32,128]{2,1,0:T(8,128)} fusion(f32[2,256,128]{2,1,0:T(8,128)} %shard_map.55, f32[3,2,32,256]{3,2,1,0:T(8,128)} %param.6), kind=kOutput, calls=%fused_computation.41 | convolution fusion | flops 25165824 | bytes 360448 | tf_op jit(solution)/shard_map/sci,sir->scr/dot_general | solution.py:299
  17.6 1.5 slice_bitcast_fusion
  19.2 30.0 %shard_map.56 = (f32[15,2,32,128]{3,2,1,0:T(8,128)}, f32[2,256,256]{2,1,0:T(8,128)}) custom-call(f32[2,32,128]{2,1,0:T(8,128)} %fusion.26.v_ref, f32[2,32,256]{2,1,0:T(8,128)} %get-tuple-element.22.d_ref), custom_call_target="tpu_custom_call" | custom-call | tf_op jit(solution)/shard_map/pallas_call | solution.py:222
  50.0 1.6 gather_fusion
  52.4 0.7 convolution_bitcast_fusion.1
  53.4 0.7 dynamic_update_slice.6
  54.3 1.3 fusion.54.x_ref
  55.6 27.2 %shard_map.57 = (f32[2,32,128]{2,1,0:T(8,128)}, f32[15,2,32,128]{3,2,1,0:T(8,128)}, f32[2,256,256]{2,1,0:T(8,128)}) custom-call(f32[2,256,128]{2,1,0:T(8,128)} %fusion.54.x_ref, f32[2,32,256]{2,1,0:T(8,128)} %get-tuple-element.21.d_ref), custom_call_target="tpu_custom_call" | custom-call | tf_op jit(solution)/shard_map/pallas_call | solution.py:222
  82.8 1.1 pad_maximum_fusion
  84.6 0.7 convolution_bitcast_fusion
  85.6 0.7 dynamic_update_slice.7
  86.5 1.3 fusion.55.x_ref
  87.8 19.9 %shard_map.58 = (f32[2,32,128]{2,1,0:T(8,128)}, f32[2,256,128]{2,1,0:T(8,128)}) custom-call(f32[2,256,128]{2,1,0:T(8,128)} %fusion.55.x_ref), custom_call_target="tpu_custom_call" | custom-call | tf_op jit(solution)/shard_map/pallas_call | solution.py:222
  107.7 2.0 %fusion.56 = f32[2,256,128]{2,1,0:T(8,128)S(1)} fusion(f32[2,256,256]{2,1,0:T(8,128)S(1)} %copy-done.2, f32[2,256,128]{2,1,0:T(8,128)} %get-tuple-element.17), kind=kOutput, calls=%fused_computation.159 | convolution fusion | flops 201326592 | bytes 1048576 | tf_op jit(solution)/shard_map/sji,sjr->sir/dot_general | solution.py:316
  111.1 1.3 copy.39
  112.4 32.9 %shard_map.59 = (f32[2,2,32,128]{3,2,1,0:T(8,128)}, f32[2,256,128]{2,1,0:T(8,128)}) custom-call(f32[15,2,2,32,128]{4,3,2,1,0:T(8,128)} %bitcast.173, f32[2,32,128]{2,1,0:T(8,128)} %get-tuple-element.18.f_ref), custom_call_target="tpu_custom_call" | custom-call | tf_op jit(solution)/shard_map/pallas_call | solution.py:222
  145.3 2.0 %fusion.57 = f32[2,256,128]{2,1,0:T(8,128)S(1)} fusion(f32[2,256,256]{2,1,0:T(8,128)S(1)} %copy-done.1, f32[2,256,128]{2,1,0:T(8,128)} %get-tuple-element.20), kind=kOutput, calls=%fused_computation.160 | convolution fusion | flops 201326592 | bytes 1048576 | tf_op jit(solution)/shard_map/sji,sjr->sir/dot_general | solution.py:323
  148.4 0.9 copy.40
  149.4 13.8 %shard_map.60 = f32[1,2,32,128]{3,2,1,0:T(8,128)} custom-call(f32[15,1,2,32,128]{4,3,2,1,0:T(8,128)} %bitcast.174), custom_call_target="tpu_custom_call" | custom-call | tf_op jit(solution)/shard_map/pallas_call | solution.py:222
  163.3 2.2 %convolution_bitcast_fusion.2.x_ref = f32[2,256,128]{2,1,0:T(8,128)} fusion(f32[3,2,32,256]{3,2,1,0:T(8,128)} %param.6, f32[2,32,128]{2,1,0:T(8,128)S(1)} %copy-done.4, f32[1,2,32,128]{3,2,1,0:T(8,128)} %shard_map.60, f32[2,2,32,128]{3,2,1,0:T(8,128)S(1)} %copy-done.7), kind=kOutput, calls=%fused_computation.6 | convolution fusion | flops 25182208 | bytes 425984 | tf_op jit(solution)/shard_map/sci,scr->sir/dot_general | solution.py:330
  165.4 14.3 %shard_map.61 = f32[2,32,128]{2,1,0:T(8,128)} custom-call(f32[2,256,128]{2,1,0:T(8,128)} %convolution_bitcast_fusion.2.x_ref), custom_call_target="tpu_custom_call" | custom-call | tf_op jit(solution)/shard_map/pallas_call | solution.py:222
  179.8 0.7 copy-done.5
  (45 shorter events, 6.3 us)
Async XLA Ops:
  0.0 52.4 %copy-start = (f32[2,2,8,32,256]{4,3,2,1,0:T(8,128)S(1)}, f32[2,2,8,32,256]{4,3,2,1,0:T(8,128)}, u32[]{:S(2)}) copy-start(f32[2,2,8,32,256]{4,3,2,1,0:T(8,128)} %param.7) | copy-start | bytes 3145732
  49.2 0.7 copy-start.6
  51.6 0.7 copy-start.8
  53.2 1.0 copy-start.1
  54.3 28.6 %copy-start.3 = (f32[15,2,32,128]{3,2,1,0:T(8,128)S(1)}, f32[15,2,32,128]{3,2,1,0:T(8,128)}, u32[]{:S(2)}) copy-start(f32[15,2,32,128]{3,2,1,0:T(8,128)} %get-tuple-element.14) | copy-start | bytes 1474564
  85.4 1.0 copy-start.2
  149.4 13.9 %copy-start.4 = (f32[2,32,128]{2,1,0:T(8,128)S(1)}, f32[2,32,128]{2,1,0:T(8,128)}, u32[]{:S(2)}) copy-start(f32[2,32,128]{2,1,0:T(8,128)} %fusion.26.v_ref) | copy-start | bytes 98308
  149.4 13.9 %copy-start.7 = (f32[2,2,32,128]{3,2,1,0:T(8,128)S(1)}, f32[2,2,32,128]{3,2,1,0:T(8,128)}, u32[]{:S(2)}) copy-start(f32[2,2,32,128]{3,2,1,0:T(8,128)} %get-tuple-element.19) | copy-start | bytes 196612
  179.7 0.8 copy-start.5

commit v4 on v3

--- a/solution.py
+++ b/solution.py
@@ -207,6 +207,76 @@
     p.barrier(False, True)
     sends = spread_start(p, x_ref, got_b, sb, rb)
     sum_ref[...] = spread_finish(p, x_ref, got_b, sb, rb)
+    _wait_sends(sends)
+
+
+def _dots(a_ref, b_ref, transpose_a=False):
+    outs = []
+    for s in range(a_ref.shape[0]):
+        a = a_ref[s]
+        if transpose_a:
+            a = a.T
+        outs.append(jnp.dot(a, b_ref[s], precision=lax.Precision.HIGHEST, preferred_element_type=jnp.float32))
+    return jnp.stack(outs, 0)
+
+
+def _first_kernel(n, count, y_ref, d0_ref, d1_ref, fv_ref, win_ref, dfull_ref, got_y, sy, ry, whole, got_w, sw, rw, got_d, sd, rd):
+    p = Place(n, count)
+    p.barrier(True, True)
+    sends = gather_start(p, y_ref, got_y, sy, ry)
+    gather_finish(p, y_ref, got_y, sy, ry, whole)
+    fv_ref[...] = _dots(d0_ref, whole)
+    sends += bcast_start(p, fv_ref, got_w, sw, rw) + gather_start(p, d1_ref, got_d, sd, rd)
+    bcast_finish(p, fv_ref, got_w, sw, rw, win_ref)
+    gather_finish(p, d1_ref, got_d, sd, rd, dfull_ref)
+    _wait_sends(sends)
+
+
+def _level1_kernel(
+    n, count, share_ref, dw_ref, d_ref, own_ref, win_ref, dfull_ref, x_ref, got_x, sx, rx, got_w, sw, rw, got_d, sd, rd
+):
+    p = Place(n, count)
+    p.barrier(True, True)
+    x_ref[...] = _dots(dw_ref, share_ref)
+    sends = scatter_start(p, x_ref, got_x, sx, rx)
+    own_ref[...] = scatter_finish(p, x_ref, got_x, sx, rx)
+    sends += bcast_start(p, own_ref, got_w, sw, rw) + gather_start(p, d_ref, got_d, sd, rd)
+    bcast_finish(p, own_ref, got_w, sw, rw, win_ref)
+    gather_finish(p, d_ref, got_d, sd, rd, dfull_ref)
+    _wait_sends(sends)
+
+
+def _level2_kernel(n, count, share_ref, dw_ref, own_ref, sol_ref, x_ref, got_x, sx, rx, full, got_y, sy, ry):
+    p = Place(n, count)
+    p.barrier(True, False)
+    x_ref[...] = _dots(dw_ref, share_ref)
+    sends = scatter_start(p, x_ref, got_x, sx, rx)
+    own_ref[...] = scatter_finish(p, x_ref, got_x, sx, rx)
+    sends += gather_start(p, own_ref, got_y, sy, ry)
+    gather_finish(p, own_ref, got_y, sy, ry, full)
+    sol_ref[...] = _dots(dw_ref, full, transpose_a=True)
+    _wait_sends(sends)
+
+
+def _back2_kernel(n, count, x_ref, f_ref, dw_ref, sum_ref, sol_ref, got_b, sb, rb, res, full, got_y, sy, ry):
+    p = Place(n, count)
+    p.barrier(True, True)
+    sends = spread_start(p, x_ref, got_b, sb, rb)
+    acc = spread_finish(p, x_ref, got_b, sb, rb)
+    sum_ref[...] = acc
+    res[...] = f_ref[...] - acc[acc.shape[0] - 1]
+    sends += gather_start(p, res, got_y, sy, ry)
+    gather_finish(p, res, got_y, sy, ry, full)
+    sol_ref[...] = _dots(dw_ref, full, transpose_a=True)
+    _wait_sends(sends)
+
+
+def _last_kernel(n, count, res_ref, d0_ref, own_ref, x_ref, got, s, r):
+    p = Place(n, count)
+    p.barrier(True, False)
+    x_ref[...] = _dots(d0_ref, res_ref, transpose_a=True)
+    sends = scatter_start(p, x_ref, got, s, r)
+    own_ref[...] = scatter_finish(p, x_ref, got, s, r)
     _wait_sends(sends)
 
 
@@ -295,40 +365,32 @@
         push_outgoing = outgoing.reshape(height, window_len, owned_count, share_rows, columns)
         return push_outgoing.transpose(1, 0, 2, 3, 4)
 
-    (whole0,) = _call(_gather_kernel, n, count, 0, [rhs[0]], [whole], [pltpu.VMEM((n,) + blk, jnp.float32)] + _dma(n))
-    fv0 = jnp.einsum("sci,sir->scr", diag_inv[0], whole0, precision=highest)
-    win0, d1 = _call(
-        _bcast_gather_kernel, n, count, 1, [fv0, diag_inv[1]], [win, dwhole],
-        [pltpu.VMEM(win, jnp.float32)] + _dma(slots) + [pltpu.VMEM((n,) + dblk, jnp.float32)] + _dma(n),
-    )
-    spread1 = jnp.einsum("sij,sjr->sir", d1, forward_share(1, [win0]), precision=highest)
+    def vm(shape):
+        return pltpu.VMEM(shape, jnp.float32)
+
+    fv0, win0, d1 = _call(
+        _first_kernel, n, count, 0, [rhs[0], diag_inv[0], diag_inv[1]], [blk, win, dwhole],
+        [vm((n,) + blk)] + _dma(n) + [vm(whole)] + [vm(win)] + _dma(slots) + [vm((n,) + dblk)] + _dma(n),
+    )
     fv1, win1, d2 = _call(
-        _scatter_bcast_gather_kernel, n, count, 2, [spread1, diag_inv[2]], [blk, win, dwhole],
-        [pltpu.VMEM((n,) + blk, jnp.float32)] + _dma(n)
-        + [pltpu.VMEM(win, jnp.float32)] + _dma(slots)
-        + [pltpu.VMEM((n,) + dblk, jnp.float32)] + _dma(n),
-    )
-    spread2 = jnp.einsum("sij,sjr->sir", d2, forward_share(2, [win0, win1]), precision=highest)
-    fv2, whole_res2 = _call(
-        _scatter_gather_kernel, n, count, 3, [spread2], [blk, whole],
-        [pltpu.VMEM((n,) + blk, jnp.float32)] + _dma(n) + [pltpu.VMEM((n,) + blk, jnp.float32)] + _dma(n),
-    )
-    sol2 = jnp.einsum("sji,sjr->sir", d2, whole_res2, precision=highest)
+        _level1_kernel, n, count, 1, [forward_share(1, [win0]), d1, diag_inv[2]], [blk, win, dwhole],
+        [vm(whole), vm((n,) + blk)] + _dma(n) + [vm(win)] + _dma(slots) + [vm((n,) + dblk)] + _dma(n),
+    )
+    fv2, sol2 = _call(
+        _level2_kernel, n, count, 2, [forward_share(2, [win0, win1]), d2], [blk, whole],
+        [vm(whole), vm((n,) + blk)] + _dma(n) + [vm(whole), vm((n,) + blk)] + _dma(n),
+    )
     out2 = buckets(2, sol2)
-    got2, whole_res1 = _call(
-        _spread_gather_kernel, n, count, 4, [out2, fv1], [out2.shape[1:], whole],
-        [pltpu.VMEM(out2.shape, jnp.float32)] + _dma(slots)
-        + [pltpu.VMEM(blk, jnp.float32), pltpu.VMEM((n,) + blk, jnp.float32)] + _dma(n),
-    )
-    sol1 = jnp.einsum("sji,sjr->sir", d1, whole_res1, precision=highest)
+    got2, sol1 = _call(
+        _back2_kernel, n, count, 3, [out2, fv1, d1], [out2.shape[1:], whole],
+        [vm(out2.shape)] + _dma(slots) + [vm(blk), vm(whole), vm((n,) + blk)] + _dma(n),
+    )
     out1 = buckets(1, sol1)
-    (got1,) = _call(
-        _spread_kernel, n, count, 5, [out1], [out1.shape[1:]],
-        [pltpu.VMEM(out1.shape, jnp.float32)] + _dma(slots),
-    )
+    (got1,) = _call(_spread_kernel, n, count, 4, [out1], [out1.shape[1:]], [vm(out1.shape)] + _dma(slots))
     res0 = fv0 - (got2[0] + got1[0])
-    partial0 = jnp.einsum("sci,scr->sir", diag_inv[0], res0, precision=highest)
-    (sol0,) = _call(_scatter_kernel, n, count, 6, [partial0], [blk], [pltpu.VMEM((n,) + blk, jnp.float32)] + _dma(n))
+    (sol0,) = _call(
+        _last_kernel, n, count, 5, [res0, diag_inv[0]], [blk], [vm(whole), vm((n,) + blk)] + _dma(n)
+    )
     return jnp.stack([sol0, own_rows(sol1), own_rows(sol2)], 0)
 
 

time: 183 us -> 174 us (0.951)
  matrix products: 14.4 us -> 6.42 us
  other arithmetic: 2.2 us -> 4.08 us
    dot_general x6 -> x0, matrix products: 10.6 us -> none  [the longest x1 2.16 us: local(): partial0 = jnp.einsum('sci,scr->sir', diag_inv[0], res0, precision=highest)]
    dot_general x2, matrix products: 1.2 us -> 3.11 us  [buckets(): jnp.einsum('skci,sir->skcr', factor_tiles[height - 1], whole_block, preci...]
    pallas_call x7 -> x6, Pallas kernels: 152 us -> 151 us  [_call(): pl.pallas_call(functools.partial(body, n, count), out_shape=tuple((_f32(o...]
where the time goes in v4:
time: 174 us; the launch traced here: 173 us
  Pallas kernels  151 us (87%)
  local copies, waits for them, and re-layouts  11.2 us (6%)
  matrix products  6.42 us (4%)
  other arithmetic  4.08 us (2%)
    pallas_call x6, Pallas kernels, _call(): pl.pallas_call(functools.partial(body, n, count), out_shape=tuple((_f32(o...  151 us

profile of v4, /device:TPU:1, one launch (start us, length us, event | category | flops | bytes accessed | tf_op | source)
XLA Modules:
  0.0 173.0 jit_solution(1998833918497140849)
XLA Ops:
  0.0 1.7 slice_bitcast_fusion
  2.3 36.8 %shard_map.55 = (f32[2,32,128]{2,1,0:T(8,128)}, f32[15,2,32,128]{3,2,1,0:T(8,128)}, f32[2,256,256]{2,1,0:T(8,128)}) custom-call(f32[2,32,128]{2,1,0:T(8,128)} %slice_bitcast_fusion.3.y_ref, f32[2,32,256]{2,1,0:T(8,128)} %get-tuple-element.24.d0_ref, f32[2,32,256]{2,1,0:T(8,128)} %get-tuple-element.25.d1_ref), custom_call_target="tpu_custom_call" | custom-call | tf_op jit(solution)/shard_map/pallas_call | solution.py:292
  39.2 0.7 compare_select_fusion
  40.0 1.6 gather_fusion
  41.6 0.7 copy-done.9
  43.0 1.1 convolution_bitcast_fusion.1
  44.1 0.7 copy-done.3
  44.8 29.7 %shard_map.56 = (f32[2,32,128]{2,1,0:T(8,128)}, f32[15,2,32,128]{3,2,1,0:T(8,128)}, f32[2,256,256]{2,1,0:T(8,128)}) custom-call(f32[2,256,128]{2,1,0:T(8,128)} %copy-done.3, f32[2,256,256]{2,1,0:T(8,128)} %get-tuple-element.16.dw_ref, f32[2,32,256]{2,1,0:T(8,128)} %get-tuple-element.23.d_ref), custom_call_target="tpu_custom_call" | custom-call | tf_op jit(solution)/shard_map/pallas_call | solution.py:292
  74.6 1.1 pad_maximum_fusion
  76.3 1.1 convolution_bitcast_fusion
  77.5 0.7 copy-done.2
  78.2 20.5 %shard_map.57 = (f32[2,32,128]{2,1,0:T(8,128)}, f32[2,256,128]{2,1,0:T(8,128)}) custom-call(f32[2,256,128]{2,1,0:T(8,128)} %copy-done.2, f32[2,256,256]{2,1,0:T(8,128)} %get-tuple-element.18.dw_ref), custom_call_target="tpu_custom_call" | custom-call | tf_op jit(solution)/shard_map/pallas_call | solution.py:292
  98.7 1.6 convolution_multiply_fusion.1
  100.5 0.6 fusion.12
  101.1 1.2 copy.35
  102.4 35.5 %shard_map.58 = (f32[2,2,32,128]{3,2,1,0:T(8,128)}, f32[2,256,128]{2,1,0:T(8,128)}) custom-call(f32[15,2,2,32,128]{4,3,2,1,0:T(8,128)} %bitcast.164, f32[2,32,128]{2,1,0:T(8,128)} %get-tuple-element.20.f_ref, f32[2,256,256]{2,1,0:T(8,128)} %get-tuple-element.16.dw_ref), custom_call_target="tpu_custom_call" | custom-call | tf_op jit(solution)/shard_map/pallas_call | solution.py:292
  137.9 1.6 convolution_multiply_fusion
  140.0 1.0 copy.36
  140.9 13.4 %shard_map.59 = f32[1,2,32,128]{3,2,1,0:T(8,128)} custom-call(f32[15,1,2,32,128]{4,3,2,1,0:T(8,128)} %bitcast.165), custom_call_target="tpu_custom_call" | custom-call | tf_op jit(solution)/shard_map/pallas_call | solution.py:292
  154.4 1.4 bitcast_subtract_fusion.res_ref
  155.7 15.0 %shard_map.60 = f32[2,32,128]{2,1,0:T(8,128)} custom-call(f32[2,32,128]{2,1,0:T(8,128)} %bitcast_subtract_fusion.res_ref, f32[2,32,256]{2,1,0:T(8,128)} %get-tuple-element.24.d0_ref), custom_call_target="tpu_custom_call" | custom-call | tf_op jit(solution)/shard_map/pallas_call | solution.py:292
  170.8 0.8 dynamic-slice_bitcast_fusion.1
  171.5 0.8 dynamic-slice_bitcast_fusion
  172.3 0.6 pad_maximum_fusion.1
  (37 shorter events, 2.9 us)
Async XLA Ops:
  0.0 1.7 copy-start.5
  0.0 43.0 %copy-start = (f32[2,2,8,32,256]{4,3,2,1,0:T(8,128)S(1)}, f32[2,2,8,32,256]{4,3,2,1,0:T(8,128)}, u32[]{:S(2)}) copy-start(f32[2,2,8,32,256]{4,3,2,1,0:T(8,128)} %param.7) | copy-start | bytes 3145732
  41.6 0.7 copy-start.9
  42.3 0.7 copy-start.7
  44.1 30.4 %copy-start.1 = (f32[15,2,32,128]{3,2,1,0:T(8,128)S(1)}, f32[15,2,32,128]{3,2,1,0:T(8,128)}, u32[]{:S(2)}) copy-start(f32[15,2,32,128]{3,2,1,0:T(8,128)} %get-tuple-element.15) | copy-start | bytes 1474564
  44.1 0.7 copy-start.3
  77.5 0.7 copy-start.2
  140.9 13.4 %copy-start.6 = (f32[2,32,128]{2,1,0:T(8,128)S(1)}, f32[2,32,128]{2,1,0:T(8,128)}, u32[]{:S(2)}) copy-start(f32[2,32,128]{2,1,0:T(8,128)} %get-tuple-element.14) | copy-start | bytes 98308
  140.9 13.4 %copy-start.8 = (f32[2,2,32,128]{3,2,1,0:T(8,128)S(1)}, f32[2,2,32,128]{3,2,1,0:T(8,128)}, u32[]{:S(2)}) copy-start(f32[2,2,32,128]{3,2,1,0:T(8,128)} %get-tuple-element.21) | copy-start | bytes 196612
  171.5 0.8 copy-start.4

commit v5 on v4

--- a/solution.py
+++ b/solution.py
@@ -277,6 +277,23 @@
     x_ref[...] = _dots(d0_ref, res_ref, transpose_a=True)
     sends = scatter_start(p, x_ref, got, s, r)
     own_ref[...] = scatter_finish(p, x_ref, got, s, r)
+    _wait_sends(sends)
+
+
+def _final_kernel(n, count, x_ref, f_ref, d0_ref, own_ref, got_b, sb, rb, x2_ref, got, s, r):
+    p = Place(n, count)
+    p.barrier(True, True)
+    sends = spread_start(p, x_ref, got_b, sb, rb)
+    acc = spread_finish(p, x_ref, got_b, sb, rb)
+    res = f_ref[...] - acc[0]
+    outs = []
+    for q in range(d0_ref.shape[0]):
+        outs.append(
+            jnp.dot(d0_ref[q].T, res[q], precision=lax.Precision.HIGHEST, preferred_element_type=jnp.float32)
+        )
+    x2_ref[...] = jnp.stack(outs, 0)
+    sends += scatter_start(p, x2_ref, got, s, r)
+    own_ref[...] = scatter_finish(p, x2_ref, got, s, r)
     _wait_sends(sends)
 
 
@@ -382,14 +399,13 @@
     )
     out2 = buckets(2, sol2)
     got2, sol1 = _call(
-        _back2_kernel, n, count, 3, [out2, fv1, d1], [out2.shape[1:], whole],
-        [vm(out2.shape)] + _dma(slots) + [vm(blk), vm(whole), vm((n,) + blk)] + _dma(n),
-    )
-    out1 = buckets(1, sol1)
-    (got1,) = _call(_spread_kernel, n, count, 4, [out1], [out1.shape[1:]], [vm(out1.shape)] + _dma(slots))
-    res0 = fv0 - (got2[0] + got1[0])
+        _back2_kernel, n, count, 3, [out2[:, 1:], fv1, d1], [out2[:, 1:].shape[1:], whole],
+        [vm(out2[:, 1:].shape)] + _dma(slots) + [vm(blk), vm(whole), vm((n,) + blk)] + _dma(n),
+    )
+    out1 = buckets(1, sol1) + out2[:, :1]
     (sol0,) = _call(
-        _last_kernel, n, count, 5, [res0, diag_inv[0]], [blk], [vm(whole), vm((n,) + blk)] + _dma(n)
+        _final_kernel, n, count, 4, [out1, fv0, diag_inv[0]], [blk],
+        [vm(out1.shape)] + _dma(slots) + [vm(whole), vm((n,) + blk)] + _dma(n),
     )
     return jnp.stack([sol0, own_rows(sol1), own_rows(sol2)], 0)
 

time: 174 us -> 163 us (0.937)
  Pallas kernels: 151 us -> 141 us
    pallas_call x6 -> x5, Pallas kernels: 151 us -> 141 us  [_call(): pl.pallas_call(functools.partial(body, n, count), out_shape=tuple((_f32(o...]
    dot_general x2 -> x1, local copies, waits for them, and re-layouts: 2.19 us -> 0.32 us  [buckets(): jnp.einsum('ms,slg->mlg', one_hot, term_set.reshape(owned_count * slot_co...]
where the time goes in v5:
time: 163 us; the launch traced here: 162 us
  Pallas kernels  141 us (87%)
  local copies, waits for them, and re-layouts  10.2 us (6%)
  matrix products  6.42 us (4%)
  other arithmetic  3.72 us (2%)
    pallas_call x5, Pallas kernels, _call(): pl.pallas_call(functools.partial(body, n, count), out_shape=tuple((_f32(o...  141 us

profile of v5, /device:TPU:1, one launch (start us, length us, event | category | flops | bytes accessed | tf_op | source)
XLA Modules:
  0.0 161.8 jit_solution(6568463249031503663)
XLA Ops:
  0.0 1.7 %slice_bitcast_fusion = (f32[2,32,256]{2,1,0:T(8,128)}, f32[2,32,256]{2,1,0:T(8,128)}, f32[2,32,256]{2,1,0:T(8,128)}) fusion(f32[3,2,32,256]{3,2,1,0:T(8,128)} %param.6), kind=kLoop, calls=%fused_computation.37 | loop fusion | bytes 393216 | tf_op jit(solution)/shard_map/squeeze | solution.py:393
  1.7 0.6 slice_bitcast_fusion.3.y_ref
  2.3 36.9 %shard_map.55 = (f32[2,32,128]{2,1,0:T(8,128)}, f32[15,2,32,128]{3,2,1,0:T(8,128)}, f32[2,256,256]{2,1,0:T(8,128)}) custom-call(f32[2,32,128]{2,1,0:T(8,128)} %slice_bitcast_fusion.3.y_ref, f32[2,32,256]{2,1,0:T(8,128)} %get-tuple-element.22.d0_ref, f32[2,32,256]{2,1,0:T(8,128)} %get-tuple-element.23.d1_ref), custom_call_target="tpu_custom_call" | custom-call | tf_op jit(solution)/shard_map/pallas_call | solution.py:309
  39.2 0.7 compare_select_fusion
  40.0 1.6 gather_fusion
  41.6 0.7 copy-done.7
  42.3 0.6 copy-done.6
  43.0 1.1 convolution_bitcast_fusion.1
  44.2 0.7 copy-done.3
  44.9 29.7 %shard_map.56 = (f32[2,32,128]{2,1,0:T(8,128)}, f32[15,2,32,128]{3,2,1,0:T(8,128)}, f32[2,256,256]{2,1,0:T(8,128)}) custom-call(f32[2,256,128]{2,1,0:T(8,128)} %copy-done.3, f32[2,256,256]{2,1,0:T(8,128)} %get-tuple-element.14.dw_ref, f32[2,32,256]{2,1,0:T(8,128)} %get-tuple-element.21.d_ref), custom_call_target="tpu_custom_call" | custom-call | tf_op jit(solution)/shard_map/pallas_call | solution.py:309
  74.6 1.1 pad_maximum_fusion
  76.3 1.1 convolution_bitcast_fusion
  77.5 0.7 copy-done.2
  78.2 20.1 %shard_map.57 = (f32[2,32,128]{2,1,0:T(8,128)}, f32[2,256,128]{2,1,0:T(8,128)}) custom-call(f32[2,256,128]{2,1,0:T(8,128)} %copy-done.2, f32[2,256,256]{2,1,0:T(8,128)} %get-tuple-element.16.dw_ref), custom_call_target="tpu_custom_call" | custom-call | tf_op jit(solution)/shard_map/pallas_call | solution.py:309
  98.3 1.6 convolution_multiply_fusion.1
  100.1 0.6 fusion.12
  101.1 0.8 slice.67.x_ref
  101.9 30.0 %shard_map.58 = (f32[1,2,32,128]{3,2,1,0:T(8,128)}, f32[2,256,128]{2,1,0:T(8,128)}) custom-call(f32[15,1,2,32,128]{4,3,2,1,0:T(8,128)} %slice.67.x_ref, f32[2,32,128]{2,1,0:T(8,128)} %get-tuple-element.18.f_ref, f32[2,256,256]{2,1,0:T(8,128)} %get-tuple-element.14.dw_ref), custom_call_target="tpu_custom_call" | custom-call | tf_op jit(solution)/shard_map/pallas_call | solution.py:309
  131.9 1.5 convolution_multiply_fusion
  134.0 1.0 slice_add_fusion.x_ref
  135.0 24.6 %shard_map.59 = f32[2,32,128]{2,1,0:T(8,128)} custom-call(f32[15,1,2,32,128]{4,3,2,1,0:T(8,128)} %slice_add_fusion.x_ref, f32[2,32,128]{2,1,0:T(8,128)} %get-tuple-element.20.f_ref, f32[2,32,256]{2,1,0:T(8,128)} %get-tuple-element.22.d0_ref), custom_call_target="tpu_custom_call" | custom-call | tf_op jit(solution)/shard_map/pallas_call | solution.py:309
  159.6 0.8 dynamic-slice_bitcast_fusion.1
  160.4 0.8 dynamic-slice_bitcast_fusion
  161.2 0.6 pad_maximum_fusion.1
  (32 shorter events, 2.0 us)
Async XLA Ops:
  0.0 1.7 %copy-start.5 = (f32[3,2,32,128]{3,2,1,0:T(8,128)S(1)}, f32[3,2,32,128]{3,2,1,0:T(8,128)}, u32[]{:S(2)}) copy-start(f32[3,2,32,128]{3,2,1,0:T(8,128)} %param.5) | copy-start | bytes 294916
  0.0 43.0 %copy-start = (f32[2,2,8,32,256]{4,3,2,1,0:T(8,128)S(1)}, f32[2,2,8,32,256]{4,3,2,1,0:T(8,128)}, u32[]{:S(2)}) copy-start(f32[2,2,8,32,256]{4,3,2,1,0:T(8,128)} %param.7) | copy-start | bytes 3145732
  41.6 0.7 copy-start.7
  42.3 0.7 copy-start.6
  44.1 30.4 %copy-start.1 = (f32[15,2,32,128]{3,2,1,0:T(8,128)S(1)}, f32[15,2,32,128]{3,2,1,0:T(8,128)}, u32[]{:S(2)}) copy-start(f32[15,2,32,128]{3,2,1,0:T(8,128)} %get-tuple-element.13) | copy-start | bytes 1474564
  44.2 0.7 copy-start.3
  77.5 0.7 copy-start.2
  160.4 0.8 copy-start.4

commit v6 on v5

--- a/solution.py
+++ b/solution.py
@@ -294,6 +294,65 @@
     x2_ref[...] = jnp.stack(outs, 0)
     sends += scatter_start(p, x2_ref, got, s, r)
     own_ref[...] = scatter_finish(p, x2_ref, got, s, r)
+    _wait_sends(sends)
+
+
+def _mm(a, b):
+    return jnp.dot(a, b, precision=lax.Precision.HIGHEST, preferred_element_type=jnp.float32)
+
+
+def _fill_buckets(bucket_ref, rows, level):
+    slots, owned, share, r = bucket_ref.shape
+    span = owned * share
+    for w in range(slots):
+        start = (level * slots + w) * span
+        for q in range(owned):
+            bucket_ref[w, q] = rows[start + q * share : start + (q + 1) * share]
+
+
+def _products(t_ref, sol_ref, w_ref):
+    owned, span, unused = t_ref.shape
+    total = None
+    for q in range(owned):
+        terms = _mm(t_ref[q], sol_ref[q])
+        part = _mm(w_ref[:, q * span : (q + 1) * span], terms)
+        total = part if total is None else total + part
+    return total
+
+
+def _tail_kernel(
+    n, count,
+    share_ref, d2_ref, d1_ref, d0_ref, f1_ref, f0_ref, t2_ref, t1_ref, w2_ref, w1_ref,
+    s0_ref, s1_ref, s2_ref,
+    x2, got_x2, sx2, rx2, res2, got_y2, sy2, ry2, full2, sol2,
+    bucket1, got_b1, sb1, rb1, res1, got_y1, sy1, ry1, full1, sol1,
+    bucket0, got_b0, sb0, rb0, x0, got_x0, sx0, rx0,
+):
+    p = Place(n, count)
+    p.barrier(True, True)
+    share = s0_ref.shape[1]
+    x2[...] = _dots(d2_ref, share_ref)
+    sends = scatter_start(p, x2, got_x2, sx2, rx2)
+    res2[...] = scatter_finish(p, x2, got_x2, sx2, rx2)
+    sends += gather_start(p, res2, got_y2, sy2, ry2)
+    gather_finish(p, res2, got_y2, sy2, ry2, full2)
+    sol2[...] = _dots(d2_ref, full2, transpose_a=True)
+    s2_ref[...] = _rows_of(sol2, p.col, share)[...]
+    routed2 = _products(t2_ref, sol2, w2_ref)
+    _fill_buckets(bucket1, routed2, 1)
+    sends += spread_start(p, bucket1, got_b1, sb1, rb1)
+    res1[...] = f1_ref[...] - spread_finish(p, bucket1, got_b1, sb1, rb1)
+    sends += gather_start(p, res1, got_y1, sy1, ry1)
+    gather_finish(p, res1, got_y1, sy1, ry1, full1)
+    sol1[...] = _dots(d1_ref, full1, transpose_a=True)
+    s1_ref[...] = _rows_of(sol1, p.col, share)[...]
+    routed1 = _products(t1_ref, sol1, w1_ref)
+    _fill_buckets(bucket0, routed1 + routed2[: routed1.shape[0]], 0)
+    sends += spread_start(p, bucket0, got_b0, sb0, rb0)
+    res0 = f0_ref[...] - spread_finish(p, bucket0, got_b0, sb0, rb0)
+    x0[...] = jnp.stack([_mm(d0_ref[q].T, res0[q]) for q in range(res0.shape[0])], 0)
+    sends += scatter_start(p, x0, got_x0, sx0, rx0)
+    s0_ref[...] = scatter_finish(p, x0, got_x0, sx0, rx0)
     _wait_sends(sends)
 
 
@@ -393,21 +452,32 @@
         _level1_kernel, n, count, 1, [forward_share(1, [win0]), d1, diag_inv[2]], [blk, win, dwhole],
         [vm(whole), vm((n,) + blk)] + _dma(n) + [vm(win)] + _dma(slots) + [vm((n,) + dblk)] + _dma(n),
     )
-    fv2, sol2 = _call(
-        _level2_kernel, n, count, 2, [forward_share(2, [win0, win1]), d2], [blk, whole],
-        [vm(whole), vm((n,) + blk)] + _dma(n) + [vm(whole), vm((n,) + blk)] + _dma(n),
-    )
-    out2 = buckets(2, sol2)
-    got2, sol1 = _call(
-        _back2_kernel, n, count, 3, [out2[:, 1:], fv1, d1], [out2[:, 1:].shape[1:], whole],
-        [vm(out2[:, 1:].shape)] + _dma(slots) + [vm(blk), vm(whole), vm((n,) + blk)] + _dma(n),
-    )
-    out1 = buckets(1, sol1) + out2[:, :1]
-    (sol0,) = _call(
-        _final_kernel, n, count, 4, [out1, fv0, diag_inv[0]], [blk],
-        [vm(out1.shape)] + _dma(slots) + [vm(whole), vm((n,) + blk)] + _dma(n),
-    )
-    return jnp.stack([sol0, own_rows(sol1), own_rows(sol2)], 0)
+    def selection(height):
+        places = window_places(tile_source[height - 1]).reshape(-1)
+        live = live_mask(tile_count[height - 1]).reshape(-1)
+        targets = height * window_len * owned_count
+        pick = (jnp.arange(targets, dtype=jnp.int32)[:, None] == places[None, :]).astype(jnp.float32)
+        pick = pick * live[None, :]
+        eye = jnp.eye(share_rows, dtype=jnp.float32)
+        return (pick[:, None, :, None] * eye[None, :, None, :]).reshape(
+            targets * share_rows, places.shape[0] * share_rows
+        )
+
+    def flat_tiles(height):
+        t = factor_tiles[height - 1]
+        return t.reshape(t.shape[0], t.shape[1] * t.shape[2], t.shape[3])
+
+    nblk = (n,) + blk
+    sol0, sol1, sol2 = _call(
+        _tail_kernel, n, count, 2,
+        [forward_share(2, [win0, win1]), d2, d1, diag_inv[0], fv1, fv0, flat_tiles(2), flat_tiles(1),
+         selection(2), selection(1)],
+        [blk, blk, blk],
+        [vm(whole), vm(nblk)] + _dma(n) + [vm(blk), vm(nblk)] + _dma(n) + [vm(whole), vm(whole)]
+        + [vm(win), vm(win)] + _dma(slots) + [vm(blk), vm(nblk)] + _dma(n) + [vm(whole), vm(whole)]
+        + [vm(win), vm(win)] + _dma(slots) + [vm(whole), vm(nblk)] + _dma(n),
+    )
+    return jnp.stack([sol0, sol1, sol2], 0)
 
 
 def solution(mesh):

time: 163 us -> 191 us (1.17)
  local copies, waits for them, and re-layouts: 10.2 us -> 27.2 us
  other arithmetic: 3.72 us -> 17.3 us
  matrix products: 6.42 us -> 4.29 us
    mul x0 -> x2, local copies, waits for them, and re-layouts: none -> 19.1 us  [selection(): pick[:, None, :, None] * eye[None, :, None, :]]
    mul x0 -> x4, other arithmetic: none -> 11.4 us  [the longest x2 11.4 us: selection(): pick[:, None, :, None] * eye[None, :, None, :]]
    dot_general x4 -> x0, matrix products: 4.21 us -> none  [the longest x2 3.1 us: buckets(): jnp.einsum('skci,sir->skcr', factor_tiles[height - 1], whole_block, preci...]
    dot_general x2, matrix products: 2.21 us -> 4.29 us  [forward_share(): jnp.einsum('skci,skcr->sir', factor_tiles[height - 1], picked, precision=...]
    unnamed x16 -> x8, local copies, waits for them, and re-layouts: 2.69 us -> 0.72 us
    pallas_call x5 -> x3, Pallas kernels: 141 us -> 140 us  [_call(): pl.pallas_call(functools.partial(body, n, count), out_shape=tuple((_f32(o...]
where the time goes in v6:
time: 191 us; the launch traced here: 189 us
  Pallas kernels  140 us (73%)
  local copies, waits for them, and re-layouts  27.2 us (14%)
  other arithmetic  17.3 us (9%)
  matrix products  4.29 us (2%)
    pallas_call x3, Pallas kernels, _call(): pl.pallas_call(functools.partial(body, n, count), out_shape=tuple((_f32(o...  140 us
    mul x2, local copies, waits for them, and re-layouts, selection(): pick[:, None, :, None] * eye[None, :, None, :]  19.1 us
    mul x2, other arithmetic, selection(): pick[:, None, :, None] * eye[None, :, None, :]  11.4 us
    dot_general x2, matrix products, forward_share(): jnp.einsum('skci,skcr->sir', factor_tiles[height - 1], picked, precision=...  4.29 us

profile of v6, /device:TPU:1, one launch (start us, length us, event | category | flops | bytes accessed | tf_op | source)
XLA Modules:
  0.0 189.1 jit_solution(1962007774032937425)
XLA Ops:
  0.0 1.6 slice_bitcast_fusion
  1.6 1.4 slice_bitcast_fusion.3.y_ref
  3.0 36.8 %shard_map.55 = (f32[2,32,128]{2,1,0:T(8,128)}, f32[15,2,32,128]{3,2,1,0:T(8,128)}, f32[2,256,256]{2,1,0:T(8,128)}) custom-call(f32[2,32,128]{2,1,0:T(8,128)} %slice_bitcast_fusion.3.y_ref, f32[2,32,256]{2,1,0:T(8,128)} %get-tuple-element.26.d0_ref, f32[2,32,256]{2,1,0:T(8,128)} %get-tuple-element.27.d1_ref), custom_call_target="tpu_custom_call" | custom-call | tf_op jit(solution)/shard_map/pallas_call | solution.py:368
  39.8 0.7 compare_select_fusion
  40.5 0.1 reshape.712
  40.6 1.6 gather_fusion
  42.2 0.8 slice_bitcast_fusion.4
  43.1 0.7 compare_and_fusion.1
  43.8 2.1 %convolution_bitcast_fusion.1 = f32[2,128,256]{1,2,0:T(8,128)S(1)} fusion(f32[2,8,32,128]{3,2,1,0:T(8,128)S(1)} %bitcast.130, f32[2,8]{1,0:T(2,128)S(1)} %get-tuple-element.39, pred[2,8]{1,0:T(4,128)(4,1)S(1)} %get-tuple-element.31, f32[2,2,8,32,256]{4,3,2,1,0:T(8,128)} %param.7), kind=kOutput, calls=%fused_computation.5 | convolution fusion | flops 201457664 | bytes 1048656 | tf_op jit(solution)/shard_map/skci,skcr->sir/dot_general | solution.py:418
  46.0 0.8 fusion.13.share_ref
  46.7 0.7 copy-done.2
  47.4 29.7 %shard_map.56 = (f32[2,32,128]{2,1,0:T(8,128)}, f32[15,2,32,128]{3,2,1,0:T(8,128)}, f32[2,256,256]{2,1,0:T(8,128)}) custom-call(f32[2,256,128]{2,1,0:T(8,128)} %copy-done.2, f32[2,256,256]{2,1,0:T(8,128)} %get-tuple-element.15.dw_ref.d1_ref, f32[2,32,256]{2,1,0:T(8,128)} %get-tuple-element.25.d_ref), custom_call_target="tpu_custom_call" | custom-call | tf_op jit(solution)/shard_map/pallas_call | solution.py:368
  77.2 1.2 pad_maximum_fusion
  78.4 0.1 reshape.720
  78.5 0.6 gather_fusion.1
  79.1 2.1 %convolution_bitcast_fusion = f32[2,128,256]{1,2,0:T(8,128)S(1)} fusion(f32[2,8,32,128]{3,2,1,0:T(8,128)S(1)} %bitcast.131, f32[2,8]{1,0:T(2,128)S(1)} %get-tuple-element.38, pred[2,8]{1,0:T(4,128)(4,1)S(1)} %get-tuple-element.30, f32[2,2,8,32,256]{4,3,2,1,0:T(8,128)} %param.7), kind=kOutput, calls=%fused_computation.4 | convolution fusion | flops 201457664 | bytes 1048656 | tf_op jit(solution)/shard_map/skci,skcr->sir/dot_general | solution.py:418
  81.3 0.8 fusion.12.share_ref
  82.4 7.4 %broadcast_multiply_fusion = f32[60,32,16,32]{3,2,1,0:T(8,128)} fusion(f32[32,32]{1,0:T(8,128)S(1)} %fusion.15, f32[60,16]{1,0:T(8,128)S(1)} %fusion.14), kind=kLoop, calls=%fused_computation.2 | loop fusion | flops 983040 | bytes 3940096 | tf_op jit(solution)/shard_map/mul | solution.py:462
  89.8 12.2 %mul.173.w2_ref = f32[1920,512]{1,0:T(8,128)} reshape(f32[60,32,16,32]{3,2,1,0:T(8,128)} %broadcast_multiply_fusion) | data formatting | bytes 7864320 | tf_op jit(solution)/shard_map/mul | solution.py:462
  102.1 4.0 %broadcast_multiply_fusion.1 = f32[30,32,16,32]{3,2,1,0:T(8,128)} fusion(f32[32,32]{1,0:T(8,128)S(1)} %fusion.15, f32[30,16]{1,0:T(8,128)S(1)} %fusion.16), kind=kLoop, calls=%fused_computation.3 | loop fusion | flops 491520 | bytes 1972096 | tf_op jit(solution)/shard_map/mul | solution.py:462
  106.1 6.9 %mul.181.w1_ref = f32[960,512]{1,0:T(8,128)} reshape(f32[30,32,16,32]{3,2,1,0:T(8,128)} %broadcast_multiply_fusion.1) | data formatting | bytes 3932160 | tf_op jit(solution)/shard_map/mul | solution.py:462
  113.0 1.1 fusion.31
  114.0 73.6 %shard_map.57 = (f32[2,32,128]{2,1,0:T(8,128)}, f32[2,32,128]{2,1,0:T(8,128)}, f32[2,32,128]{2,1,0:T(8,128)}) custom-call(f32[2,256,128]{2,1,0:T(8,128)} %copy-done.1, f32[2,256,256]{2,1,0:T(8,128)} %get-tuple-element.17.d2_ref, f32[2,256,256]{2,1,0:T(8,128)} %get-tuple-element.15.dw_ref.d1_ref, f32[2,32,256]{2,1,0:T(8,128)} %get-tuple-element.26.d0_ref, ...), custom_call_target="tpu_custom_call" | custom-call | tf_op jit(solution)/shard_map/pallas_call | solution.py:368
  187.7 1.4 pad_maximum_fusion.1
  (21 shorter events, 0.5 us)
Async XLA Ops:
  0.0 82.1 %copy-start.3 = (s32[2,2,8]{2,1,0:T(2,128)S(1)}, s32[2,2,8]{2,1,0:T(2,128)}, u32[]{:S(2)}) copy-start(s32[2,2,8]{2,1,0:T(2,128)} %param.8) | copy-start | bytes 388
  46.7 0.7 copy-start.2
  82.1 7.7 %copy-start.1 = (f32[2,256,128]{2,1,0:T(8,128)}, f32[2,256,128]{2,1,0:T(8,128)S(1)}, u32[]{:S(2)}) copy-start(f32[2,256,128]{2,1,0:T(8,128)S(1)} %fusion.12.share_ref) | copy-start | bytes 786436
  102.1 10.9 %copy-start = (f32[2,2,8,32,256]{4,3,2,1,0:T(8,128)S(1)}, f32[2,2,8,32,256]{4,3,2,1,0:T(8,128)}, u32[]{:S(2)}) copy-start(f32[2,2,8,32,256]{4,3,2,1,0:T(8,128)} %param.7) | copy-start | bytes 3145732

commit v7 on v5

--- a/solution.py
+++ b/solution.py
@@ -220,7 +220,8 @@
     return jnp.stack(outs, 0)
 
 
-def _first_kernel(n, count, y_ref, d0_ref, d1_ref, fv_ref, win_ref, dfull_ref, got_y, sy, ry, whole, got_w, sw, rw, got_d, sd, rd):
+def _first_kernel(n, count, rhs_ref, dinv_ref, fv_ref, win_ref, dfull_ref, got_y, sy, ry, whole, got_w, sw, rw, got_d, sd, rd):
+    y_ref, d0_ref, d1_ref = rhs_ref.at[0], dinv_ref.at[0], dinv_ref.at[1]
     p = Place(n, count)
     p.barrier(True, True)
     sends = gather_start(p, y_ref, got_y, sy, ry)
@@ -233,8 +234,9 @@
 
 
 def _level1_kernel(
-    n, count, share_ref, dw_ref, d_ref, own_ref, win_ref, dfull_ref, x_ref, got_x, sx, rx, got_w, sw, rw, got_d, sd, rd
+    n, count, share_ref, dw_ref, dinv_ref, own_ref, win_ref, dfull_ref, x_ref, got_x, sx, rx, got_w, sw, rw, got_d, sd, rd
 ):
+    d_ref = dinv_ref.at[2]
     p = Place(n, count)
     p.barrier(True, True)
     x_ref[...] = _dots(dw_ref, share_ref)
@@ -246,7 +248,7 @@
     _wait_sends(sends)
 
 
-def _level2_kernel(n, count, share_ref, dw_ref, own_ref, sol_ref, x_ref, got_x, sx, rx, full, got_y, sy, ry):
+def _level2_kernel(n, count, share_ref, dw_ref, own_ref, sol_ref, mine_ref, x_ref, got_x, sx, rx, full, got_y, sy, ry):
     p = Place(n, count)
     p.barrier(True, False)
     x_ref[...] = _dots(dw_ref, share_ref)
@@ -255,10 +257,11 @@
     sends += gather_start(p, own_ref, got_y, sy, ry)
     gather_finish(p, own_ref, got_y, sy, ry, full)
     sol_ref[...] = _dots(dw_ref, full, transpose_a=True)
-    _wait_sends(sends)
-
-
-def _back2_kernel(n, count, x_ref, f_ref, dw_ref, sum_ref, sol_ref, got_b, sb, rb, res, full, got_y, sy, ry):
+    mine_ref[...] = _rows_of(sol_ref, p.col, mine_ref.shape[1])[...]
+    _wait_sends(sends)
+
+
+def _back2_kernel(n, count, x_ref, f_ref, dw_ref, sum_ref, sol_ref, mine_ref, got_b, sb, rb, res, full, got_y, sy, ry):
     p = Place(n, count)
     p.barrier(True, True)
     sends = spread_start(p, x_ref, got_b, sb, rb)
@@ -268,6 +271,7 @@
     sends += gather_start(p, res, got_y, sy, ry)
     gather_finish(p, res, got_y, sy, ry, full)
     sol_ref[...] = _dots(dw_ref, full, transpose_a=True)
+    mine_ref[...] = _rows_of(sol_ref, p.col, mine_ref.shape[1])[...]
     _wait_sends(sends)
 
 
@@ -280,7 +284,8 @@
     _wait_sends(sends)
 
 
-def _final_kernel(n, count, x_ref, f_ref, d0_ref, own_ref, got_b, sb, rb, x2_ref, got, s, r):
+def _final_kernel(n, count, x_ref, f_ref, dinv_ref, own_ref, got_b, sb, rb, x2_ref, got, s, r):
+    d0_ref = dinv_ref.at[0]
     p = Place(n, count)
     p.barrier(True, True)
     sends = spread_start(p, x_ref, got_b, sb, rb)
@@ -386,28 +391,28 @@
         return pltpu.VMEM(shape, jnp.float32)
 
     fv0, win0, d1 = _call(
-        _first_kernel, n, count, 0, [rhs[0], diag_inv[0], diag_inv[1]], [blk, win, dwhole],
+        _first_kernel, n, count, 0, [rhs, diag_inv], [blk, win, dwhole],
         [vm((n,) + blk)] + _dma(n) + [vm(whole)] + [vm(win)] + _dma(slots) + [vm((n,) + dblk)] + _dma(n),
     )
     fv1, win1, d2 = _call(
-        _level1_kernel, n, count, 1, [forward_share(1, [win0]), d1, diag_inv[2]], [blk, win, dwhole],
+        _level1_kernel, n, count, 1, [forward_share(1, [win0]), d1, diag_inv], [blk, win, dwhole],
         [vm(whole), vm((n,) + blk)] + _dma(n) + [vm(win)] + _dma(slots) + [vm((n,) + dblk)] + _dma(n),
     )
-    fv2, sol2 = _call(
-        _level2_kernel, n, count, 2, [forward_share(2, [win0, win1]), d2], [blk, whole],
+    fv2, sol2, mine2 = _call(
+        _level2_kernel, n, count, 2, [forward_share(2, [win0, win1]), d2], [blk, whole, blk],
         [vm(whole), vm((n,) + blk)] + _dma(n) + [vm(whole), vm((n,) + blk)] + _dma(n),
     )
     out2 = buckets(2, sol2)
-    got2, sol1 = _call(
-        _back2_kernel, n, count, 3, [out2[:, 1:], fv1, d1], [out2[:, 1:].shape[1:], whole],
+    got2, sol1, mine1 = _call(
+        _back2_kernel, n, count, 3, [out2[:, 1:], fv1, d1], [out2[:, 1:].shape[1:], whole, blk],
         [vm(out2[:, 1:].shape)] + _dma(slots) + [vm(blk), vm(whole), vm((n,) + blk)] + _dma(n),
     )
     out1 = buckets(1, sol1) + out2[:, :1]
     (sol0,) = _call(
-        _final_kernel, n, count, 4, [out1, fv0, diag_inv[0]], [blk],
+        _final_kernel, n, count, 4, [out1, fv0, diag_inv], [blk],
         [vm(out1.shape)] + _dma(slots) + [vm(whole), vm((n,) + blk)] + _dma(n),
     )
-    return jnp.stack([sol0, own_rows(sol1), own_rows(sol2)], 0)
+    return jnp.stack([sol0, mine1, mine2], 0)
 
 
 def solution(mesh):

time: 163 us -> 161 us (0.988)
  local copies, waits for them, and re-layouts: 10.2 us -> 7.28 us
    squeeze x2 -> x0, local copies, waits for them, and re-layouts: 2.29 us -> none  [the longest x1 1.68 us: local(): diag_inv[2]]
    unnamed x16 -> x18, local copies, waits for them, and re-layouts: 2.69 us -> 3.64 us
where the time goes in v7:
time: 161 us
  Pallas kernels  142 us (88%)
  matrix products  7.45 us (5%)
  local copies, waits for them, and re-layouts  7.28 us (5%)
  other arithmetic  3.86 us (2%)
    pallas_call x5, Pallas kernels, _call(): pl.pallas_call(functools.partial(body, n, count), out_shape=tuple((_f32(o...  142 us
    unnamed x18, local copies, waits for them, and re-layouts  3.64 us
    dot_general x2, matrix products, forward_share(): jnp.einsum('skci,skcr->sir', factor_tiles[height - 1], picked, precision=...  3.24 us

profile of v7, /device:TPU:1, one launch (start us, length us, event | category | flops | bytes accessed | tf_op | source)
XLA Modules:
  0.0 160.6 jit_solution(16316290969984867374)
XLA Ops:
  0.0 0.7 copy-done.7
  0.7 0.1 reshape.652
  0.8 36.9 %shard_map.55 = (f32[2,32,128]{2,1,0:T(8,128)}, f32[15,2,32,128]{3,2,1,0:T(8,128)}, f32[2,256,256]{2,1,0:T(8,128)}) custom-call(f32[3,2,32,128]{3,2,1,0:T(8,128)} %rhs_ref.1, f32[3,2,32,256]{3,2,1,0:T(8,128)} %dinv_ref.5), custom_call_target="tpu_custom_call" | custom-call | tf_op jit(solution)/shard_map/pallas_call | solution.py:314
  37.7 1.6 gather_fusion
  39.4 0.7 copy-done.8
  40.1 2.1 %convolution_bitcast_fusion.1 = f32[2,128,256]{1,2,0:T(8,128)S(1)} fusion(f32[2,2,8,32,256]{4,3,2,1,0:T(8,128)} %param.7, f32[2,8,32,128]{3,2,1,0:T(8,128)S(1)} %bitcast.157, f32[2,8]{1,0:T(2,128)S(1)} %get-tuple-element.36, pred[2,8]{1,0:T(4,128)(4,1)S(1)} %get-tuple-element.28), kind=kOutput, calls=%fused_computation.5 | convolution fusion | flops 201457664 | bytes 1048656 | tf_op jit(solution)/shard_map/skci,skcr->sir/dot_general | solution.py:364
  42.3 0.9 copy-done.4
  43.2 0.7 copy-done.3
  43.9 29.9 %shard_map.56 = (f32[2,32,128]{2,1,0:T(8,128)}, f32[15,2,32,128]{3,2,1,0:T(8,128)}, f32[2,256,256]{2,1,0:T(8,128)}) custom-call(f32[2,256,128]{2,1,0:T(8,128)} %copy-done.3, f32[2,256,256]{2,1,0:T(8,128)} %get-tuple-element.16.dw_ref, f32[3,2,32,256]{3,2,1,0:T(8,128)} %dinv_ref.5), custom_call_target="tpu_custom_call" | custom-call | tf_op jit(solution)/shard_map/pallas_call | solution.py:314
  73.8 1.2 pad_maximum_fusion
  75.1 0.6 gather_fusion.1
  75.7 1.1 convolution_bitcast_fusion
  76.8 0.7 copy-done.2
  77.5 19.7 %shard_map.57 = (f32[2,32,128]{2,1,0:T(8,128)}, f32[2,256,128]{2,1,0:T(8,128)}, f32[2,32,128]{2,1,0:T(8,128)}) custom-call(f32[2,256,128]{2,1,0:T(8,128)} %copy-done.2, f32[2,256,256]{2,1,0:T(8,128)} %get-tuple-element.18.dw_ref), custom_call_target="tpu_custom_call" | custom-call | tf_op jit(solution)/shard_map/pallas_call | solution.py:314
  97.2 1.6 convolution_multiply_fusion.1
  99.0 0.6 fusion.12
  99.6 0.3 copy.35
  99.9 0.8 slice.50.x_ref
  100.8 30.5 %shard_map.58 = (f32[1,2,32,128]{3,2,1,0:T(8,128)}, f32[2,256,128]{2,1,0:T(8,128)}, f32[2,32,128]{2,1,0:T(8,128)}) custom-call(f32[15,1,2,32,128]{4,3,2,1,0:T(8,128)} %slice.50.x_ref, f32[2,32,128]{2,1,0:T(8,128)} %get-tuple-element.20.f_ref, f32[2,256,256]{2,1,0:T(8,128)} %get-tuple-element.16.dw_ref), custom_call_target="tpu_custom_call" | custom-call | tf_op jit(solution)/shard_map/pallas_call | solution.py:314
  131.3 1.5 convolution_multiply_fusion
  132.9 0.5 fusion.10
  133.4 1.0 slice_add_fusion.x_ref
  134.4 24.8 %shard_map.59 = f32[2,32,128]{2,1,0:T(8,128)} custom-call(f32[15,1,2,32,128]{4,3,2,1,0:T(8,128)} %slice_add_fusion.x_ref, f32[2,32,128]{2,1,0:T(8,128)} %get-tuple-element.22.f_ref, f32[3,2,32,256]{3,2,1,0:T(8,128)} %dinv_ref.5), custom_call_target="tpu_custom_call" | custom-call | tf_op jit(solution)/shard_map/pallas_call | solution.py:314
  159.2 1.4 pad_maximum_fusion.1
  (30 shorter events, 0.5 us)
Async XLA Ops:
  0.0 0.7 copy-start.7
  39.3 0.7 copy-start.8
  42.3 0.9 copy-start.4
  43.2 0.7 copy-start.3
  43.9 29.9 %copy-start.1 = (f32[15,2,32,128]{3,2,1,0:T(8,128)S(1)}, f32[15,2,32,128]{3,2,1,0:T(8,128)}, u32[]{:S(2)}) copy-start(f32[15,2,32,128]{3,2,1,0:T(8,128)} %get-tuple-element.15) | copy-start | bytes 1474564
  73.8 1.9 %copy-start = (f32[2,2,8,32,256]{4,3,2,1,0:T(8,128)S(1)}, f32[2,2,8,32,256]{4,3,2,1,0:T(8,128)}, u32[]{:S(2)}) copy-start(f32[2,2,8,32,256]{4,3,2,1,0:T(8,128)} %param.7) | copy-start | bytes 3145732
  76.8 0.7 copy-start.2
  134.4 24.8 %copy-start.5 = (f32[2,32,128]{2,1,0:T(8,128)S(1)}, f32[2,32,128]{2,1,0:T(8,128)}, u32[]{:S(2)}) copy-start(f32[2,32,128]{2,1,0:T(8,128)} %get-tuple-element.24) | copy-start | bytes 98308
  134.4 24.8 %copy-start.6 = (f32[2,32,128]{2,1,0:T(8,128)S(1)}, f32[2,32,128]{2,1,0:T(8,128)}, u32[]{:S(2)}) copy-start(f32[2,32,128]{2,1,0:T(8,128)} %get-tuple-element.23) | copy-start | bytes 98308

commit v8 on v7

--- a/solution.py
+++ b/solution.py
@@ -299,6 +299,67 @@
     x2_ref[...] = jnp.stack(outs, 0)
     sends += scatter_start(p, x2_ref, got, s, r)
     own_ref[...] = scatter_finish(p, x2_ref, got, s, r)
+    _wait_sends(sends)
+
+
+def _mm(a, b):
+    return jnp.dot(a, b, precision=lax.Precision.HIGHEST, preferred_element_type=jnp.float32)
+
+
+def _smem():
+    return pl.BlockSpec(memory_space=pltpu.SMEM)
+
+
+def _share(p, wins, t_ref, lev_ref, slot_ref, sup_ref, live_ref, rhs_ref, out_ref):
+    owned, share, r = rhs_ref.shape
+    slots = lev_ref.shape[1]
+    mine = pl.ds(pl.multiple_of(p.col * share, share), share)
+    for s in range(owned):
+        pieces = []
+        for k in range(slots):
+            w = slot_ref[s, k]
+            q = sup_ref[s, k]
+            v = wins[0][w, q]
+            if len(wins) > 1:
+                v = jnp.where(lev_ref[s, k] == 0, v, wins[1][w, q])
+            pieces.append(v * live_ref[s, k])
+        picked = jnp.concatenate(pieces, axis=0)
+        out_ref[s] = -_mm(t_ref[s].T, picked)
+        out_ref[s, mine, :] = rhs_ref[s] + out_ref[s, mine, :]
+
+
+def _forward_kernel(
+    n, count,
+    rhs_ref, dinv_ref, t1_ref, t2_ref, lv1, sl1, su1, li1, lv2, sl2, su2, li2,
+    fv0_ref, fv1_ref, sol2_ref, mine2_ref, d1_ref, d2_ref,
+    got_y, sy, ry, whole, win0, got_w0, sw0, rw0, got_d1, sd1, rd1, got_d2, sd2, rd2,
+    share1, x1, got_x1, sx1, rx1, win1, got_w1, sw1, rw1,
+    share2, x2, got_x2, sx2, rx2, fv2, full2, got_y2, sy2, ry2,
+):
+    p = Place(n, count)
+    p.barrier(True, True)
+    sends = gather_start(p, rhs_ref.at[0], got_y, sy, ry)
+    gather_finish(p, rhs_ref.at[0], got_y, sy, ry, whole)
+    fv0_ref[...] = _dots(dinv_ref.at[0], whole)
+    sends += bcast_start(p, fv0_ref, got_w0, sw0, rw0)
+    sends += gather_start(p, dinv_ref.at[1], got_d1, sd1, rd1) + gather_start(p, dinv_ref.at[2], got_d2, sd2, rd2)
+    bcast_finish(p, fv0_ref, got_w0, sw0, rw0, win0)
+    gather_finish(p, dinv_ref.at[1], got_d1, sd1, rd1, d1_ref)
+    _share(p, [win0], t1_ref, lv1, sl1, su1, li1, rhs_ref.at[1], share1)
+    x1[...] = _dots(d1_ref, share1)
+    sends += scatter_start(p, x1, got_x1, sx1, rx1)
+    fv1_ref[...] = scatter_finish(p, x1, got_x1, sx1, rx1)
+    sends += bcast_start(p, fv1_ref, got_w1, sw1, rw1)
+    bcast_finish(p, fv1_ref, got_w1, sw1, rw1, win1)
+    gather_finish(p, dinv_ref.at[2], got_d2, sd2, rd2, d2_ref)
+    _share(p, [win0, win1], t2_ref, lv2, sl2, su2, li2, rhs_ref.at[2], share2)
+    x2[...] = _dots(d2_ref, share2)
+    sends += scatter_start(p, x2, got_x2, sx2, rx2)
+    fv2[...] = scatter_finish(p, x2, got_x2, sx2, rx2)
+    sends += gather_start(p, fv2, got_y2, sy2, ry2)
+    gather_finish(p, fv2, got_y2, sy2, ry2, full2)
+    sol2_ref[...] = _dots(d2_ref, full2, transpose_a=True)
+    mine2_ref[...] = _rows_of(sol2_ref, p.col, mine2_ref.shape[1])[...]
     _wait_sends(sends)
 
 
@@ -390,18 +451,33 @@
     def vm(shape):
         return pltpu.VMEM(shape, jnp.float32)
 
-    fv0, win0, d1 = _call(
-        _first_kernel, n, count, 0, [rhs, diag_inv], [blk, win, dwhole],
-        [vm((n,) + blk)] + _dma(n) + [vm(whole)] + [vm(win)] + _dma(slots) + [vm((n,) + dblk)] + _dma(n),
-    )
-    fv1, win1, d2 = _call(
-        _level1_kernel, n, count, 1, [forward_share(1, [win0]), d1, diag_inv], [blk, win, dwhole],
-        [vm(whole), vm((n,) + blk)] + _dma(n) + [vm(win)] + _dma(slots) + [vm((n,) + dblk)] + _dma(n),
-    )
-    fv2, sol2, mine2 = _call(
-        _level2_kernel, n, count, 2, [forward_share(2, [win0, win1]), d2], [blk, whole, blk],
-        [vm(whole), vm((n,) + blk)] + _dma(n) + [vm(whole), vm((n,) + blk)] + _dma(n),
-    )
+    def source_tables(height):
+        sources = tile_source[height - 1]
+        src_level = jnp.clip(sources // total_sup, 0, height - 1)
+        within = sources % total_sup
+        slot = jnp.clip(within // owned_count - row_place + reach_dev, 0, window_len - 1)
+        return [src_level, slot, within % owned_count, live_mask(tile_count[height - 1])]
+
+    def flat_tiles(height):
+        t = factor_tiles[height - 1]
+        return t.reshape(t.shape[0], t.shape[1] * t.shape[2], t.shape[3])
+
+    nblk = (n,) + blk
+    fwd_args = [rhs, diag_inv, flat_tiles(1), flat_tiles(2)] + source_tables(1) + source_tables(2)
+    fv0, fv1, sol2, mine2, d1, d2 = pl.pallas_call(
+        functools.partial(_forward_kernel, n, count),
+        out_shape=tuple(_f32(o) for o in [blk, blk, whole, blk, dwhole, dwhole]),
+        in_specs=[_vmem()] * 4 + [_smem()] * 8,
+        out_specs=tuple(_vmem() for o in range(6)),
+        scratch_shapes=[vm(nblk)] + _dma(n) + [vm(whole)]
+        + [vm(win), vm(win)] + _dma(slots)
+        + [vm((n,) + dblk)] + _dma(n) + [vm((n,) + dblk)] + _dma(n)
+        + [vm(whole), vm(whole), vm(nblk)] + _dma(n)
+        + [vm(win), vm(win)] + _dma(slots)
+        + [vm(whole), vm(whole), vm(nblk)] + _dma(n)
+        + [vm(blk), vm(whole), vm(nblk)] + _dma(n),
+        compiler_params=_params(0),
+    )(*fwd_args)
     out2 = buckets(2, sol2)
     got2, sol1, mine1 = _call(
         _back2_kernel, n, count, 3, [out2[:, 1:], fv1, d1], [out2[:, 1:].shape[1:], whole, blk],

time: 161 us -> 149 us (0.925)
  Pallas kernels: 142 us -> 133 us
  matrix products: 7.45 us -> 4.23 us
  local copies, waits for them, and re-layouts: 7.28 us -> 5.66 us
    pallas_call x5 -> x2, Pallas kernels: 142 us -> 49.6 us  [_call(): pl.pallas_call(functools.partial(body, n, count), out_shape=tuple((_f32(o...]
    pallas_call x0 -> x1, Pallas kernels: none -> 83.2 us  [local(): pl.pallas_call(functools.partial(_forward_kernel, n, count), out_shape=tu...]
    dot_general x2 -> x0, matrix products: 3.24 us -> none  [forward_share(): jnp.einsum('skci,skcr->sir', factor_tiles[height - 1], picked, precision=...]
    slice x0 -> x1, local copies, waits for them, and re-layouts: none -> 2.32 us  [buckets(): factor_tiles[height - 1]]
    gather x2 -> x0, local copies, waits for them, and re-layouts: 2.16 us -> none  [forward_share(): jnp.take(stacked, places, axis=0)]
    unnamed x18 -> x14, local copies, waits for them, and re-layouts: 3.64 us -> 2.03 us
where the time goes in v8:
time: 149 us; the launch traced here: 148 us
  Pallas kernels  133 us (89%)
  local copies, waits for them, and re-layouts  5.66 us (4%)
  other arithmetic  5.03 us (3%)
  matrix products  4.23 us (3%)
    pallas_call x1, Pallas kernels, local(): pl.pallas_call(functools.partial(_forward_kernel, n, count), out_shape=tu...  83.2 us
    pallas_call x2, Pallas kernels, _call(): pl.pallas_call(functools.partial(body, n, count), out_shape=tuple((_f32(o...  49.6 us
    dot_general x2, matrix products, buckets(): jnp.einsum('skci,sir->skcr', factor_tiles[height - 1], whole_block, preci...  3.11 us

profile of v8, /device:TPU:1, one launch (start us, length us, event | category | flops | bytes accessed | tf_op | source)
XLA Modules:
  0.0 147.9 jit_solution(16435107548687528721)
XLA Ops:
  0.0 1.3 and_select_fusion
  1.3 0.6 add_clamp_fusion
  1.9 0.7 copy-done.6
  2.6 0.7 compare_convert_fusion
  3.3 2.3 %fusion.22 = (f32[1,2,8,32,256]{4,3,2,1,0:T(8,128)}, f32[1,2,8,32,256]{4,3,2,1,0:T(8,128)}) fusion(f32[2,2,8,32,256]{4,3,2,1,0:T(8,128)} %param.7), kind=kLoop, calls=%fused_computation.86 | loop fusion | bytes 2097152 | tf_op jit(solution)/shard_map/slice | solution.py:434
  5.6 83.2 %shard_map.55 = (f32[2,32,128]{2,1,0:T(8,128)}, f32[2,32,128]{2,1,0:T(8,128)}, f32[2,256,128]{2,1,0:T(8,128)}, f32[2,32,128]{2,1,0:T(8,128)}, f32[2,256,256]{2,1,0:T(8,128)}, /*index=5*/f32[2,256,256]{2,1,0:T(8,128)}) custom-call(f32[3,2,32,128]{3,2,1,0:T(8,128)} %rhs_ref.1, f32[3,2,32,256]{3,2,1,0:T(8,128)} %dinv_ref.3, f32[2,256,256]{2,1,0:T(8,128)} %bitcast.100, ...), custom_call_target="tpu_custom_call" | custom-call | tf_op jit(solution)/shard_map/pallas_call | solution.py:467
  88.8 0.0 copy-start.4
  88.8 0.0 copy-done
  88.9 0.7 copy-done.4
  89.5 1.6 %convolution_multiply_fusion.1 = f32[2,128,8,32]{1,3,2,0:T(8,128)S(1)} fusion(f32[2,256,128]{2,1,0:T(8,128)} %get-tuple-element.12, f32[2,8]{1,0:T(2,128)S(1)} %copy-done.4, f32[2,2,8,32,256]{4,3,2,1,0:T(8,128)S(1)} %copy-done), kind=kOutput, calls=%fused_computation.1 | convolution fusion | flops 201392128 | bytes 1049600 | tf_op jit(solution)/shard_map/skci,sir->skcr/dot_general | solution.py:433
  91.1 0.0 copy-done.5
  91.1 0.1 squeeze.18
  91.2 0.1 squeeze.19
  91.3 0.6 fusion.6
  91.9 0.3 copy.25
  92.3 0.8 slice.38.x_ref
  93.1 25.4 %shard_map.56 = (f32[1,2,32,128]{3,2,1,0:T(8,128)}, f32[2,256,128]{2,1,0:T(8,128)}, f32[2,32,128]{2,1,0:T(8,128)}) custom-call(f32[15,1,2,32,128]{4,3,2,1,0:T(8,128)} %slice.38.x_ref, f32[2,32,128]{2,1,0:T(8,128)} %get-tuple-element.13.f_ref, f32[2,256,256]{2,1,0:T(8,128)} %get-tuple-element.14.dw_ref), custom_call_target="tpu_custom_call" | custom-call | tf_op jit(solution)/shard_map/pallas_call | solution.py:375
  118.5 0.0 copy-start.3
  118.5 0.7 copy-done.3
  119.2 1.5 %convolution_multiply_fusion = f32[2,128,8,32]{1,3,2,0:T(8,128)S(1)} fusion(f32[2,256,128]{2,1,0:T(8,128)} %get-tuple-element.15, f32[2,8]{1,0:T(2,128)S(1)} %copy-done.3, f32[2,2,8,32,256]{4,3,2,1,0:T(8,128)S(1)} %copy-done), kind=kOutput, calls=%fused_computation | convolution fusion | flops 201392128 | bytes 1049600 | tf_op jit(solution)/shard_map/skci,sir->skcr/dot_general | solution.py:433
  120.7 0.5 fusion.4
  121.2 1.0 slice_add_fusion.x_ref
  122.2 24.2 %shard_map.57 = f32[2,32,128]{2,1,0:T(8,128)} custom-call(f32[15,1,2,32,128]{4,3,2,1,0:T(8,128)} %slice_add_fusion.x_ref, f32[2,32,128]{2,1,0:T(8,128)} %get-tuple-element.16.f_ref, f32[3,2,32,256]{3,2,1,0:T(8,128)} %dinv_ref.3), custom_call_target="tpu_custom_call" | custom-call | tf_op jit(solution)/shard_map/pallas_call | solution.py:375
  146.5 1.4 pad_maximum_fusion
  (12 shorter events, 0.1 us)
Async XLA Ops:
  1.9 0.7 copy-start.6
  5.6 83.3 %copy-start = (f32[2,2,8,32,256]{4,3,2,1,0:T(8,128)S(1)}, f32[2,2,8,32,256]{4,3,2,1,0:T(8,128)}, u32[]{:S(2)}) copy-start(f32[2,2,8,32,256]{4,3,2,1,0:T(8,128)} %param.7) | copy-start | bytes 3145732
  88.8 0.7 copy-start.4
  89.5 1.6 %copy-start.5 = (s32[2,2,8]{2,1,0:T(2,128)S(1)}, s32[2,2,8]{2,1,0:T(2,128)}, u32[]{:S(2)}) copy-start(s32[2,2,8]{2,1,0:T(2,128)} %param.8) | copy-start | bytes 388
  118.5 0.7 copy-start.3
  122.2 24.2 %copy-start.1 = (f32[2,32,128]{2,1,0:T(8,128)S(1)}, f32[2,32,128]{2,1,0:T(8,128)}, u32[]{:S(2)}) copy-start(f32[2,32,128]{2,1,0:T(8,128)} %get-tuple-element.18) | copy-start | bytes 98308
  122.2 24.2 %copy-start.2 = (f32[2,32,128]{2,1,0:T(8,128)S(1)}, f32[2,32,128]{2,1,0:T(8,128)}, u32[]{:S(2)}) copy-start(f32[2,32,128]{2,1,0:T(8,128)} %get-tuple-element.17) | copy-start | bytes 98308

commit v9 on v8

--- a/solution.py
+++ b/solution.py
@@ -328,13 +328,37 @@
         out_ref[s, mine, :] = rhs_ref[s] + out_ref[s, mine, :]
 
 
+def _terms(t_ref, sol_ref, terms_ref):
+    owned, slots, share, r = terms_ref.shape
+    for s in range(owned):
+        full = _mm(t_ref[s], sol_ref[s])
+        for k in range(slots):
+            terms_ref[s, k] = full[k * share : (k + 1) * share]
+
+
+def _route(bucket_ref, level, parts):
+    slots, owned, share, r = bucket_ref.shape
+    for w in range(slots):
+        for q in range(owned):
+            m = (level * slots + w) * owned + q
+            acc = None
+            for terms_ref, pick_ref, flag_ref in parts:
+                for s in range(terms_ref.shape[0]):
+                    v = terms_ref[s, pick_ref[m, s]] * flag_ref[m, s]
+                    acc = v if acc is None else acc + v
+            bucket_ref[w, q] = acc
+
+
 def _forward_kernel(
     n, count,
-    rhs_ref, dinv_ref, t1_ref, t2_ref, lv1, sl1, su1, li1, lv2, sl2, su2, li2,
-    fv0_ref, fv1_ref, sol2_ref, mine2_ref, d1_ref, d2_ref,
+    rhs_ref, dinv_ref, t1_ref, t2_ref, lv1, sl1, su1, li1, lv2, sl2, su2, li2, pk1, fl1, pk2, fl2,
+    out_ref,
+    fv0_ref, fv1_ref, sol2_ref, d1_ref, d2_ref,
     got_y, sy, ry, whole, win0, got_w0, sw0, rw0, got_d1, sd1, rd1, got_d2, sd2, rd2,
     share1, x1, got_x1, sx1, rx1, win1, got_w1, sw1, rw1,
     share2, x2, got_x2, sx2, rx2, fv2, full2, got_y2, sy2, ry2,
+    terms2, bucket1, got_b1, sb1, rb1, res1, got_z1, sz1, rz1, full1, sol1,
+    terms1, bucket0, got_b0, sb0, rb0, x0, got_x0, sx0, rx0,
 ):
     p = Place(n, count)
     p.barrier(True, True)
@@ -359,7 +383,24 @@
     sends += gather_start(p, fv2, got_y2, sy2, ry2)
     gather_finish(p, fv2, got_y2, sy2, ry2, full2)
     sol2_ref[...] = _dots(d2_ref, full2, transpose_a=True)
-    mine2_ref[...] = _rows_of(sol2_ref, p.col, mine2_ref.shape[1])[...]
+    share = fv2.shape[1]
+    out_ref[2] = _rows_of(sol2_ref, p.col, share)[...]
+    _terms(t2_ref, sol2_ref, terms2)
+    _route(bucket1, 1, [(terms2, pk2, fl2)])
+    sends += spread_start(p, bucket1, got_b1, sb1, rb1)
+    res1[...] = fv1_ref[...] - spread_finish(p, bucket1, got_b1, sb1, rb1)
+    sends += gather_start(p, res1, got_z1, sz1, rz1)
+    gather_finish(p, res1, got_z1, sz1, rz1, full1)
+    sol1[...] = _dots(d1_ref, full1, transpose_a=True)
+    out_ref[1] = _rows_of(sol1, p.col, share)[...]
+    _terms(t1_ref, sol1, terms1)
+    _route(bucket0, 0, [(terms2, pk2, fl2), (terms1, pk1, fl1)])
+    sends += spread_start(p, bucket0, got_b0, sb0, rb0)
+    res0 = fv0_ref[...] - spread_finish(p, bucket0, got_b0, sb0, rb0)
+    d0 = dinv_ref.at[0]
+    x0[...] = jnp.stack([_mm(d0[q].T, res0[q]) for q in range(res0.shape[0])], 0)
+    sends += scatter_start(p, x0, got_x0, sx0, rx0)
+    out_ref[0] = scatter_finish(p, x0, got_x0, sx0, rx0)
     _wait_sends(sends)
 
 
@@ -462,12 +503,24 @@
         t = factor_tiles[height - 1]
         return t.reshape(t.shape[0], t.shape[1] * t.shape[2], t.shape[3])
 
+    def lookup(height):
+        places = window_places(tile_source[height - 1])
+        live = tile_count[height - 1][:, None] > slot_ids[None, :]
+        targets = height * window_len * owned_count
+        match = (places[None, :, :] == jnp.arange(targets, dtype=jnp.int32)[:, None, None]) & live[None]
+        pick = jnp.sum(match.astype(jnp.int32) * slot_ids[None, None, :], axis=-1)
+        return [pick, jnp.any(match, axis=-1).astype(jnp.float32)]
+
     nblk = (n,) + blk
-    fwd_args = [rhs, diag_inv, flat_tiles(1), flat_tiles(2)] + source_tables(1) + source_tables(2)
-    fv0, fv1, sol2, mine2, d1, d2 = pl.pallas_call(
+    tiles = (owned_count, slot_count, share_rows, columns)
+    args = (
+        [rhs, diag_inv, flat_tiles(1), flat_tiles(2)] + source_tables(1) + source_tables(2)
+        + lookup(1) + lookup(2)
+    )
+    outs = pl.pallas_call(
         functools.partial(_forward_kernel, n, count),
-        out_shape=tuple(_f32(o) for o in [blk, blk, whole, blk, dwhole, dwhole]),
-        in_specs=[_vmem()] * 4 + [_smem()] * 8,
+        out_shape=tuple(_f32(o) for o in [rhs.shape, blk, blk, whole, dwhole, dwhole]),
+        in_specs=[_vmem()] * 4 + [_smem()] * 12,
         out_specs=tuple(_vmem() for o in range(6)),
         scratch_shapes=[vm(nblk)] + _dma(n) + [vm(whole)]
         + [vm(win), vm(win)] + _dma(slots)
@@ -475,20 +528,12 @@
         + [vm(whole), vm(whole), vm(nblk)] + _dma(n)
         + [vm(win), vm(win)] + _dma(slots)
         + [vm(whole), vm(whole), vm(nblk)] + _dma(n)
-        + [vm(blk), vm(whole), vm(nblk)] + _dma(n),
+        + [vm(blk), vm(whole), vm(nblk)] + _dma(n)
+        + [vm(tiles), vm(win), vm(win)] + _dma(slots) + [vm(blk), vm(nblk)] + _dma(n) + [vm(whole), vm(whole)]
+        + [vm(tiles), vm(win), vm(win)] + _dma(slots) + [vm(whole), vm(nblk)] + _dma(n),
         compiler_params=_params(0),
-    )(*fwd_args)
-    out2 = buckets(2, sol2)
-    got2, sol1, mine1 = _call(
-        _back2_kernel, n, count, 3, [out2[:, 1:], fv1, d1], [out2[:, 1:].shape[1:], whole, blk],
-        [vm(out2[:, 1:].shape)] + _dma(slots) + [vm(blk), vm(whole), vm((n,) + blk)] + _dma(n),
-    )
-    out1 = buckets(1, sol1) + out2[:, :1]
-    (sol0,) = _call(
-        _final_kernel, n, count, 4, [out1, fv0, diag_inv], [blk],
-        [vm(out1.shape)] + _dma(slots) + [vm(whole), vm((n,) + blk)] + _dma(n),
-    )
-    return jnp.stack([sol0, mine1, mine2], 0)
+    )(*args)
+    return outs[0]
 
 
 def solution(mesh):

time: 149 us -> 132 us (0.89)
  Pallas kernels: 133 us -> 122 us
  matrix products: 4.23 us -> 0 us
  other arithmetic: 5.03 us -> 1.7 us
  local copies, waits for them, and re-layouts: 5.66 us -> 8 us
    pallas_call x2 -> x0, Pallas kernels: 49.6 us -> none  [_call(): pl.pallas_call(functools.partial(body, n, count), out_shape=tuple((_f32(o...]
    pallas_call x1, Pallas kernels: 83.2 us -> 122 us  [local(): pl.pallas_call(functools.partial(_forward_kernel, n, count), out_shape=tu...]
    dot_general x4 -> x0, matrix products: 4.23 us -> none  [the longest x2 3.11 us: buckets(): jnp.einsum('skci,sir->skcr', factor_tiles[height - 1], whole_block, preci...]
    slice x3 -> x1, local copies, waits for them, and re-layouts: 3.15 us -> 2.31 us  [flat_tiles(): t = factor_tiles[height - 1]]
where the time goes in v9:
time: 132 us; the launch traced here: 131 us
  Pallas kernels  122 us (92%)
  local copies, waits for them, and re-layouts  8 us (6%)
  other arithmetic  1.7 us (1%)
    pallas_call x1, Pallas kernels, local(): pl.pallas_call(functools.partial(_forward_kernel, n, count), out_shape=tu...  122 us
    unnamed x5, local copies, waits for them, and re-layouts  2.9 us

profile of v9, /device:TPU:1, one launch (start us, length us, event | category | flops | bytes accessed | tf_op | source)
XLA Modules:
  0.0 131.5 jit_solution(13309116559168009027)
XLA Ops:
  0.0 0.0 copy-start.1
  0.0 0.7 copy-done.1
  0.7 0.7 iota_compare_fusion.2
  1.4 0.0 copy-start
  1.4 0.7 copy-done
  2.1 0.1 fusion.3
  2.2 0.1 select_reduce_fusion
  2.2 0.1 fusion.1
  2.3 0.1 select_reduce_fusion.1
  2.4 0.6 and_select_fusion.8
  3.1 0.7 copy.11.fl1
  3.8 0.7 copy.10.pk1
  4.4 0.7 copy.13.fl2
  5.2 0.7 copy.12.pk2
  5.9 2.3 %fusion.11 = (f32[1,2,8,32,256]{4,3,2,1,0:T(8,128)}, f32[1,2,8,32,256]{4,3,2,1,0:T(8,128)}) fusion(f32[2,2,8,32,256]{4,3,2,1,0:T(8,128)} %param.7), kind=kLoop, calls=%fused_computation.74 | loop fusion | bytes 2097152 | tf_op jit(solution)/shard_map/slice | solution.py:503
  8.2 121.8 %shard_map.55 = (f32[3,2,32,128]{3,2,1,0:T(8,128)}, f32[2,32,128]{2,1,0:T(8,128)}, f32[2,32,128]{2,1,0:T(8,128)}, f32[2,256,128]{2,1,0:T(8,128)}, f32[2,256,256]{2,1,0:T(8,128)}, /*index=5*/f32[2,256,256]{2,1,0:T(8,128)}) custom-call(f32[3,2,32,128]{3,2,1,0:T(8,128)} %rhs_ref.1, f32[3,2,32,256]{3,2,1,0:T(8,128)} %dinv_ref.1, f32[2,256,256]{2,1,0:T(8,128)} %bitcast.59, ...), custom_call_target="tpu_custom_call" | custom-call | tf_op jit(solution)/shard_map/pallas_call | solution.py:520
  130.0 1.5 %copy.15 = f32[3,2,32,128]{3,2,1,0:T(8,128)} copy(f32[3,2,32,128]{3,2,1,0:T(8,128)} %get-tuple-element.6) | data formatting | bytes 196608
  (4 shorter events, 0.0 us)
Async XLA Ops:
  0.0 0.7 copy-start.1
  1.4 0.7 copy-start

commit v10 on v9

--- a/solution.py
+++ b/solution.py
@@ -310,19 +310,20 @@
     return pl.BlockSpec(memory_space=pltpu.SMEM)
 
 
-def _share(p, wins, t_ref, lev_ref, slot_ref, sup_ref, live_ref, rhs_ref, out_ref):
+def _share(p, wins, t_ref, table, base, slots, rhs_ref, out_ref):
     owned, share, r = rhs_ref.shape
-    slots = lev_ref.shape[1]
     mine = pl.ds(pl.multiple_of(p.col * share, share), share)
+    size = owned * slots
     for s in range(owned):
         pieces = []
         for k in range(slots):
-            w = slot_ref[s, k]
-            q = sup_ref[s, k]
+            at = base + s * slots + k
+            w = table[at + size]
+            q = table[at + 2 * size]
             v = wins[0][w, q]
             if len(wins) > 1:
-                v = jnp.where(lev_ref[s, k] == 0, v, wins[1][w, q])
-            pieces.append(v * live_ref[s, k])
+                v = jnp.where(table[at] == 0, v, wins[1][w, q])
+            pieces.append(jnp.where(table[at + 3 * size] != 0, v, 0.0))
         picked = jnp.concatenate(pieces, axis=0)
         out_ref[s] = -_mm(t_ref[s].T, picked)
         out_ref[s, mine, :] = rhs_ref[s] + out_ref[s, mine, :]
@@ -336,22 +337,24 @@
             terms_ref[s, k] = full[k * share : (k + 1) * share]
 
 
-def _route(bucket_ref, level, parts):
+def _route(bucket_ref, level, table, parts):
     slots, owned, share, r = bucket_ref.shape
     for w in range(slots):
         for q in range(owned):
             m = (level * slots + w) * owned + q
             acc = None
-            for terms_ref, pick_ref, flag_ref in parts:
-                for s in range(terms_ref.shape[0]):
-                    v = terms_ref[s, pick_ref[m, s]] * flag_ref[m, s]
+            for terms_ref, base in parts:
+                count = terms_ref.shape[0]
+                for s in range(count):
+                    at = base + 2 * (m * count + s)
+                    v = jnp.where(table[at + 1] != 0, terms_ref[s, table[at]], 0.0)
                     acc = v if acc is None else acc + v
             bucket_ref[w, q] = acc
 
 
 def _forward_kernel(
     n, count,
-    rhs_ref, dinv_ref, t1_ref, t2_ref, lv1, sl1, su1, li1, lv2, sl2, su2, li2, pk1, fl1, pk2, fl2,
+    rhs_ref, dinv_ref, ft_ref, table,
     out_ref,
     fv0_ref, fv1_ref, sol2_ref, d1_ref, d2_ref,
     got_y, sy, ry, whole, win0, got_w0, sw0, rw0, got_d1, sd1, rd1, got_d2, sd2, rd2,
@@ -360,6 +363,12 @@
     terms2, bucket1, got_b1, sb1, rb1, res1, got_z1, sz1, rz1, full1, sol1,
     terms1, bucket0, got_b0, sb0, rb0, x0, got_x0, sx0, rx0,
 ):
+    t1_ref, t2_ref = ft_ref.at[0], ft_ref.at[1]
+    owned = rhs_ref.shape[1]
+    slots = terms1.shape[1]
+    size = owned * slots
+    lookup1 = 8 * size
+    lookup2 = lookup1 + (2 * KDEV + 1) * owned * owned * 2
     p = Place(n, count)
     p.barrier(True, True)
     sends = gather_start(p, rhs_ref.at[0], got_y, sy, ry)
@@ -369,14 +378,14 @@
     sends += gather_start(p, dinv_ref.at[1], got_d1, sd1, rd1) + gather_start(p, dinv_ref.at[2], got_d2, sd2, rd2)
     bcast_finish(p, fv0_ref, got_w0, sw0, rw0, win0)
     gather_finish(p, dinv_ref.at[1], got_d1, sd1, rd1, d1_ref)
-    _share(p, [win0], t1_ref, lv1, sl1, su1, li1, rhs_ref.at[1], share1)
+    _share(p, [win0], t1_ref, table, 0, slots, rhs_ref.at[1], share1)
     x1[...] = _dots(d1_ref, share1)
     sends += scatter_start(p, x1, got_x1, sx1, rx1)
     fv1_ref[...] = scatter_finish(p, x1, got_x1, sx1, rx1)
     sends += bcast_start(p, fv1_ref, got_w1, sw1, rw1)
     bcast_finish(p, fv1_ref, got_w1, sw1, rw1, win1)
     gather_finish(p, dinv_ref.at[2], got_d2, sd2, rd2, d2_ref)
-    _share(p, [win0, win1], t2_ref, lv2, sl2, su2, li2, rhs_ref.at[2], share2)
+    _share(p, [win0, win1], t2_ref, table, 4 * size, slots, rhs_ref.at[2], share2)
     x2[...] = _dots(d2_ref, share2)
     sends += scatter_start(p, x2, got_x2, sx2, rx2)
     fv2[...] = scatter_finish(p, x2, got_x2, sx2, rx2)
@@ -386,7 +395,7 @@
     share = fv2.shape[1]
     out_ref[2] = _rows_of(sol2_ref, p.col, share)[...]
     _terms(t2_ref, sol2_ref, terms2)
-    _route(bucket1, 1, [(terms2, pk2, fl2)])
+    _route(bucket1, 1, table, [(terms2, lookup2)])
     sends += spread_start(p, bucket1, got_b1, sb1, rb1)
     res1[...] = fv1_ref[...] - spread_finish(p, bucket1, got_b1, sb1, rb1)
     sends += gather_start(p, res1, got_z1, sz1, rz1)
@@ -394,7 +403,7 @@
     sol1[...] = _dots(d1_ref, full1, transpose_a=True)
     out_ref[1] = _rows_of(sol1, p.col, share)[...]
     _terms(t1_ref, sol1, terms1)
-    _route(bucket0, 0, [(terms2, pk2, fl2), (terms1, pk1, fl1)])
+    _route(bucket0, 0, table, [(terms2, lookup2), (terms1, lookup1)])
     sends += spread_start(p, bucket0, got_b0, sb0, rb0)
     res0 = fv0_ref[...] - spread_finish(p, bucket0, got_b0, sb0, rb0)
     d0 = dinv_ref.at[0]
@@ -497,7 +506,8 @@
         src_level = jnp.clip(sources // total_sup, 0, height - 1)
         within = sources % total_sup
         slot = jnp.clip(within // owned_count - row_place + reach_dev, 0, window_len - 1)
-        return [src_level, slot, within % owned_count, live_mask(tile_count[height - 1])]
+        live = (tile_count[height - 1][:, None] > slot_ids[None, :]).astype(jnp.int32)
+        return [src_level, slot, within % owned_count, live]
 
     def flat_tiles(height):
         t = factor_tiles[height - 1]
@@ -509,18 +519,18 @@
         targets = height * window_len * owned_count
         match = (places[None, :, :] == jnp.arange(targets, dtype=jnp.int32)[:, None, None]) & live[None]
         pick = jnp.sum(match.astype(jnp.int32) * slot_ids[None, None, :], axis=-1)
-        return [pick, jnp.any(match, axis=-1).astype(jnp.float32)]
+        return [jnp.stack([pick, jnp.any(match, axis=-1).astype(jnp.int32)], -1)]
 
     nblk = (n,) + blk
     tiles = (owned_count, slot_count, share_rows, columns)
     args = (
-        [rhs, diag_inv, flat_tiles(1), flat_tiles(2)] + source_tables(1) + source_tables(2)
-        + lookup(1) + lookup(2)
+        [rhs, diag_inv, factor_tiles.reshape(factor_tiles.shape[:2] + (slot_count * share_rows, -1))]
+        + [jnp.concatenate([t.reshape(-1) for t in source_tables(1) + source_tables(2) + lookup(1) + lookup(2)])]
     )
     outs = pl.pallas_call(
         functools.partial(_forward_kernel, n, count),
         out_shape=tuple(_f32(o) for o in [rhs.shape, blk, blk, whole, dwhole, dwhole]),
-        in_specs=[_vmem()] * 4 + [_smem()] * 12,
+        in_specs=[_vmem()] * 3 + [_smem()],
         out_specs=tuple(_vmem() for o in range(6)),
         scratch_shapes=[vm(nblk)] + _dma(n) + [vm(whole)]
         + [vm(win), vm(win)] + _dma(slots)

time: 132 us -> 126 us (0.955)
  local copies, waits for them, and re-layouts: 8 us -> 4.27 us
    slice x1 -> x0, local copies, waits for them, and re-layouts: 2.31 us -> none  [flat_tiles(): t = factor_tiles[height - 1]]
    reduce_sum x2 -> x0, local copies, waits for them, and re-layouts: 1.41 us -> none  [lookup(): pick = jnp.sum(match.astype(jnp.int32) * slot_ids[None, None, :], axis=-1)]
where the time goes in v10:
time: 126 us
  Pallas kernels  121 us (96%)
  local copies, waits for them, and re-layouts  4.27 us (3%)
    pallas_call x1, Pallas kernels, local(): pl.pallas_call(functools.partial(_forward_kernel, n, count), out_shape=tu...  121 us
    unnamed x5, local copies, waits for them, and re-layouts  2.74 us

profile of v10, /device:TPU:1, one launch (start us, length us, event | category | flops | bytes accessed | tf_op | source)
XLA Modules:
  0.0 125.5 jit_solution(900114964998240913)
XLA Ops:
  0.0 0.0 copy-start.1
  0.0 0.7 copy-done.1
  0.7 0.1 iota_compare_fusion.2
  0.8 0.0 copy-start
  0.8 0.1 reshape.95
  0.8 0.1 reshape.94
  0.9 0.5 copy-done
  1.5 0.1 squeeze.9
  1.6 0.1 squeeze.8
  1.6 0.1 fusion.3
  1.7 0.1 select_reduce_fusion
  1.8 0.1 fusion.1
  1.9 0.1 select_reduce_fusion.1
  2.1 0.1 copy.9
  2.2 0.1 reshape.92
  2.4 0.1 copy.10
  2.5 0.2 reshape.93
  2.6 0.7 concatenate.3.table
  3.3 120.7 %shard_map.55 = (f32[3,2,32,128]{3,2,1,0:T(8,128)}, f32[2,32,128]{2,1,0:T(8,128)}, f32[2,32,128]{2,1,0:T(8,128)}, f32[2,256,128]{2,1,0:T(8,128)}, f32[2,256,256]{2,1,0:T(8,128)}, /*index=5*/f32[2,256,256]{2,1,0:T(8,128)}) custom-call(f32[3,2,32,128]{3,2,1,0:T(8,128)} %rhs_ref.1, f32[3,2,32,256]{3,2,1,0:T(8,128)} %dinv_ref.1, f32[2,2,256,256]{3,2,1,0:T(8,128)} %bitcast.15, ...), custom_call_target="tpu_custom_call" | custom-call | tf_op jit(solution)/shard_map/pallas_call | solution.py:530
  124.0 1.5 %copy.12 = f32[3,2,32,128]{3,2,1,0:T(8,128)} copy(f32[3,2,32,128]{3,2,1,0:T(8,128)} %get-tuple-element.6) | data formatting | bytes 196608
  (9 shorter events, 0.1 us)
Async XLA Ops:
  0.0 0.7 copy-start.1
  0.8 0.7 copy-start

commit v11 on v10

--- a/solution.py
+++ b/solution.py
@@ -375,9 +375,10 @@
     gather_finish(p, rhs_ref.at[0], got_y, sy, ry, whole)
     fv0_ref[...] = _dots(dinv_ref.at[0], whole)
     sends += bcast_start(p, fv0_ref, got_w0, sw0, rw0)
-    sends += gather_start(p, dinv_ref.at[1], got_d1, sd1, rd1) + gather_start(p, dinv_ref.at[2], got_d2, sd2, rd2)
+    sends += gather_start(p, dinv_ref.at[1], got_d1, sd1, rd1)
     bcast_finish(p, fv0_ref, got_w0, sw0, rw0, win0)
     gather_finish(p, dinv_ref.at[1], got_d1, sd1, rd1, d1_ref)
+    sends += gather_start(p, dinv_ref.at[2], got_d2, sd2, rd2)
     _share(p, [win0], t1_ref, table, 0, slots, rhs_ref.at[1], share1)
     x1[...] = _dots(d1_ref, share1)
     sends += scatter_start(p, x1, got_x1, sx1, rx1)

time: 126 us -> 129 us (1.024)
  Pallas kernels: 121 us -> 123 us
    pallas_call x1, Pallas kernels: 121 us -> 123 us  [local(): pl.pallas_call(functools.partial(_forward_kernel, n, count), out_shape=tu...]
where the time goes in v11:
time: 129 us; the launch traced here: 128 us
  Pallas kernels  123 us (95%)
  local copies, waits for them, and re-layouts  4.27 us (3%)
    pallas_call x1, Pallas kernels, local(): pl.pallas_call(functools.partial(_forward_kernel, n, count), out_shape=tu...  123 us
    unnamed x5, local copies, waits for them, and re-layouts  2.74 us

profile of v11, /device:TPU:1, one launch (start us, length us, event | category | flops | bytes accessed | tf_op | source)
XLA Modules:
  0.0 128.3 jit_solution(5099447192623165559)
XLA Ops:
  0.0 0.0 copy-start.1
  0.0 0.7 copy-done.1
  0.7 0.1 iota_compare_fusion.2
  0.8 0.0 copy-start
  0.8 0.1 reshape.95
  0.8 0.1 reshape.94
  0.9 0.5 copy-done
  1.5 0.1 squeeze.9
  1.6 0.1 squeeze.8
  1.6 0.1 fusion.3
  1.7 0.1 select_reduce_fusion
  1.8 0.1 fusion.1
  1.9 0.1 select_reduce_fusion.1
  2.1 0.1 copy.9
  2.2 0.1 reshape.92
  2.4 0.1 copy.10
  2.5 0.2 reshape.93
  2.6 0.7 concatenate.3.table
  3.3 123.4 %shard_map.55 = (f32[3,2,32,128]{3,2,1,0:T(8,128)}, f32[2,32,128]{2,1,0:T(8,128)}, f32[2,32,128]{2,1,0:T(8,128)}, f32[2,256,128]{2,1,0:T(8,128)}, f32[2,256,256]{2,1,0:T(8,128)}, /*index=5*/f32[2,256,256]{2,1,0:T(8,128)}) custom-call(f32[3,2,32,128]{3,2,1,0:T(8,128)} %rhs_ref.1, f32[3,2,32,256]{3,2,1,0:T(8,128)} %dinv_ref.1, f32[2,2,256,256]{3,2,1,0:T(8,128)} %bitcast.15, ...), custom_call_target="tpu_custom_call" | custom-call | tf_op jit(solution)/shard_map/pallas_call | solution.py:531
  126.8 1.5 %copy.12 = f32[3,2,32,128]{3,2,1,0:T(8,128)} copy(f32[3,2,32,128]{3,2,1,0:T(8,128)} %get-tuple-element.6) | data formatting | bytes 196608
  (9 shorter events, 0.1 us)
Async XLA Ops:
  0.0 0.7 copy-start.1
  0.8 0.7 copy-start

commit v12 on v10

--- a/solution.py
+++ b/solution.py
@@ -10,6 +10,11 @@
 KDEV = 7
 MESH = pl.DeviceIdType.MESH
 OFFSETS = [d for d in range(-KDEV, KDEV + 1) if d != 0]
+SEND_OFFSETS = sorted(OFFSETS, key=lambda d: (-abs(d), d))
+
+
+def _send_order(n):
+    return sorted(range(1, n), key=lambda k: (-min(k, n - k), k))
 
 
 def _params(cid):
@@ -74,7 +79,7 @@
 def scatter_start(p, x_ref, got, send, recv):
     chunk = got.shape[2]
     out = []
-    for k in range(1, p.n):
+    for k in _send_order(p.n):
         peer = p.col_peer(k)
         out.append(
             _copy(_rows_of(x_ref, peer, chunk), got.at[p.col], send.at[peer], recv.at[p.col], (p.row, peer))
@@ -94,7 +99,7 @@
 
 def gather_start(p, y_ref, got, send, recv):
     out = []
-    for k in range(1, p.n):
+    for k in _send_order(p.n):
         peer = p.col_peer(k)
         out.append(_copy(y_ref, got.at[p.col], send.at[peer], recv.at[p.col], (p.row, peer)))
     return _start_all(out)
@@ -111,7 +116,7 @@
 
 def bcast_start(p, v_ref, got, send, recv):
     out = []
-    for d in OFFSETS:
+    for d in SEND_OFFSETS:
         out.append(_copy(v_ref, got.at[KDEV - d], send.at[KDEV + d], recv.at[KDEV - d], (p.row_peer(d), p.col)))
     return _start_all(out)
 
@@ -126,7 +131,7 @@
 
 def spread_start(p, x_ref, got, send, recv):
     out = []
-    for d in OFFSETS:
+    for d in SEND_OFFSETS:
         out.append(
             _copy(x_ref.at[KDEV + d], got.at[KDEV - d], send.at[KDEV + d], recv.at[KDEV - d], (p.row_peer(d), p.col))
         )

time: 126 us -> 122 us (0.968)
  Pallas kernels: 121 us -> 117 us
    pallas_call x1, Pallas kernels: 121 us -> 117 us  [local(): pl.pallas_call(functools.partial(_forward_kernel, n, count), out_shape=tu...]
where the time goes in v12:
time: 122 us
  Pallas kernels  117 us (96%)
  local copies, waits for them, and re-layouts  4.27 us (3%)
    pallas_call x1, Pallas kernels, local(): pl.pallas_call(functools.partial(_forward_kernel, n, count), out_shape=tu...  117 us
    unnamed x5, local copies, waits for them, and re-layouts  2.74 us

profile of v12, /device:TPU:1, one launch (start us, length us, event | category | flops | bytes accessed | tf_op | source)
XLA Modules:
  0.0 121.8 jit_solution(2742438307009743423)
XLA Ops:
  0.0 0.0 copy-start.1
  0.0 0.7 copy-done.1
  0.7 0.1 iota_compare_fusion.2
  0.8 0.0 copy-start
  0.8 0.1 reshape.95
  0.8 0.1 reshape.94
  0.9 0.5 copy-done
  1.5 0.1 squeeze.9
  1.6 0.1 squeeze.8
  1.6 0.1 fusion.3
  1.7 0.1 select_reduce_fusion
  1.8 0.1 fusion.1
  1.9 0.1 select_reduce_fusion.1
  2.1 0.1 copy.9
  2.2 0.1 reshape.92
  2.4 0.1 copy.10
  2.5 0.2 reshape.93
  2.6 0.7 concatenate.3.table
  3.3 116.9 %shard_map.55 = (f32[3,2,32,128]{3,2,1,0:T(8,128)}, f32[2,32,128]{2,1,0:T(8,128)}, f32[2,32,128]{2,1,0:T(8,128)}, f32[2,256,128]{2,1,0:T(8,128)}, f32[2,256,256]{2,1,0:T(8,128)}, /*index=5*/f32[2,256,256]{2,1,0:T(8,128)}) custom-call(f32[3,2,32,128]{3,2,1,0:T(8,128)} %rhs_ref.1, f32[3,2,32,256]{3,2,1,0:T(8,128)} %dinv_ref.1, f32[2,2,256,256]{3,2,1,0:T(8,128)} %bitcast.15, ...), custom_call_target="tpu_custom_call" | custom-call | tf_op jit(solution)/shard_map/pallas_call | solution.py:535
  120.3 1.5 %copy.12 = f32[3,2,32,128]{3,2,1,0:T(8,128)} copy(f32[3,2,32,128]{3,2,1,0:T(8,128)} %get-tuple-element.6) | data formatting | bytes 196608
  (9 shorter events, 0.1 us)
Async XLA Ops:
  0.0 0.7 copy-start.1
  0.8 0.7 copy-start

commit v13 on v12

--- a/solution.py
+++ b/solution.py
@@ -112,6 +112,59 @@
         src = p.col_peer(p.n - k)
         _copy(y_ref, got.at[src], send.at[src], recv.at[src], (p.row, src)).wait_recv()
         _rows_of(full_ref, src, chunk)[...] = got[src]
+
+
+def _lane_block(ref, b):
+    return ref.at[:, :, pl.ds(b * 128, 128)]
+
+
+def tri_gather_start(p, d_ref, got, send, recv):
+    share = d_ref.shape[1]
+    blocks = d_ref.shape[2] // 128
+    out = []
+    for b in range(blocks):
+        copies = [
+            _copy(_lane_block(d_ref, b), _lane_block(got.at[p.col], b), send.at[b, p.col_peer(k)],
+                  recv.at[b, p.col], (p.row, p.col_peer(k)))
+            for k in _send_order(p.n)
+        ]
+        out.append((b, copies))
+
+        @pl.when((p.col + 1) * share > b * 128)
+        def _():
+            for c in copies:
+                c.start()
+    return out
+
+
+def tri_gather_finish(p, d_ref, got, send, recv, full_ref):
+    share = d_ref.shape[1]
+    blocks = d_ref.shape[2] // 128
+    _rows_of(full_ref, p.col, share)[...] = d_ref[...]
+    for k in range(1, p.n):
+        src = p.col_peer(p.n - k)
+        rows = pl.ds(pl.multiple_of(src * share, share), share)
+        for b in range(blocks):
+            lanes = pl.ds(b * 128, 128)
+
+            @pl.when((src + 1) * share > b * 128)
+            def _():
+                _copy(_lane_block(d_ref, b), _lane_block(got.at[src], b), send.at[b, src], recv.at[b, src],
+                      (p.row, src)).wait_recv()
+                full_ref[:, rows, lanes] = got[src, :, :, lanes]
+
+            @pl.when((src + 1) * share <= b * 128)
+            def _():
+                full_ref[:, rows, lanes] = jnp.zeros(full_ref.shape[:1] + (share, 128), jnp.float32)
+
+
+def tri_wait_sends(p, share, started):
+    for b, copies in started:
+
+        @pl.when((p.col + 1) * share > b * 128)
+        def _():
+            for c in copies:
+                c.wait_send()
 
 
 def bcast_start(p, v_ref, got, send, recv):
@@ -380,16 +433,16 @@
     gather_finish(p, rhs_ref.at[0], got_y, sy, ry, whole)
     fv0_ref[...] = _dots(dinv_ref.at[0], whole)
     sends += bcast_start(p, fv0_ref, got_w0, sw0, rw0)
-    sends += gather_start(p, dinv_ref.at[1], got_d1, sd1, rd1) + gather_start(p, dinv_ref.at[2], got_d2, sd2, rd2)
+    tri = [tri_gather_start(p, dinv_ref.at[1], got_d1, sd1, rd1), tri_gather_start(p, dinv_ref.at[2], got_d2, sd2, rd2)]
     bcast_finish(p, fv0_ref, got_w0, sw0, rw0, win0)
-    gather_finish(p, dinv_ref.at[1], got_d1, sd1, rd1, d1_ref)
+    tri_gather_finish(p, dinv_ref.at[1], got_d1, sd1, rd1, d1_ref)
     _share(p, [win0], t1_ref, table, 0, slots, rhs_ref.at[1], share1)
     x1[...] = _dots(d1_ref, share1)
     sends += scatter_start(p, x1, got_x1, sx1, rx1)
     fv1_ref[...] = scatter_finish(p, x1, got_x1, sx1, rx1)
     sends += bcast_start(p, fv1_ref, got_w1, sw1, rw1)
     bcast_finish(p, fv1_ref, got_w1, sw1, rw1, win1)
-    gather_finish(p, dinv_ref.at[2], got_d2, sd2, rd2, d2_ref)
+    tri_gather_finish(p, dinv_ref.at[2], got_d2, sd2, rd2, d2_ref)
     _share(p, [win0, win1], t2_ref, table, 4 * size, slots, rhs_ref.at[2], share2)
     x2[...] = _dots(d2_ref, share2)
     sends += scatter_start(p, x2, got_x2, sx2, rx2)
@@ -416,6 +469,8 @@
     sends += scatter_start(p, x0, got_x0, sx0, rx0)
     out_ref[0] = scatter_finish(p, x0, got_x0, sx0, rx0)
     _wait_sends(sends)
+    for started in tri:
+        tri_wait_sends(p, share, started)
 
 
 def _f32(shape):
@@ -527,6 +582,8 @@
         return [jnp.stack([pick, jnp.any(match, axis=-1).astype(jnp.int32)], -1)]
 
     nblk = (n,) + blk
+    lane_blocks = diag_inv.shape[3] // 128
+    tri_dma = [pltpu.SemaphoreType.DMA((lane_blocks, n)), pltpu.SemaphoreType.DMA((lane_blocks, n))]
     tiles = (owned_count, slot_count, share_rows, columns)
     args = (
         [rhs, diag_inv, factor_tiles.reshape(factor_tiles.shape[:2] + (slot_count * share_rows, -1))]
@@ -539,7 +596,7 @@
         out_specs=tuple(_vmem() for o in range(6)),
         scratch_shapes=[vm(nblk)] + _dma(n) + [vm(whole)]
         + [vm(win), vm(win)] + _dma(slots)
-        + [vm((n,) + dblk)] + _dma(n) + [vm((n,) + dblk)] + _dma(n)
+        + [vm((n,) + dblk)] + tri_dma + [vm((n,) + dblk)] + tri_dma
         + [vm(whole), vm(whole), vm(nblk)] + _dma(n)
         + [vm(win), vm(win)] + _dma(slots)
         + [vm(whole), vm(whole), vm(nblk)] + _dma(n)

time: 122 us -> 122 us (level)
  no operation moved by 1% of the time
where the time goes in v13:
time: 122 us
  Pallas kernels  117 us (96%)
  local copies, waits for them, and re-layouts  4.27 us (3%)
    pallas_call x1, Pallas kernels, local(): pl.pallas_call(functools.partial(_forward_kernel, n, count), out_shape=tu...  117 us
    unnamed x5, local copies, waits for them, and re-layouts  2.74 us

profile of v13, /device:TPU:1, one launch (start us, length us, event | category | flops | bytes accessed | tf_op | source)
XLA Modules:
  0.0 122.3 jit_solution(4694463247473920703)
XLA Ops:
  0.0 0.0 copy-start.1
  0.0 0.7 copy-done.1
  0.7 0.1 iota_compare_fusion.2
  0.8 0.0 copy-start
  0.8 0.1 reshape.95
  0.8 0.1 reshape.94
  0.9 0.5 copy-done
  1.5 0.1 squeeze.9
  1.6 0.1 squeeze.8
  1.6 0.1 fusion.3
  1.7 0.1 select_reduce_fusion
  1.8 0.1 fusion.1
  1.9 0.1 select_reduce_fusion.1
  2.1 0.1 copy.9
  2.2 0.1 reshape.92
  2.4 0.1 copy.10
  2.5 0.2 reshape.93
  2.6 0.7 concatenate.3.table
  3.3 117.4 %shard_map.55 = (f32[3,2,32,128]{3,2,1,0:T(8,128)}, f32[2,32,128]{2,1,0:T(8,128)}, f32[2,32,128]{2,1,0:T(8,128)}, f32[2,256,128]{2,1,0:T(8,128)}, f32[2,256,256]{2,1,0:T(8,128)}, /*index=5*/f32[2,256,256]{2,1,0:T(8,128)}) custom-call(f32[3,2,32,128]{3,2,1,0:T(8,128)} %rhs_ref.1, f32[3,2,32,256]{3,2,1,0:T(8,128)} %dinv_ref.1, f32[2,2,256,256]{3,2,1,0:T(8,128)} %bitcast.15, ...), custom_call_target="tpu_custom_call" | custom-call | tf_op jit(solution)/shard_map/pallas_call | solution.py:592
  120.7 1.5 %copy.12 = f32[3,2,32,128]{3,2,1,0:T(8,128)} copy(f32[3,2,32,128]{3,2,1,0:T(8,128)} %get-tuple-element.6) | data formatting | bytes 196608
  (9 shorter events, 0.1 us)
Async XLA Ops:
  0.0 0.7 copy-start.1
  0.8 0.7 copy-start

commit v14 on v12

--- a/solution.py
+++ b/solution.py
@@ -112,6 +112,65 @@
         src = p.col_peer(p.n - k)
         _copy(y_ref, got.at[src], send.at[src], recv.at[src], (p.row, src)).wait_recv()
         _rows_of(full_ref, src, chunk)[...] = got[src]
+
+
+def _when_start(cond, copy):
+    pl.when(cond)(copy.start)
+    return (cond, copy)
+
+
+def _wait_sends_when(pairs):
+    for cond, copy in pairs:
+        pl.when(cond)(copy.wait_send)
+
+
+def lower_gather_start(p, y_ref, got, send, recv):
+    out = []
+    for k in _send_order(p.n):
+        peer = p.col_peer(k)
+        out.append(_when_start(peer > p.col, _copy(y_ref, got.at[p.col], send.at[peer], recv.at[p.col], (p.row, peer))))
+    return out
+
+
+def lower_gather_finish(p, y_ref, got, send, recv, full_ref):
+    chunk = got.shape[2]
+    _rows_of(full_ref, p.col, chunk)[...] = y_ref[...]
+    for k in range(1, p.n):
+        src = p.col_peer(p.n - k)
+        rows = _rows_of(full_ref, src, chunk)
+
+        @pl.when(src < p.col)
+        def _():
+            _copy(y_ref, got.at[src], send.at[src], recv.at[src], (p.row, src)).wait_recv()
+            rows[...] = got[src]
+
+        @pl.when(src > p.col)
+        def _():
+            rows[...] = jnp.zeros(y_ref.shape, jnp.float32)
+
+
+def upper_scatter_start(p, x_ref, got, send, recv):
+    chunk = got.shape[2]
+    out = []
+    for k in _send_order(p.n):
+        peer = p.col_peer(k)
+        out.append(_when_start(
+            peer < p.col,
+            _copy(_rows_of(x_ref, peer, chunk), got.at[p.col], send.at[peer], recv.at[p.col], (p.row, peer)),
+        ))
+    return out
+
+
+def upper_scatter_finish(p, x_ref, got, send, recv, acc_ref):
+    chunk = got.shape[2]
+    acc_ref[...] = _rows_of(x_ref, p.col, chunk)[...]
+    for k in range(1, p.n):
+        src = p.col_peer(p.n - k)
+
+        @pl.when(src > p.col)
+        def _():
+            _copy(_rows_of(x_ref, src, chunk), got.at[src], send.at[src], recv.at[src], (p.row, src)).wait_recv()
+            acc_ref[...] = acc_ref[...] + got[src]
 
 
 def bcast_start(p, v_ref, got, send, recv):
@@ -376,8 +435,9 @@
     lookup2 = lookup1 + (2 * KDEV + 1) * owned * owned * 2
     p = Place(n, count)
     p.barrier(True, True)
-    sends = gather_start(p, rhs_ref.at[0], got_y, sy, ry)
-    gather_finish(p, rhs_ref.at[0], got_y, sy, ry, whole)
+    lower = lower_gather_start(p, rhs_ref.at[0], got_y, sy, ry)
+    lower_gather_finish(p, rhs_ref.at[0], got_y, sy, ry, whole)
+    sends = []
     fv0_ref[...] = _dots(dinv_ref.at[0], whole)
     sends += bcast_start(p, fv0_ref, got_w0, sw0, rw0)
     sends += gather_start(p, dinv_ref.at[1], got_d1, sd1, rd1) + gather_start(p, dinv_ref.at[2], got_d2, sd2, rd2)
@@ -413,9 +473,10 @@
     res0 = fv0_ref[...] - spread_finish(p, bucket0, got_b0, sb0, rb0)
     d0 = dinv_ref.at[0]
     x0[...] = jnp.stack([_mm(d0[q].T, res0[q]) for q in range(res0.shape[0])], 0)
-    sends += scatter_start(p, x0, got_x0, sx0, rx0)
-    out_ref[0] = scatter_finish(p, x0, got_x0, sx0, rx0)
-    _wait_sends(sends)
+    upper = upper_scatter_start(p, x0, got_x0, sx0, rx0)
+    upper_scatter_finish(p, x0, got_x0, sx0, rx0, out_ref.at[0])
+    _wait_sends(sends)
+    _wait_sends_when(lower + upper)
 
 
 def _f32(shape):

time: 122 us -> 123 us (level)
    pallas_call x1, Pallas kernels: 117 us -> 118 us  [local(): pl.pallas_call(functools.partial(_forward_kernel, n, count), out_shape=tu...]
where the time goes in v14:
time: 123 us
  Pallas kernels  118 us (96%)
  local copies, waits for them, and re-layouts  4.27 us (3%)
    pallas_call x1, Pallas kernels, local(): pl.pallas_call(functools.partial(_forward_kernel, n, count), out_shape=tu...  118 us
    unnamed x5, local copies, waits for them, and re-layouts  2.74 us

profile of v14, /device:TPU:1, one launch (start us, length us, event | category | flops | bytes accessed | tf_op | source)
XLA Modules:
  0.0 123.2 jit_solution(3550430314465188188)
XLA Ops:
  0.0 0.0 copy-start.1
  0.0 0.7 copy-done.1
  0.7 0.1 iota_compare_fusion.2
  0.8 0.0 copy-start
  0.8 0.1 reshape.95
  0.8 0.1 reshape.94
  0.9 0.5 copy-done
  1.5 0.1 squeeze.9
  1.6 0.1 squeeze.8
  1.6 0.1 fusion.3
  1.7 0.1 select_reduce_fusion
  1.8 0.1 fusion.1
  1.9 0.1 select_reduce_fusion.1
  2.1 0.1 copy.9
  2.2 0.1 reshape.92
  2.4 0.1 copy.10
  2.5 0.2 reshape.93
  2.6 0.7 concatenate.3.table
  3.3 118.3 %shard_map.55 = (f32[3,2,32,128]{3,2,1,0:T(8,128)}, f32[2,32,128]{2,1,0:T(8,128)}, f32[2,32,128]{2,1,0:T(8,128)}, f32[2,256,128]{2,1,0:T(8,128)}, f32[2,256,256]{2,1,0:T(8,128)}, /*index=5*/f32[2,256,256]{2,1,0:T(8,128)}) custom-call(f32[3,2,32,128]{3,2,1,0:T(8,128)} %rhs_ref.1, f32[3,2,32,256]{3,2,1,0:T(8,128)} %dinv_ref.1, f32[2,2,256,256]{3,2,1,0:T(8,128)} %bitcast.15, ...), custom_call_target="tpu_custom_call" | custom-call | tf_op jit(solution)/shard_map/pallas_call | solution.py:596
  121.7 1.5 %copy.12 = f32[3,2,32,128]{3,2,1,0:T(8,128)} copy(f32[3,2,32,128]{3,2,1,0:T(8,128)} %get-tuple-element.6) | data formatting | bytes 196608
  (9 shorter events, 0.1 us)
Async XLA Ops:
  0.0 0.7 copy-start.1
  0.8 0.7 copy-start

commit v15 on v12

--- a/solution.py
+++ b/solution.py
@@ -11,6 +11,13 @@
 MESH = pl.DeviceIdType.MESH
 OFFSETS = [d for d in range(-KDEV, KDEV + 1) if d != 0]
 SEND_OFFSETS = sorted(OFFSETS, key=lambda d: (-abs(d), d))
+
+
+WAIT_OFFSETS = sorted(OFFSETS, key=lambda d: (abs(d), d))
+
+
+def _wait_order(n):
+    return sorted(range(1, n), key=lambda k: (min(k, n - k), k))
 
 
 def _send_order(n):
@@ -90,7 +97,7 @@
 def scatter_finish(p, x_ref, got, send, recv):
     chunk = got.shape[2]
     acc = _rows_of(x_ref, p.col, chunk)[...]
-    for k in range(1, p.n):
+    for k in _wait_order(p.n):
         src = p.col_peer(p.n - k)
         _copy(_rows_of(x_ref, src, chunk), got.at[src], send.at[src], recv.at[src], (p.row, src)).wait_recv()
         acc = acc + got[src]
@@ -108,7 +115,7 @@
 def gather_finish(p, y_ref, got, send, recv, full_ref):
     chunk = got.shape[2]
     _rows_of(full_ref, p.col, chunk)[...] = y_ref[...]
-    for k in range(1, p.n):
+    for k in _wait_order(p.n):
         src = p.col_peer(p.n - k)
         _copy(y_ref, got.at[src], send.at[src], recv.at[src], (p.row, src)).wait_recv()
         _rows_of(full_ref, src, chunk)[...] = got[src]
@@ -123,7 +130,7 @@
 
 def bcast_finish(p, v_ref, got, send, recv, win_ref):
     win_ref[KDEV] = v_ref[...]
-    for o in OFFSETS:
+    for o in WAIT_OFFSETS:
         w = KDEV + o
         _copy(v_ref, got.at[w], send.at[w], recv.at[w], (p.row_peer(o), p.col)).wait_recv()
         win_ref[w] = got[w]
@@ -140,7 +147,7 @@
 
 def spread_finish(p, x_ref, got, send, recv):
     acc = x_ref[KDEV]
-    for o in OFFSETS:
+    for o in WAIT_OFFSETS:
         w = KDEV + o
         _copy(x_ref.at[w], got.at[w], send.at[w], recv.at[w], (p.row_peer(o), p.col)).wait_recv()
         acc = acc + got[w]

time: 122 us -> 123 us (level)
  no operation moved by 1% of the time
where the time goes in v15:
time: 123 us; the launch traced here: 122 us
  Pallas kernels  117 us (95%)
  local copies, waits for them, and re-layouts  4.27 us (3%)
    pallas_call x1, Pallas kernels, local(): pl.pallas_call(functools.partial(_forward_kernel, n, count), out_shape=tu...  117 us
    unnamed x5, local copies, waits for them, and re-layouts  2.74 us

profile of v15, /device:TPU:1, one launch (start us, length us, event | category | flops | bytes accessed | tf_op | source)
XLA Modules:
  0.0 122.4 jit_solution(3156458771967075226)
XLA Ops:
  0.0 0.0 copy-start.1
  0.0 0.7 copy-done.1
  0.7 0.1 iota_compare_fusion.2
  0.8 0.0 copy-start
  0.8 0.1 reshape.95
  0.8 0.1 reshape.94
  0.9 0.5 copy-done
  1.5 0.1 squeeze.9
  1.6 0.1 squeeze.8
  1.6 0.1 fusion.3
  1.7 0.1 select_reduce_fusion
  1.8 0.1 fusion.1
  1.9 0.1 select_reduce_fusion.1
  2.1 0.1 copy.9
  2.2 0.1 reshape.92
  2.4 0.1 copy.10
  2.5 0.2 reshape.93
  2.6 0.7 concatenate.3.table
  3.3 117.5 %shard_map.55 = (f32[3,2,32,128]{3,2,1,0:T(8,128)}, f32[2,32,128]{2,1,0:T(8,128)}, f32[2,32,128]{2,1,0:T(8,128)}, f32[2,256,128]{2,1,0:T(8,128)}, f32[2,256,256]{2,1,0:T(8,128)}, /*index=5*/f32[2,256,256]{2,1,0:T(8,128)}) custom-call(f32[3,2,32,128]{3,2,1,0:T(8,128)} %rhs_ref.1, f32[3,2,32,256]{3,2,1,0:T(8,128)} %dinv_ref.1, f32[2,2,256,256]{3,2,1,0:T(8,128)} %bitcast.15, ...), custom_call_target="tpu_custom_call" | custom-call | tf_op jit(solution)/shard_map/pallas_call | solution.py:542
  120.8 1.5 %copy.12 = f32[3,2,32,128]{3,2,1,0:T(8,128)} copy(f32[3,2,32,128]{3,2,1,0:T(8,128)} %get-tuple-element.6) | data formatting | bytes 196608
  (9 shorter events, 0.1 us)
Async XLA Ops:
  0.0 0.7 copy-start.1
  0.8 0.7 copy-start

commit v16 on v12

--- a/solution.py
+++ b/solution.py
@@ -126,7 +126,8 @@
     for o in OFFSETS:
         w = KDEV + o
         _copy(v_ref, got.at[w], send.at[w], recv.at[w], (p.row_peer(o), p.col)).wait_recv()
-        win_ref[w] = got[w]
+        if win_ref is not got:
+            win_ref[w] = got[w]
 
 
 def spread_start(p, x_ref, got, send, recv):
@@ -381,16 +382,16 @@
     fv0_ref[...] = _dots(dinv_ref.at[0], whole)
     sends += bcast_start(p, fv0_ref, got_w0, sw0, rw0)
     sends += gather_start(p, dinv_ref.at[1], got_d1, sd1, rd1) + gather_start(p, dinv_ref.at[2], got_d2, sd2, rd2)
-    bcast_finish(p, fv0_ref, got_w0, sw0, rw0, win0)
+    bcast_finish(p, fv0_ref, got_w0, sw0, rw0, got_w0)
     gather_finish(p, dinv_ref.at[1], got_d1, sd1, rd1, d1_ref)
-    _share(p, [win0], t1_ref, table, 0, slots, rhs_ref.at[1], share1)
+    _share(p, [got_w0], t1_ref, table, 0, slots, rhs_ref.at[1], share1)
     x1[...] = _dots(d1_ref, share1)
     sends += scatter_start(p, x1, got_x1, sx1, rx1)
     fv1_ref[...] = scatter_finish(p, x1, got_x1, sx1, rx1)
     sends += bcast_start(p, fv1_ref, got_w1, sw1, rw1)
-    bcast_finish(p, fv1_ref, got_w1, sw1, rw1, win1)
+    bcast_finish(p, fv1_ref, got_w1, sw1, rw1, got_w1)
     gather_finish(p, dinv_ref.at[2], got_d2, sd2, rd2, d2_ref)
-    _share(p, [win0, win1], t2_ref, table, 4 * size, slots, rhs_ref.at[2], share2)
+    _share(p, [got_w0, got_w1], t2_ref, table, 4 * size, slots, rhs_ref.at[2], share2)
     x2[...] = _dots(d2_ref, share2)
     sends += scatter_start(p, x2, got_x2, sx2, rx2)
     fv2[...] = scatter_finish(p, x2, got_x2, sx2, rx2)

time: 122 us -> 122 us (level)
  no operation moved by 1% of the time
where the time goes in v16:
time: 122 us
  Pallas kernels  117 us (96%)
  local copies, waits for them, and re-layouts  4.27 us (3%)
    pallas_call x1, Pallas kernels, local(): pl.pallas_call(functools.partial(_forward_kernel, n, count), out_shape=tu...  117 us
    unnamed x5, local copies, waits for them, and re-layouts  2.74 us

profile of v16, /device:TPU:1, one launch (start us, length us, event | category | flops | bytes accessed | tf_op | source)
XLA Modules:
  0.0 121.8 jit_solution(15856850054504849238)
XLA Ops:
  0.0 0.0 copy-start.1
  0.0 0.7 copy-done.1
  0.7 0.1 iota_compare_fusion.2
  0.8 0.0 copy-start
  0.8 0.1 reshape.95
  0.8 0.1 reshape.94
  0.9 0.5 copy-done
  1.5 0.1 squeeze.9
  1.6 0.1 squeeze.8
  1.6 0.1 fusion.3
  1.7 0.1 select_reduce_fusion
  1.8 0.1 fusion.1
  1.9 0.1 select_reduce_fusion.1
  2.1 0.1 copy.9
  2.2 0.1 reshape.92
  2.4 0.1 copy.10
  2.5 0.2 reshape.93
  2.6 0.7 concatenate.3.table
  3.3 116.9 %shard_map.55 = (f32[3,2,32,128]{3,2,1,0:T(8,128)}, f32[2,32,128]{2,1,0:T(8,128)}, f32[2,32,128]{2,1,0:T(8,128)}, f32[2,256,128]{2,1,0:T(8,128)}, f32[2,256,256]{2,1,0:T(8,128)}, /*index=5*/f32[2,256,256]{2,1,0:T(8,128)}) custom-call(f32[3,2,32,128]{3,2,1,0:T(8,128)} %rhs_ref.1, f32[3,2,32,256]{3,2,1,0:T(8,128)} %dinv_ref.1, f32[2,2,256,256]{3,2,1,0:T(8,128)} %bitcast.15, ...), custom_call_target="tpu_custom_call" | custom-call | tf_op jit(solution)/shard_map/pallas_call | solution.py:536
  120.3 1.5 %copy.12 = f32[3,2,32,128]{3,2,1,0:T(8,128)} copy(f32[3,2,32,128]{3,2,1,0:T(8,128)} %get-tuple-element.6) | data formatting | bytes 196608
  (9 shorter events, 0.1 us)
Async XLA Ops:
  0.0 0.7 copy-start.1
  0.8 0.7 copy-start

commit v17 on v12

--- a/solution.py
+++ b/solution.py
@@ -380,14 +380,14 @@
     gather_finish(p, rhs_ref.at[0], got_y, sy, ry, whole)
     fv0_ref[...] = _dots(dinv_ref.at[0], whole)
     sends += bcast_start(p, fv0_ref, got_w0, sw0, rw0)
-    sends += gather_start(p, dinv_ref.at[1], got_d1, sd1, rd1) + gather_start(p, dinv_ref.at[2], got_d2, sd2, rd2)
+    sends += gather_start(p, dinv_ref.at[1], got_d1, sd1, rd1)
     bcast_finish(p, fv0_ref, got_w0, sw0, rw0, win0)
     gather_finish(p, dinv_ref.at[1], got_d1, sd1, rd1, d1_ref)
     _share(p, [win0], t1_ref, table, 0, slots, rhs_ref.at[1], share1)
     x1[...] = _dots(d1_ref, share1)
     sends += scatter_start(p, x1, got_x1, sx1, rx1)
     fv1_ref[...] = scatter_finish(p, x1, got_x1, sx1, rx1)
-    sends += bcast_start(p, fv1_ref, got_w1, sw1, rw1)
+    sends += bcast_start(p, fv1_ref, got_w1, sw1, rw1) + gather_start(p, dinv_ref.at[2], got_d2, sd2, rd2)
     bcast_finish(p, fv1_ref, got_w1, sw1, rw1, win1)
     gather_finish(p, dinv_ref.at[2], got_d2, sd2, rd2, d2_ref)
     _share(p, [win0, win1], t2_ref, table, 4 * size, slots, rhs_ref.at[2], share2)

time: 122 us -> 121 us (level)
  no operation moved by 1% of the time
where the time goes in v17:
time: 121 us
  Pallas kernels  116 us (96%)
  local copies, waits for them, and re-layouts  4.27 us (4%)
    pallas_call x1, Pallas kernels, local(): pl.pallas_call(functools.partial(_forward_kernel, n, count), out_shape=tu...  116 us
    unnamed x5, local copies, waits for them, and re-layouts  2.74 us

profile of v17, /device:TPU:1, one launch (start us, length us, event | category | flops | bytes accessed | tf_op | source)
XLA Modules:
  0.0 120.9 jit_solution(5202026270157516058)
XLA Ops:
  0.0 0.0 copy-start.1
  0.0 0.7 copy-done.1
  0.7 0.1 iota_compare_fusion.2
  0.8 0.0 copy-start
  0.8 0.1 reshape.95
  0.8 0.1 reshape.94
  0.9 0.5 copy-done
  1.5 0.1 squeeze.9
  1.6 0.1 squeeze.8
  1.6 0.1 fusion.3
  1.7 0.1 select_reduce_fusion
  1.8 0.1 fusion.1
  1.9 0.1 select_reduce_fusion.1
  2.1 0.1 copy.9
  2.2 0.1 reshape.92
  2.4 0.1 copy.10
  2.5 0.2 reshape.93
  2.6 0.7 concatenate.3.table
  3.3 116.0 %shard_map.55 = (f32[3,2,32,128]{3,2,1,0:T(8,128)}, f32[2,32,128]{2,1,0:T(8,128)}, f32[2,32,128]{2,1,0:T(8,128)}, f32[2,256,128]{2,1,0:T(8,128)}, f32[2,256,256]{2,1,0:T(8,128)}, /*index=5*/f32[2,256,256]{2,1,0:T(8,128)}) custom-call(f32[3,2,32,128]{3,2,1,0:T(8,128)} %rhs_ref.1, f32[3,2,32,256]{3,2,1,0:T(8,128)} %dinv_ref.1, f32[2,2,256,256]{3,2,1,0:T(8,128)} %bitcast.15, ...), custom_call_target="tpu_custom_call" | custom-call | tf_op jit(solution)/shard_map/pallas_call | solution.py:535
  119.4 1.5 %copy.12 = f32[3,2,32,128]{3,2,1,0:T(8,128)} copy(f32[3,2,32,128]{3,2,1,0:T(8,128)} %get-tuple-element.6) | data formatting | bytes 196608
  (9 shorter events, 0.1 us)
Async XLA Ops:
  0.0 0.7 copy-start.1
  0.8 0.7 copy-start

commit v18 on v17

--- a/solution.py
+++ b/solution.py
@@ -378,9 +378,9 @@
     p.barrier(True, True)
     sends = gather_start(p, rhs_ref.at[0], got_y, sy, ry)
     gather_finish(p, rhs_ref.at[0], got_y, sy, ry, whole)
+    sends += gather_start(p, dinv_ref.at[1], got_d1, sd1, rd1)
     fv0_ref[...] = _dots(dinv_ref.at[0], whole)
     sends += bcast_start(p, fv0_ref, got_w0, sw0, rw0)
-    sends += gather_start(p, dinv_ref.at[1], got_d1, sd1, rd1)
     bcast_finish(p, fv0_ref, got_w0, sw0, rw0, win0)
     gather_finish(p, dinv_ref.at[1], got_d1, sd1, rd1, d1_ref)
     _share(p, [win0], t1_ref, table, 0, slots, rhs_ref.at[1], share1)

time: 121 us -> 120 us (level)
  no operation moved by 1% of the time
where the time goes in v18:
time: 120 us
  Pallas kernels  115 us (96%)
  local copies, waits for them, and re-layouts  4.27 us (4%)
    pallas_call x1, Pallas kernels, local(): pl.pallas_call(functools.partial(_forward_kernel, n, count), out_shape=tu...  115 us
    unnamed x5, local copies, waits for them, and re-layouts  2.74 us

profile of v18, /device:TPU:1, one launch (start us, length us, event | category | flops | bytes accessed | tf_op | source)
XLA Modules:
  0.0 119.8 jit_solution(17781364835497393797)
XLA Ops:
  0.0 0.0 copy-start.1
  0.0 0.7 copy-done.1
  0.7 0.1 iota_compare_fusion.2
  0.8 0.0 copy-start
  0.8 0.1 reshape.95
  0.8 0.1 reshape.94
  0.9 0.5 copy-done
  1.5 0.1 squeeze.9
  1.6 0.1 squeeze.8
  1.6 0.1 fusion.3
  1.7 0.1 select_reduce_fusion
  1.8 0.1 fusion.1
  1.9 0.1 select_reduce_fusion.1
  2.1 0.1 copy.9
  2.2 0.1 reshape.92
  2.4 0.1 copy.10
  2.5 0.2 reshape.93
  2.6 0.7 concatenate.3.table
  3.3 114.9 %shard_map.55 = (f32[3,2,32,128]{3,2,1,0:T(8,128)}, f32[2,32,128]{2,1,0:T(8,128)}, f32[2,32,128]{2,1,0:T(8,128)}, f32[2,256,128]{2,1,0:T(8,128)}, f32[2,256,256]{2,1,0:T(8,128)}, /*index=5*/f32[2,256,256]{2,1,0:T(8,128)}) custom-call(f32[3,2,32,128]{3,2,1,0:T(8,128)} %rhs_ref.1, f32[3,2,32,256]{3,2,1,0:T(8,128)} %dinv_ref.1, f32[2,2,256,256]{3,2,1,0:T(8,128)} %bitcast.15, ...), custom_call_target="tpu_custom_call" | custom-call | tf_op jit(solution)/shard_map/pallas_call | solution.py:535
  118.3 1.5 %copy.12 = f32[3,2,32,128]{3,2,1,0:T(8,128)} copy(f32[3,2,32,128]{3,2,1,0:T(8,128)} %get-tuple-element.6) | data formatting | bytes 196608
  (9 shorter events, 0.1 us)
Async XLA Ops:
  0.0 0.7 copy-start.1
  0.8 0.7 copy-start
